TPU v7x, 512 devices: a whole 4x8x8 slice. The times are simulated.
512 devices in a mesh: rows: 32 (over y_lo, z, core), cols: 16 (over x, y_hi).
Axes of the slice: x: 4, y: 8 (y_hi: 4, y_lo: 2; y = y_hi * 2 + y_lo), z: 8, core: 2. Of those that a mesh axis runs over, the one named last changes fastest.
Arguments:
- pair_rep: bfloat16 [128, 4096, 128], P('rows', 'cols'), may hold values from -6 to 6
- project_weight: bfloat16 [128, 512], replicated, may hold values from -0.5 to 0.5
- output_weight: bfloat16 [128, 128], replicated, may hold values from -0.5 to 0.5
- pair_bias: bfloat16 [4, 4096, 4096], P(None, 'cols', 'rows'), may hold values from -4 to 300
- chain_valid: int32 [32], replicated, may hold values from 1 to 128, as said below
Outputs:
- update: bfloat16 [128, 4096, 128], P('rows', 'cols')
Inputs may be any that keep to these rules, and one draw needn't show every extreme that they name: Chain c occupies residues c * 128 to (c + 1) * 128 - 1; its first chain_valid[c] residues are valid; some chain is full.
All inputs are finite; a program needn't handle non-finite values.
Results may differ from a plain program's by a relative error of at most 0.0075.
Values may be sent and summed in bfloat16 or wider, within the bound.
No kernel may reach another device: no remote copies, remote signals or barrier semaphores. Data moves between devices by JAX's collectives and lax.ppermute only.
A program may use at most 64 MiB of HBM per device.

v0:
```python
import jax
import jax.numpy as jnp
from jax import lax
from jax.sharding import PartitionSpec as P

SLOT = 128


def attend(carry, query_head, key_piece, value_piece, bias_piece, chain_valid):
    count = key_piece.shape[2]
    position = jnp.arange(count, dtype=jnp.int32)
    chains = chain_valid.shape[0]
    member = (position // SLOT)[:, None] == jnp.arange(chains, dtype=jnp.int32)[None, :]
    allowed = jnp.sum(jnp.where(member, chain_valid[None, :], 0), axis=1)
    mask_add = jnp.where(position % SLOT < allowed, 0.0, -1000000000.0).astype(jnp.float32)
    block = 512

    def step(number, state):
        total, running_max, running_sum = state
        offset = number * block
        key_block = lax.dynamic_slice_in_dim(key_piece, offset, block, 2)
        value_block = lax.dynamic_slice_in_dim(value_piece, offset, block, 2)
        bias_block = lax.dynamic_slice_in_dim(bias_piece, offset, block, 1)
        mask_block = lax.dynamic_slice_in_dim(mask_add, offset, block, 0)
        scores = jnp.einsum(
            "rjd,rdk->rjk", query_head, key_block, preferred_element_type=jnp.float32
        )
        scores = scores + bias_block.astype(jnp.float32)[None] + mask_block[None, None, :]
        new_max = jnp.maximum(running_max, jnp.max(scores, axis=2))
        rescale = jnp.exp(running_max - new_max)
        weights = jnp.exp(scores - new_max[:, :, None])
        running_sum = running_sum * rescale + jnp.sum(weights, axis=2)
        weighted = jnp.einsum(
            "rdk,rjk->rdj",
            value_block,
            weights.astype(jnp.bfloat16),
            preferred_element_type=jnp.float32,
        )
        total = total * rescale[:, None, :] + weighted
        return (total, new_max, running_sum)

    return lax.fori_loop(0, count // block, step, carry)


def local(pair_rep, project_weight, output_weight, pair_bias, chain_valid):
    rows_here, cols_here, width = pair_rep.shape
    heads = pair_bias.shape[0]
    inner = output_weight.shape[0]
    head_size = inner // heads
    pair_f = pair_rep.astype(jnp.float32)
    center = jnp.mean(pair_f, axis=-1, keepdims=True)
    spread = jnp.mean(jnp.square(pair_f - center), axis=-1, keepdims=True)
    normed = ((pair_f - center) * lax.rsqrt(spread + 1e-05)).astype(jnp.bfloat16)
    project = jnp.dot(
        normed.reshape(rows_here * cols_here, width),
        project_weight,
        preferred_element_type=jnp.float32,
    )
    queries = (project[:, :inner] * head_size ** (-0.5)).astype(jnp.bfloat16)
    queries = queries.reshape(rows_here, cols_here, heads, head_size).transpose(0, 2, 1, 3)
    key_part = project[:, inner : 2 * inner].astype(jnp.bfloat16)
    key_part = key_part.reshape(rows_here, cols_here, heads, head_size).transpose(0, 2, 3, 1)
    value_part = project[:, 2 * inner : 3 * inner].astype(jnp.bfloat16)
    value_part = value_part.reshape(rows_here, cols_here, heads, head_size).transpose(0, 2, 3, 1)
    gate = jax.nn.sigmoid(project[:, 3 * inner :])
    outputs = []
    for head_index in range(heads):
        query_head = queries[:, head_index]
        key_head = key_part[:, head_index]
        value_head = value_part[:, head_index]
        bias_head = pair_bias[head_index]
        start_state = (
            jnp.zeros((rows_here, head_size, cols_here), jnp.float32),
            jnp.full((rows_here, cols_here), -jnp.inf, jnp.float32),
            jnp.zeros((rows_here, cols_here), jnp.float32),
        )
        bias_row = lax.all_gather(bias_head, "rows", axis=1, tiled=True)
        state = attend(
            start_state,
            query_head,
            lax.all_gather(key_head, "cols", axis=2, tiled=True),
            lax.all_gather(value_head, "cols", axis=2, tiled=True),
            bias_row,
            chain_valid,
        )
        total, running_max, running_sum = state
        outputs.append(total / running_sum[:, None, :])
    stacked = jnp.stack(outputs, axis=1).transpose(0, 3, 1, 2).reshape(rows_here * cols_here, inner)
    gated = (stacked * gate).astype(jnp.bfloat16)
    update = jnp.dot(gated, output_weight, preferred_element_type=jnp.float32).astype(jnp.bfloat16)
    return update.reshape(rows_here, cols_here, width)


def solution(mesh):
    return jax.shard_map(
        local,
        mesh=mesh,
        in_specs=(P("rows", "cols", None), P(), P(), P(None, "cols", "rows"), P()),
        out_specs=P("rows", "cols", None),
        check_vma=False,
    )
```

profile of v0, /device:TPU:1, one launch (start us, length us, event | category | flops | bytes accessed | tf_op | source)
XLA Modules:
  0.0 814.8 jit_solution(14056148589035336416)
XLA Ops:
  6.5 1.1 convert_reduce_fusion
  7.7 1.3 fusion.34
  9.0 1.3 fusion.35
  21.5 53.6 %all-gather.25.cloned.1.call-done = bf16[4,1,32,4096]{3,0,2,1:T(4,128)(2,1)} async-done(((bf16[4,1,32,256]{3,0,2,1:T(4,128)(2,1)}), bf16[4,1,32,4096]{3,0,2,1:T(4,128)(2,1)}) %all-gather.25.cloned.1.call-update) | async-done | bytes 1048592 | tf_op jit(solution)/shard_map/all_gather | solution.py:81
  75.2 60.8 %all-gather.29.cloned.1.call-done = bf16[4,1,32,4096]{3,0,2,1:T(4,128)(2,1)} async-done(((bf16[4,1,32,256]{3,0,2,1:T(4,128)(2,1)}), bf16[4,1,32,4096]{3,0,2,1:T(4,128)(2,1)}) %all-gather.29.cloned.1.call-update) | async-done | bytes 1048592 | tf_op jit(solution)/shard_map/all_gather | solution.py:82
  135.9 70.5 %all-gather.27.cloned.1.call-done = bf16[1,256,4096]{1,2,0:T(8,128)(2,1)} async-done(((bf16[1,256,128]{1,2,0:T(8,128)(2,1)}), bf16[1,256,4096]{1,2,0:T(8,128)(2,1)}) %all-gather.27.cloned.1.call-update) | async-done | bytes 2097168 | tf_op jit(solution)/shard_map/all_gather | solution.py:77
  206.4 27.7 %while.72 = (s32[]{:T(128)}, f32[4,32,256]{2,1,0:T(8,128)S(1)}, f32[4,256]{1,0:T(4,128)S(1)}, f32[4,256]{1,0:T(4,128)S(1)}, bf16[4,32,4096]{2,0,1:T(4,128)(2,1)}...) while((s32[]{:T(128)}, f32[4,32,256]{2,1,0:T(8,128)S(1)}, ...), condition=%wide.region_6.7_spmd.clone, body=%wide.region_3.6_spmd.clone.sunk | while | flops 71013376 | bytes 8788163 | solution.py:42
  220.3 1.1 constant_dynamic-slice_fusion.12
  223.7 1.1 constant_dynamic-slice_fusion.12
  234.1 31.4 %all-gather.35.cloned.1.call-done = bf16[4,1,32,4096]{3,0,2,1:T(4,128)(2,1)} async-done(((bf16[4,1,32,256]{3,0,2,1:T(4,128)(2,1)}), bf16[4,1,32,4096]{3,0,2,1:T(4,128)(2,1)}) %all-gather.35.cloned.1.call-update) | async-done | bytes 1048592 | tf_op jit(solution)/shard_map/all_gather | solution.py:82
  265.6 60.6 %all-gather.31.cloned.1.call-done = bf16[4,1,32,4096]{3,0,2,1:T(4,128)(2,1)} async-done(((bf16[4,1,32,256]{3,0,2,1:T(4,128)(2,1)}), bf16[4,1,32,4096]{3,0,2,1:T(4,128)(2,1)}) %all-gather.31.cloned.1.call-update) | async-done | bytes 1048592 | tf_op jit(solution)/shard_map/all_gather | solution.py:81
  326.2 70.3 %all-gather.33.cloned.1.call-done = bf16[1,256,4096]{1,2,0:T(8,128)(2,1)} async-done(((bf16[1,256,128]{1,2,0:T(8,128)(2,1)}), bf16[1,256,4096]{1,2,0:T(8,128)(2,1)}) %all-gather.33.cloned.1.call-update) | async-done | bytes 2097168 | tf_op jit(solution)/shard_map/all_gather | solution.py:77
  396.5 27.7 %while.73 = (s32[]{:T(128)}, f32[4,32,256]{2,1,0:T(8,128)S(1)}, f32[4,256]{1,0:T(4,128)S(1)}, f32[4,256]{1,0:T(4,128)S(1)}, bf16[4,32,4096]{2,0,1:T(4,128)(2,1)}...) while((s32[]{:T(128)}, f32[4,32,256]{2,1,0:T(8,128)S(1)}, ...), condition=%wide.region_10.11_spmd.clone, body=%wide.region_7.10_spmd.clone.sunk | while | flops 71013376 | bytes 8788163 | solution.py:42
  413.9 1.1 constant_dynamic-slice_fusion.13
  424.2 31.6 %all-gather.37.cloned.1.call-done = bf16[4,1,32,4096]{3,0,2,1:T(4,128)(2,1)} async-done(((bf16[4,1,32,256]{3,0,2,1:T(4,128)(2,1)}), bf16[4,1,32,4096]{3,0,2,1:T(4,128)(2,1)}) %all-gather.37.cloned.1.call-update) | async-done | bytes 1048592 | tf_op jit(solution)/shard_map/all_gather | solution.py:81
  455.9 60.8 %all-gather.41.cloned.1.call-done = bf16[4,1,32,4096]{3,0,2,1:T(4,128)(2,1)} async-done(((bf16[4,1,32,256]{3,0,2,1:T(4,128)(2,1)}), bf16[4,1,32,4096]{3,0,2,1:T(4,128)(2,1)}) %all-gather.41.cloned.1.call-update) | async-done | bytes 1048592 | tf_op jit(solution)/shard_map/all_gather | solution.py:82
  516.7 70.5 %all-gather.39.cloned.1.call-done = bf16[1,256,4096]{1,2,0:T(8,128)(2,1)} async-done(((bf16[1,256,128]{1,2,0:T(8,128)(2,1)}), bf16[1,256,4096]{1,2,0:T(8,128)(2,1)}) %all-gather.39.cloned.1.call-update) | async-done | bytes 2097168 | tf_op jit(solution)/shard_map/all_gather | solution.py:77
  587.1 27.7 %while.74 = (s32[]{:T(128)}, f32[4,32,256]{2,1,0:T(8,128)S(1)}, f32[4,256]{1,0:T(4,128)S(1)}, f32[4,256]{1,0:T(4,128)S(1)}, bf16[4,32,4096]{2,0,1:T(4,128)(2,1)}...) while((s32[]{:T(128)}, f32[4,32,256]{2,1,0:T(8,128)S(1)}, ...), condition=%wide.region_14.15_spmd.clone, body=%wide.region_11.14_spmd.clone.sunk | while | flops 71013376 | bytes 8788163 | solution.py:42
  604.4 1.1 constant_dynamic-slice_fusion.14
  614.8 31.5 %all-gather.43.cloned.1.call-done = bf16[4,1,32,4096]{3,0,2,1:T(4,128)(2,1)} async-done(((bf16[4,1,32,256]{3,0,2,1:T(4,128)(2,1)}), bf16[4,1,32,4096]{3,0,2,1:T(4,128)(2,1)}) %all-gather.43.cloned.1.call-update) | async-done | bytes 1048592 | tf_op jit(solution)/shard_map/all_gather | solution.py:81
  646.3 60.8 %all-gather.47.cloned.1.call-done = bf16[4,1,32,4096]{3,0,2,1:T(4,128)(2,1)} async-done(((bf16[4,1,32,256]{3,0,2,1:T(4,128)(2,1)}), bf16[4,1,32,4096]{3,0,2,1:T(4,128)(2,1)}) %all-gather.47.cloned.1.call-update) | async-done | bytes 1048592 | tf_op jit(solution)/shard_map/all_gather | solution.py:82
  707.1 70.3 %all-gather.45.cloned.1.call-done = bf16[1,256,4096]{1,2,0:T(8,128)(2,1)} async-done(((bf16[1,256,128]{1,2,0:T(8,128)(2,1)}), bf16[1,256,4096]{1,2,0:T(8,128)(2,1)}) %all-gather.45.cloned.1.call-update) | async-done | bytes 2097168 | tf_op jit(solution)/shard_map/all_gather | solution.py:77
  777.4 27.7 %while.75 = (s32[]{:T(128)}, f32[4,32,256]{2,1,0:T(8,128)S(1)}, f32[4,256]{1,0:T(4,128)S(1)}, f32[4,256]{1,0:T(4,128)S(1)}, bf16[4,32,4096]{2,0,1:T(4,128)(2,1)}...) while((s32[]{:T(128)}, f32[4,32,256]{2,1,0:T(8,128)S(1)}, ...), condition=%wide.region_18.19_spmd.clone, body=%wide.region_15.18_spmd.clone.sunk | while | flops 71013376 | bytes 8788163 | solution.py:42
  806.0 2.0 convolution_convert_fusion
  (362 shorter events, 116.2 us)
Async XLA Ops:
  6.5 3.8 copy-start
  6.5 68.6 %all-gather.25.cloned.1.call-start = ((), (), s32[]{:S(2)}) async-start(), calls=%async_computation | async-start | bytes 1114112 | tf_op jit(solution)/shard_map/all_gather | solution.py:81
  10.8 10.0 %copy-start.1 = (f32[1024,512]{1,0:T(8,128)}, f32[1024,512]{1,0:T(8,128)S(1)}, u32[]{:S(2)}) copy-start(f32[1024,512]{1,0:T(8,128)S(1)} %get-tuple-element.940) | copy-start | bytes 6291460
  10.8 2.6 copy-start.2
  12.1 123.8 %all-gather.29.cloned.1.call-start = ((), (), s32[]{:S(2)}) async-start(), calls=%async_computation.2 | async-start | bytes 1114112 | tf_op jit(solution)/shard_map/all_gather | solution.py:82
  13.3 8.0 copy-start.3
  13.3 193.1 %all-gather.27.cloned.1.call-start = ((), (), s32[]{:S(2)}) async-start(), calls=%async_computation.1 | async-start | bytes 2162688 | tf_op jit(solution)/shard_map/all_gather | solution.py:77
  14.2 251.4 %all-gather.35.cloned.1.call-start = ((), (), s32[]{:S(2)}) async-start(), calls=%async_computation.5 | async-start | bytes 1114112 | tf_op jit(solution)/shard_map/all_gather | solution.py:82
  14.8 311.4 %all-gather.31.cloned.1.call-start = ((), (), s32[]{:S(2)}) async-start(), calls=%async_computation.3 | async-start | bytes 1114112 | tf_op jit(solution)/shard_map/all_gather | solution.py:81
  15.4 381.2 %all-gather.33.cloned.1.call-start = ((), (), s32[]{:S(2)}) async-start(), calls=%async_computation.4 | async-start | bytes 2162688 | tf_op jit(solution)/shard_map/all_gather | solution.py:77
  16.2 439.7 %all-gather.37.cloned.1.call-start = ((), (), s32[]{:S(2)}) async-start(), calls=%async_computation.6 | async-start | bytes 1114112 | tf_op jit(solution)/shard_map/all_gather | solution.py:81
  16.9 499.7 %all-gather.41.cloned.1.call-start = ((), (), s32[]{:S(2)}) async-start(), calls=%async_computation.8 | async-start | bytes 1114112 | tf_op jit(solution)/shard_map/all_gather | solution.py:82
  17.7 569.5 %all-gather.39.cloned.1.call-start = ((), (), s32[]{:S(2)}) async-start(), calls=%async_computation.7 | async-start | bytes 2162688 | tf_op jit(solution)/shard_map/all_gather | solution.py:77
  18.5 627.8 %all-gather.43.cloned.1.call-start = ((), (), s32[]{:S(2)}) async-start(), calls=%async_computation.9 | async-start | bytes 1114112 | tf_op jit(solution)/shard_map/all_gather | solution.py:81
  19.1 688.0 %all-gather.47.cloned.1.call-start = ((), (), s32[]{:S(2)}) async-start(), calls=%async_computation.11 | async-start | bytes 1114112 | tf_op jit(solution)/shard_map/all_gather | solution.py:82
  19.8 757.6 %all-gather.45.cloned.1.call-start = ((), (), s32[]{:S(2)}) async-start(), calls=%async_computation.10 | async-start | bytes 2162688 | tf_op jit(solution)/shard_map/all_gather | solution.py:77
  805.2 0.8 copy-start.4
Sparse Core Ops, SparseCore 0:
  12.3 62.8 all-gather.24
  78.1 57.7 all-gather.28
  138.1 68.2 all-gather.26
  209.3 56.2 all-gather.34
  268.4 57.7 all-gather.30
  328.2 68.2 all-gather.32
  399.5 56.3 all-gather.36
  458.9 57.7 all-gather.40
  518.8 68.2 all-gather.38
  590.0 56.2 all-gather.42
  649.3 57.7 all-gather.46
  709.1 68.2 all-gather.44
where the time goes:
time: 817 us; the launch traced here: 815 us
  waiting for transfers between devices  677 us (83%)
  other arithmetic  46.2 us (6%)
  local copies, waits for them, and re-layouts  43.4 us (5%)
  matrix products  32.4 us (4%)
  between operations  13.9 us (2%)
    all_gather x4, waiting for transfers between devices, local(): bias_row = lax.all_gather(bias_head, 'rows', axis=1, tiled=True)  282 us
    all_gather x4, waiting for transfers between devices, local(): lax.all_gather(value_head, 'cols', axis=2, tiled=True)  214 us
    all_gather x4, waiting for transfers between devices, local(): lax.all_gather(key_head, 'cols', axis=2, tiled=True)  177 us
    dynamic_slice x32, local copies, waits for them, and re-layouts, step(): value_block = lax.dynamic_slice_in_dim(value_piece, offset, block, 2)  34.1 us
    convert_element_type x32, other arithmetic, step(): bias_block.astype(jnp.float32)[None]  31.8 us
    dot_general x32, matrix products, step(): jnp.einsum('rjd,rdk->rjk', query_head, key_block, preferred_element_type=...  16.6 us
  transfers between devices with their start and end apart: 12, of which 12 were waited for; matrix products, arithmetic and copies ran while one was open for 11% of the time, Pallas kernels for 0%

commit v1 on v0

v1 whole, which is shorter than its diff:
```python
import functools

import jax
import jax.numpy as jnp
from jax import lax
from jax.experimental import pallas as pl
from jax.experimental.pallas import tpu as pltpu
from jax.sharding import PartitionSpec as P

SLOT = 128
GROUP = 16
BLOCK = 256
MASKED = -1000000000.0
LOG2E = 1.4426950408889634
REACH = 60.0
PAIR = 4

NT = (((1,), (1,)), ((), ()))
TN = (((0,), (0,)), ((), ()))


def prep_kernel(valid_ref, pair_ref, bias_ref, normed_ref, biast_ref):
    pair = pair_ref[...].astype(jnp.float32)
    center = jnp.mean(pair, axis=-1, keepdims=True)
    spread = jnp.mean(jnp.square(pair - center), axis=-1, keepdims=True)
    normed_ref[...] = ((pair - center) * lax.rsqrt(spread + 1e-05)).astype(jnp.bfloat16)
    heads, queries, keys = bias_ref.shape
    live = lax.broadcasted_iota(jnp.int32, (keys, queries), 0) < valid_ref[0]
    for head in range(heads):
        turned = jnp.transpose(bias_ref[head].astype(jnp.float32))
        biast_ref[head] = jnp.where(live, turned, MASKED).astype(jnp.bfloat16)


def prep(pair_rep, pair_bias, valid_here):
    heads, queries, keys = pair_bias.shape
    return pl.pallas_call(
        prep_kernel,
        out_shape=(
            jax.ShapeDtypeStruct(pair_rep.shape, jnp.bfloat16),
            jax.ShapeDtypeStruct((heads, keys, queries), jnp.bfloat16),
        ),
        in_specs=[
            pl.BlockSpec(memory_space=pltpu.SMEM),
            pl.BlockSpec(memory_space=pltpu.VMEM),
            pl.BlockSpec(memory_space=pltpu.VMEM),
        ],
        out_specs=(
            pl.BlockSpec(memory_space=pltpu.VMEM),
            pl.BlockSpec(memory_space=pltpu.VMEM),
        ),
        name="prep",
    )(valid_here, pair_rep, pair_bias)


def attend_kernel(
    groups_ref,
    start_ref,
    blocks_ref,
    order_ref,
    own_ref,
    near_ref,
    left_ref,
    right_ref,
    far_low_ref,
    far_high_ref,
    bias_ref,
    weight_ref,
    weight_t_ref,
    out_weight_ref,
    out_ref,
    packed,
    keys,
    values,
    queries,
    gates,
    gated,
    bias,
    shifted,
    sums,
    safe,
):
    rows, width = own_ref.shape[0], own_ref.shape[2]
    cols = own_ref.shape[1]
    chains = bias_ref.shape[0]
    inner = out_weight_ref.shape[0]
    heads = pl.num_programs(0)
    head = pl.program_id(0)
    head_size = inner // 4
    blocks = blocks_ref[0]
    total = blocks_ref[1]

    @pl.when(head == 0)
    def _():
        filler = jnp.zeros((GROUP, width), jnp.bfloat16)
        for row in range(rows):
            for group in range(BLOCK // GROUP):
                packed[row, pl.ds(pl.multiple_of(total + group * GROUP, GROUP), GROUP), :] = filler
        place = 0
        for pieces in (near_ref, left_ref, right_ref, far_low_ref, far_high_ref):
            for piece in range(pieces.shape[0]):
                for part in range(cols // SLOT):
                    chain = order_ref[place] * (cols // SLOT) + part
                    start = start_ref[chain]

                    def move(group, carry, pieces=pieces, piece=piece, part=part, start=start):
                        source = pl.multiple_of(part * SLOT + group * GROUP, GROUP)
                        target = pl.multiple_of(start + group * GROUP, GROUP)
                        for row in range(rows):
                            packed[row, pl.ds(target, GROUP), :] = pieces[
                                piece, row, pl.ds(source, GROUP), :
                            ]
                        return carry

                    lax.fori_loop(0, groups_ref[chain], move, 0)
                place += 1

        def project(block, peaks):
            fresh = []
            place = pl.ds(pl.multiple_of(block * BLOCK, BLOCK), BLOCK)
            for row in range(rows):
                part = packed[row, place, :]
                key_part = jnp.dot(
                    part, weight_ref[:, inner : 2 * inner], preferred_element_type=jnp.float32
                )
                keys[row, place, :] = key_part.astype(jnp.bfloat16)
                peak = jnp.max(jnp.abs(key_part).reshape(BLOCK // 8, 8, inner), axis=0)
                fresh.append(jnp.maximum(peaks[row], peak))
                turned = lax.dot_general(
                    weight_t_ref[2 * inner : 3 * inner, :],
                    part,
                    NT,
                    preferred_element_type=jnp.float32,
                ).astype(jnp.bfloat16)
                for h in range(4):
                    values[row, h, 0:head_size, place] = turned[h * head_size : (h + 1) * head_size]
                    values[row, h, head_size:, place] = jnp.ones(
                        (values.shape[2] - head_size, BLOCK), jnp.bfloat16
                    )
            return tuple(fresh)

        peaks = lax.fori_loop(
            0, blocks, project, tuple(jnp.zeros((8, inner), jnp.float32) for _ in range(rows))
        )
        reach = jnp.zeros((1, cols), jnp.float32)
        queries[...] = jnp.zeros_like(queries)
        for row in range(rows):
            own = own_ref[row]
            turned = lax.dot_general(
                weight_t_ref[0:inner, :], own, NT, preferred_element_type=jnp.float32
            )
            turned = (turned * head_size ** (-0.5)).astype(jnp.bfloat16)
            for h in range(4):
                span = slice(h * head_size, (h + 1) * head_size)
                queries[h, row, span, :] = turned[span]
            peak = jnp.max(peaks[row], axis=0, keepdims=True)
            peak = jnp.transpose(jnp.broadcast_to(peak, (inner, inner)))[:, 0:1]
            spread = jnp.abs(turned.astype(jnp.float32)) * peak
            for h in range(4):
                span = slice(h * head_size, (h + 1) * head_size)
                reach = jnp.maximum(reach, jnp.sum(spread[span], axis=0, keepdims=True))
            gate = jax.nn.sigmoid(
                lax.dot_general(
                    weight_t_ref[3 * inner : 4 * inner, :],
                    own,
                    NT,
                    preferred_element_type=jnp.float32,
                )
            )
            for h in range(4):
                gates[h, row] = gate[h * head_size : (h + 1) * head_size]
        safe[0] = (jnp.max(reach) < REACH).astype(jnp.int32)

    barrier = jnp.full((GROUP, cols), MASKED, jnp.bfloat16)
    for group in range(BLOCK // GROUP):
        bias[pl.ds(pl.multiple_of(total + group * GROUP, GROUP), GROUP), :] = barrier
    top = jnp.full((GROUP, cols), MASKED, jnp.bfloat16)
    for chain in range(chains):
        start = start_ref[chain]

        def move_bias(group, top, chain=chain, start=start):
            source = pl.multiple_of(group * GROUP, GROUP)
            target = pl.multiple_of(start + group * GROUP, GROUP)
            piece = bias_ref[chain, 0, pl.ds(source, GROUP), :]
            bias[pl.ds(target, GROUP), :] = piece
            return jnp.maximum(top, piece)

        top = lax.fori_loop(0, groups_ref[chain], move_bias, top)

    top = jnp.max(top.astype(jnp.float32), axis=0, keepdims=True)
    depth = values.shape[2]
    sums[...] = jnp.zeros_like(sums)

    @pl.when(safe[0] == 1)
    def _():
        def step(block, carry):
            place = pl.ds(pl.multiple_of(block * BLOCK, BLOCK), BLOCK)
            shifted[...] = (bias[place, :].astype(jnp.float32) - top) * LOG2E
            for pair in range(0, rows, PAIR):
                members = range(pair, pair + PAIR)
                scores = [
                    jnp.dot(
                        keys[row, place, :], queries[head, row], preferred_element_type=jnp.float32
                    )
                    for row in members
                ]
                weights = [
                    jnp.exp2(part * LOG2E + shifted[...]).astype(jnp.bfloat16) for part in scores
                ]
                for row, part in zip(members, weights):
                    sums[row] += jnp.dot(
                        values[row, head, :, place], part, preferred_element_type=jnp.float32
                    )
            return carry

        lax.fori_loop(0, blocks, step, 0)

    @pl.when(safe[0] == 0)
    def _():
        def step(block, state):
            place = pl.ds(pl.multiple_of(block * BLOCK, BLOCK), BLOCK)
            bias_block = bias[place, :].astype(jnp.float32)
            fresh = []
            for row in range(rows):
                scores = jnp.dot(
                    keys[row, place, :], queries[head, row], preferred_element_type=jnp.float32
                )
                scores = scores + bias_block
                new_max = jnp.maximum(state[row], jnp.max(scores, axis=0, keepdims=True))
                weights = jnp.exp(scores - new_max).astype(jnp.bfloat16)
                weighted = jnp.dot(
                    values[row, head, :, place], weights, preferred_element_type=jnp.float32
                )
                sums[row] = sums[row] * jnp.exp(state[row] - new_max) + weighted
                fresh.append(new_max)
            return tuple(fresh)

        lax.fori_loop(
            0,
            blocks,
            step,
            tuple(jnp.full((1, cols), -jnp.inf, jnp.float32) for _ in range(rows)),
        )

    for row in range(rows):
        total_row = sums[row]
        attended = total_row[0:head_size] / total_row[head_size : head_size + 1]
        gated[row, pl.ds(pl.multiple_of(head * head_size, head_size), head_size), :] = (
            attended * gates[head, row]
        ).astype(jnp.bfloat16)

    @pl.when(head == heads - 1)
    def _():
        for row in range(rows):
            out_ref[row] = lax.dot_general(
                gated[row], out_weight_ref[...], TN, preferred_element_type=jnp.float32
            ).astype(jnp.bfloat16)


def attend(normed, pieces, order, bias, project_weight, output_weight, chain_valid):
    rows, cols, width = normed.shape
    chains, heads, slot, _ = bias.shape
    inner = output_weight.shape[0]
    head_size = inner // heads
    groups = (chain_valid + GROUP - 1) // GROUP
    ends = jnp.cumsum(groups) * GROUP
    start = ends - groups * GROUP
    total = ends[-1]
    blocks = jnp.stack([(total + BLOCK - 1) // BLOCK, total])
    room = chains * slot + BLOCK
    depth = head_size + GROUP
    whole = lambda *shape: pl.BlockSpec(
        shape, lambda h, *_: (0,) * len(shape), pipeline_mode=pl.Buffered(1)
    )
    return pl.pallas_call(
        attend_kernel,
        grid_spec=pltpu.PrefetchScalarGridSpec(
            num_scalar_prefetch=4,
            grid=(heads,),
            in_specs=[
                whole(rows, cols, width),
                *(whole(*piece.shape) for piece in pieces),
                pl.BlockSpec((chains, 1, slot, cols), lambda h, *_: (0, h, 0, 0)),
                whole(width, 4 * inner),
                whole(4 * inner, width),
                whole(inner, output_weight.shape[1]),
            ],
            out_specs=pl.BlockSpec(
                (rows, cols, output_weight.shape[1]), lambda h, *_: (0, 0, 0)
            ),
            scratch_shapes=[
                pltpu.VMEM((rows, room, width), jnp.bfloat16),
                pltpu.VMEM((rows, room, inner), jnp.bfloat16),
                pltpu.VMEM((rows, heads, depth, room), jnp.bfloat16),
                pltpu.VMEM((heads, rows, inner, cols), jnp.bfloat16),
                pltpu.VMEM((heads, rows, head_size, cols), jnp.float32),
                pltpu.VMEM((rows, inner, cols), jnp.bfloat16),
                pltpu.VMEM((room, cols), jnp.bfloat16),
                pltpu.VMEM((BLOCK, cols), jnp.float32),
                pltpu.VMEM((rows, depth, cols), jnp.float32),
                pltpu.SMEM((1,), jnp.int32),
            ],
        ),
        out_shape=jax.ShapeDtypeStruct((rows, cols, output_weight.shape[1]), jnp.bfloat16),
        name="attend",
    )(
        groups,
        start,
        blocks,
        order,
        normed,
        *pieces,
        bias,
        project_weight,
        project_weight.T,
        output_weight,
    )


XS, YS = 4, 4


def shift(value, x_step, y_step):
    pairs = [
        (x * YS + y, (x + x_step) % XS * YS + (y + y_step) % YS)
        for x in range(XS)
        for y in range(YS)
    ]
    return lax.ppermute(value, "cols", pairs)


def gather_cols(own):
    above = shift(own, 0, 1)
    below = shift(own, 0, -1)
    across = shift(own, 0, 2)
    near = jnp.stack([own, above, below, across])
    left = shift(near, 1, 0)
    right = shift(near, -1, 0)
    far_low = shift(left[:2], 1, 0)
    far_high = shift(right[2:], -1, 0)
    here = lax.axis_index("cols")
    x, y = here // YS, here % YS
    y_of = jnp.stack([y, (y - 1) % YS, (y + 1) % YS, (y + 2) % YS])
    order = jnp.concatenate(
        [x * YS + y_of, (x - 1) % XS * YS + y_of, (x + 1) % XS * YS + y_of, (x + 2) % XS * YS + y_of]
    )
    return (near, left, right, far_low, far_high), order.astype(jnp.int32)


def local(pair_rep, project_weight, output_weight, pair_bias, chain_valid):
    here = lax.axis_index("rows")
    valid_here = lax.dynamic_slice_in_dim(chain_valid, here, 1, 0)
    normed, bias_t = prep(pair_rep, pair_bias, valid_here)
    bias = lax.all_gather(bias_t, "rows")
    pieces, order = gather_cols(normed)
    return attend(normed, pieces, order, bias, project_weight, output_weight, chain_valid)


def solution(mesh):
    return jax.shard_map(
        local,
        mesh=mesh,
        in_specs=(P("rows", "cols", None), P(), P(), P(None, "cols", "rows"), P()),
        out_specs=P("rows", "cols", None),
        check_vma=False,
    )
```

time: 817 us -> 139 us (0.17)
  waiting for transfers between devices: 677 us -> 53.5 us
  other arithmetic: 46.2 us -> 6.43 us
  local copies, waits for them, and re-layouts: 43.4 us -> 3.68 us
  matrix products: 32.4 us -> 0 us
  starting transfers between devices: 0.44 us -> 30.8 us
  Pallas kernels: 0 us -> 29.2 us
    all_gather x12 -> x1, waiting for transfers between devices: 673 us -> 9.45 us  [local(): bias = lax.all_gather(bias_t, 'rows')]
    ppermute x0 -> x7, waiting for transfers between devices: none -> 44 us  [shift(): return lax.ppermute(value, 'cols', pairs)]
    dynamic_slice x64 -> x1, local copies, waits for them, and re-layouts: 36.7 us -> 1.3 us  [local(): valid_here = lax.dynamic_slice_in_dim(chain_valid, here, 1, 0)]
    convert_element_type x34 -> x0, other arithmetic: 33.1 us -> none  [the longest x32 31.8 us: step(): bias_block.astype(jnp.float32)[None]]
    dot_general x66 -> x0, matrix products: 32.4 us -> none  [the longest x32 16.6 us: step(): jnp.einsum('rjd,rdk->rjk', query_head, key_block, preferred_element_type=...]
    ppermute x0 -> x7, starting transfers between devices: none -> 30.8 us  [shift(): return lax.ppermute(value, 'cols', pairs)]
    pallas_call x0 -> x2, Pallas kernels: none -> 29.2 us  [the longest x1 26.4 us: attend(): pl.pallas_call(attend_kernel, grid_spec=pltpu.PrefetchScalarGridSpec(num_...]
    reduce_sum x35 -> x0, other arithmetic: 12.2 us -> none  [the longest x32 9.58 us: step(): running_sum = running_sum * rescale + jnp.sum(weights, axis=2)]
  transfers between devices with their start and end apart: 12 -> 8, of which waited for: 12 -> 6; matrix products, arithmetic and copies ran while one was open for 11% -> 6% of each run, Pallas kernels for 0% -> 0%
where the time goes in v1:
time: 139 us; the launch traced here: 138 us
  waiting for transfers between devices  53.5 us (38%)
  starting transfers between devices  30.8 us (22%)
  Pallas kernels  29.2 us (21%)
  between operations  14.3 us (10%)
  other arithmetic  6.43 us (5%)
  local copies, waits for them, and re-layouts  3.68 us (3%)
    ppermute x7, waiting for transfers between devices, shift(): return lax.ppermute(value, 'cols', pairs)  44 us
    ppermute x7, starting transfers between devices, shift(): return lax.ppermute(value, 'cols', pairs)  30.8 us
    pallas_call x1, Pallas kernels, attend(): pl.pallas_call(attend_kernel, grid_spec=pltpu.PrefetchScalarGridSpec(num_...  26.4 us
    all_gather x1, waiting for transfers between devices, local(): bias = lax.all_gather(bias_t, 'rows')  9.45 us
    pallas_call x1, Pallas kernels, prep(): pl.pallas_call(prep_kernel, out_shape=(jax.ShapeDtypeStruct(pair_rep.shap...  2.79 us
  transfers between devices with their start and end apart: 8, of which 6 were waited for; matrix products, arithmetic and copies ran while one was open for 6% of the time, Pallas kernels for 0%

profile of v1, /device:TPU:1, one launch (start us, length us, event | category | flops | bytes accessed | tf_op | source)
XLA Modules:
  0.0 137.9 jit_solution(5721913067061952225)
XLA Ops:
  6.5 1.3 dynamic_slice.3.valid_ref
  7.8 2.8 %prep.1 = (bf16[4,256,128]{2,1,0:T(8,128)(2,1)}, bf16[4,128,256]{2,1,0:T(8,128)(2,1)}) custom-call(s32[1]{0:T(128)} %dynamic_slice.3.valid_ref, bf16[4,256,128]{2,1,0:T(8,128)(2,1)} %pair_ref.1, bf16[4,256,128]{2,1,0:T(8,128)(2,1)} %bias_ref.1), custom_call_target="tpu_custom_call" | custom-call | tf_op jit(solution)/shard_map/prep/pallas_call | solution.py:36
  10.7 6.7 %collective-permute-start.1 = (bf16[4,256,128]{2,1,0:T(8,128)(2,1)}, bf16[4,256,128]{2,1,0:T(8,128)(2,1)S(1)}, u32[]{:S(2)}, u32[]{:S(2)}) collective-permute-start(bf16[4,256,128]{2,1,0:T(8,128)(2,1)} %get-tuple-element.7.own_ref), channel_id=1, source_target_pairs={{0,3},{1,0},{2,1},{3,2},{4,7},{5,4},{6,5},{7,6},{8,11},{9,8},{10,9... | collective-permute-start | bytes 786440 | tf_op jit(solution)/shard_map/ppermute | solution.py:328
  17.4 3.5 %collective-permute-start.2 = (bf16[4,256,128]{2,1,0:T(8,128)(2,1)}, bf16[4,256,128]{2,1,0:T(8,128)(2,1)S(1)}, u32[]{:S(2)}, u32[]{:S(2)}) collective-permute-start(bf16[4,256,128]{2,1,0:T(8,128)(2,1)} %get-tuple-element.7.own_ref), channel_id=1, source_target_pairs={{0,2},{1,3},{2,0},{3,1},{4,6},{5,7},{6,4},{7,5},{8,10},{9,11},{10,... | collective-permute-start | bytes 786440 | tf_op jit(solution)/shard_map/ppermute | solution.py:328
  20.9 4.2 %collective-permute-start = (bf16[4,256,128]{2,1,0:T(8,128)(2,1)}, bf16[4,256,128]{2,1,0:T(8,128)(2,1)S(1)}, u32[]{:S(2)}, u32[]{:S(2)}) collective-permute-start(bf16[4,256,128]{2,1,0:T(8,128)(2,1)} %get-tuple-element.7.own_ref), channel_id=1, source_target_pairs={{0,1},{1,2},{2,3},{3,0},{4,5},{5,6},{6,7},{7,4},{8,9},{9,10},{10,1... | collective-permute-start | bytes 786440 | tf_op jit(solution)/shard_map/ppermute | solution.py:328
  25.1 8.4 %collective-permute-done.1 = bf16[4,256,128]{2,1,0:T(8,128)(2,1)S(1)} collective-permute-done((bf16[4,256,128]{2,1,0:T(8,128)(2,1)}, bf16[4,256,128]{2,1,0:T(8,128)(2,1)S(1)}, u32[]{:S(2)}, u32[]{:S(2)}) %collective-permute-start.1) | collective-permute-done | bytes 262176 | tf_op jit(solution)/shard_map/ppermute | solution.py:328
  33.5 15.7 %collective-permute-done = bf16[4,256,128]{2,1,0:T(8,128)(2,1)S(1)} collective-permute-done((bf16[4,256,128]{2,1,0:T(8,128)(2,1)}, bf16[4,256,128]{2,1,0:T(8,128)(2,1)S(1)}, u32[]{:S(2)}, u32[]{:S(2)}) %collective-permute-start) | collective-permute-done | bytes 262176 | tf_op jit(solution)/shard_map/ppermute | solution.py:328
  49.2 1.1 pad_maximum_fusion.near_ref
  50.4 5.4 %collective-permute-start.3 = (bf16[4,4,256,128]{3,2,1,0:T(8,128)(2,1)S(1)}, bf16[4,4,256,128]{3,2,1,0:T(8,128)(2,1)S(1)}, u32[]{:S(2)}, u32[]{:S(2)}) collective-permute-start(bf16[4,4,256,128]{3,2,1,0:T(8,128)(2,1)S(1)} %pad_maximum_fusion.near_ref), channel_id=1, source_target_pairs={{0,4},{1,5},{2,6},{3,7},{4,8},{5,9},{6,10},{7,11},{8,12},{9,13},{1... | collective-permute-start | bytes 3145736 | tf_op jit(solution)/shard_map/ppermute | solution.py:328
  55.7 3.2 %collective-permute-start.4 = (bf16[4,4,256,128]{3,2,1,0:T(8,128)(2,1)S(1)}, bf16[4,4,256,128]{3,2,1,0:T(8,128)(2,1)S(1)}, u32[]{:S(2)}, u32[]{:S(2)}) collective-permute-start(bf16[4,4,256,128]{3,2,1,0:T(8,128)(2,1)S(1)} %pad_maximum_fusion.near_ref), channel_id=1, source_target_pairs={{0,12},{1,13},{2,14},{3,15},{4,0},{5,1},{6,2},{7,3},{8,4},{9,5},{1... | collective-permute-start | bytes 3145736 | tf_op jit(solution)/shard_map/ppermute | solution.py:328
  59.1 0.7 fusion.1
  60.0 0.5 slice.16
  61.2 1.7 %copy.11 = bf16[128,512]{0,1:T(8,128)(2,1)} copy(bf16[128,512]{1,0:T(8,128)(2,1)} %weight_ref.1) | data formatting | bytes 262144 | tf_op args[1]
  62.9 1.3 pad_add_fusion.blocks_ref
  64.2 12.9 %collective-permute-done.3.left_ref = bf16[4,4,256,128]{3,2,1,0:T(8,128)(2,1)S(1)} collective-permute-done((bf16[4,4,256,128]{3,2,1,0:T(8,128)(2,1)S(1)}, bf16[4,4,256,128]{3,2,1,0:T(8,128)(2,1)S(1)}, u32[]{:S(2)}, u32[]{:S(2)}) %collective-permute-start.3) | collective-permute-done | bytes 1048608 | tf_op jit(solution)/shard_map/ppermute | solution.py:328
  77.1 3.8 %collective-permute-start.5 = (bf16[2,4,256,128]{3,2,1,0:T(8,128)(2,1)S(1)}, bf16[2,4,256,128]{3,2,1,0:T(8,128)(2,1)}, u32[]{:S(2)}, u32[]{:S(2)}) collective-permute-start(bf16[2,4,256,128]{3,2,1,0:T(8,128)(2,1)S(1)} %slice.17), channel_id=1, source_target_pairs={{0,4},{1,5},{2,6},{3,7},{4,8},{5,9},{6,10},{7,11},{8,12},{9,13},{1... | collective-permute-start | bytes 1572872 | tf_op jit(solution)/shard_map/ppermute | solution.py:328
  81.0 4.0 %collective-permute-start.6 = (bf16[2,4,256,128]{3,2,1,0:T(8,128)(2,1)S(1)}, bf16[2,4,256,128]{3,2,1,0:T(8,128)(2,1)}, u32[]{:S(2)}, u32[]{:S(2)}) collective-permute-start(bf16[2,4,256,128]{3,2,1,0:T(8,128)(2,1)S(1)} %slice.18), channel_id=1, source_target_pairs={{0,12},{1,13},{2,14},{3,15},{4,0},{5,1},{6,2},{7,3},{8,4},{9,5},{1... | collective-permute-start | bytes 1572872 | tf_op jit(solution)/shard_map/ppermute | solution.py:328
  85.0 0.7 pad_add_fusion.2.order_ref
  85.7 1.2 and_select_fusion.groups_ref
  86.9 1.2 multiply_subtract_fusion.start_ref
  88.1 4.2 %collective-permute-done.5.far_low_ref = bf16[2,4,256,128]{3,2,1,0:T(8,128)(2,1)} collective-permute-done((bf16[2,4,256,128]{3,2,1,0:T(8,128)(2,1)S(1)}, bf16[2,4,256,128]{3,2,1,0:T(8,128)(2,1)}, u32[]{:S(2)}, u32[]{:S(2)}) %collective-permute-start.5) | collective-permute-done | bytes 524320 | tf_op jit(solution)/shard_map/ppermute | solution.py:328
  92.4 2.8 %collective-permute-done.6.far_high_ref = bf16[2,4,256,128]{3,2,1,0:T(8,128)(2,1)} collective-permute-done((bf16[2,4,256,128]{3,2,1,0:T(8,128)(2,1)S(1)}, bf16[2,4,256,128]{3,2,1,0:T(8,128)(2,1)}, u32[]{:S(2)}, u32[]{:S(2)}) %collective-permute-start.6) | collective-permute-done | bytes 524320 | tf_op jit(solution)/shard_map/ppermute | solution.py:328
  95.2 9.5 %all-gather.3.cloned.1.call-done = bf16[128,128,256]{2,1,0:T(8,128)(2,1)} async-done(((bf16[4,128,256]{2,1,0:T(8,128)(2,1)}), bf16[128,128,256]{2,1,0:T(8,128)(2,1)}) %all-gather.3.cloned.1.call-update) | async-done | bytes 8388624 | tf_op jit(solution)/shard_map/all_gather | solution.py:353
  104.6 26.4 %attend.1 = bf16[4,256,128]{2,1,0:T(8,128)(2,1)} custom-call(s32[32]{0:T(128)} %and_select_fusion.groups_ref, s32[32]{0:T(128)} %multiply_subtract_fusion.start_ref, s32[2]{0:T(128)} %pad_add_fusion.blocks_ref, s32[16]{0:T(128)} %pad_add_fusion.2.order_ref, bf16[4,256,128]{2,1,0:T(8,128)(2,1)} %get-tuple-element.7.own_ref, bf16[4,4,256,128]{3,2,1,0:T(8,128)(2,1)} %copy-done, ...), custom_call_target="tpu_custom_call" | custom-call | tf_op jit(solution)/shard_map/attend/pallas_call | solution.py:274
  (17 shorter events, 0.4 us)
Async XLA Ops:
  6.5 98.1 %all-gather.3.cloned.1.call-start = ((), (), s32[]{:S(2)}) async-start(), calls=%async_computation | async-start | bytes 8650752 | tf_op jit(solution)/shard_map/all_gather | solution.py:353
  10.7 22.9 %collective-permute-start.1 = (bf16[4,256,128]{2,1,0:T(8,128)(2,1)}, bf16[4,256,128]{2,1,0:T(8,128)(2,1)S(1)}, u32[]{:S(2)}, u32[]{:S(2)}) collective-permute-start(bf16[4,256,128]{2,1,0:T(8,128)(2,1)} %get-tuple-element.7.own_ref), channel_id=1, source_target_pairs={{0,3},{1,0},{2,1},{3,2},{4,7},{5,4},{6,5},{7,6},{8,11},{9,8},{10,9... | collective-permute-start | bytes 786440 | tf_op jit(solution)/shard_map/ppermute | solution.py:328
  17.4 16.2 %collective-permute-start.2 = (bf16[4,256,128]{2,1,0:T(8,128)(2,1)}, bf16[4,256,128]{2,1,0:T(8,128)(2,1)S(1)}, u32[]{:S(2)}, u32[]{:S(2)}) collective-permute-start(bf16[4,256,128]{2,1,0:T(8,128)(2,1)} %get-tuple-element.7.own_ref), channel_id=1, source_target_pairs={{0,2},{1,3},{2,0},{3,1},{4,6},{5,7},{6,4},{7,5},{8,10},{9,11},{10,... | collective-permute-start | bytes 786440 | tf_op jit(solution)/shard_map/ppermute | solution.py:328
  20.9 28.3 %collective-permute-start = (bf16[4,256,128]{2,1,0:T(8,128)(2,1)}, bf16[4,256,128]{2,1,0:T(8,128)(2,1)S(1)}, u32[]{:S(2)}, u32[]{:S(2)}) collective-permute-start(bf16[4,256,128]{2,1,0:T(8,128)(2,1)} %get-tuple-element.7.own_ref), channel_id=1, source_target_pairs={{0,1},{1,2},{2,3},{3,0},{4,5},{5,6},{6,7},{7,4},{8,9},{9,10},{10,1... | collective-permute-start | bytes 786440 | tf_op jit(solution)/shard_map/ppermute | solution.py:328
  50.3 54.3 %copy-start = (bf16[4,4,256,128]{3,2,1,0:T(8,128)(2,1)}, bf16[4,4,256,128]{3,2,1,0:T(8,128)(2,1)S(1)}, u32[]{:S(2)}) copy-start(bf16[4,4,256,128]{3,2,1,0:T(8,128)(2,1)S(1)} %pad_maximum_fusion.near_ref) | copy-start | bytes 3145732
  50.4 26.7 %collective-permute-start.3 = (bf16[4,4,256,128]{3,2,1,0:T(8,128)(2,1)S(1)}, bf16[4,4,256,128]{3,2,1,0:T(8,128)(2,1)S(1)}, u32[]{:S(2)}, u32[]{:S(2)}) collective-permute-start(bf16[4,4,256,128]{3,2,1,0:T(8,128)(2,1)S(1)} %pad_maximum_fusion.near_ref), channel_id=1, source_target_pairs={{0,4},{1,5},{2,6},{3,7},{4,8},{5,9},{6,10},{7,11},{8,12},{9,13},{1... | collective-permute-start | bytes 3145736 | tf_op jit(solution)/shard_map/ppermute | solution.py:328
  55.7 25.2 %collective-permute-start.4 = (bf16[4,4,256,128]{3,2,1,0:T(8,128)(2,1)S(1)}, bf16[4,4,256,128]{3,2,1,0:T(8,128)(2,1)S(1)}, u32[]{:S(2)}, u32[]{:S(2)}) collective-permute-start(bf16[4,4,256,128]{3,2,1,0:T(8,128)(2,1)S(1)} %pad_maximum_fusion.near_ref), channel_id=1, source_target_pairs={{0,12},{1,13},{2,14},{3,15},{4,0},{5,1},{6,2},{7,3},{8,4},{9,5},{1... | collective-permute-start | bytes 3145736 | tf_op jit(solution)/shard_map/ppermute | solution.py:328
  77.1 27.5 %copy-start.1 = (bf16[4,4,256,128]{3,2,1,0:T(8,128)(2,1)}, bf16[4,4,256,128]{3,2,1,0:T(8,128)(2,1)S(1)}, u32[]{:S(2)}) copy-start(bf16[4,4,256,128]{3,2,1,0:T(8,128)(2,1)S(1)} %collective-permute-done.3.left_ref) | copy-start | bytes 3145732
  77.1 15.2 %collective-permute-start.5 = (bf16[2,4,256,128]{3,2,1,0:T(8,128)(2,1)S(1)}, bf16[2,4,256,128]{3,2,1,0:T(8,128)(2,1)}, u32[]{:S(2)}, u32[]{:S(2)}) collective-permute-start(bf16[2,4,256,128]{3,2,1,0:T(8,128)(2,1)S(1)} %slice.17), channel_id=1, source_target_pairs={{0,4},{1,5},{2,6},{3,7},{4,8},{5,9},{6,10},{7,11},{8,12},{9,13},{1... | collective-permute-start | bytes 1572872 | tf_op jit(solution)/shard_map/ppermute | solution.py:328
  80.9 23.7 %copy-start.2 = (bf16[4,4,256,128]{3,2,1,0:T(8,128)(2,1)}, bf16[4,4,256,128]{3,2,1,0:T(8,128)(2,1)S(1)}, u32[]{:S(2)}) copy-start(bf16[4,4,256,128]{3,2,1,0:T(8,128)(2,1)S(1)} %collective-permute-done.4.right_ref) | copy-start | bytes 3145732
  81.0 14.2 %collective-permute-start.6 = (bf16[2,4,256,128]{3,2,1,0:T(8,128)(2,1)S(1)}, bf16[2,4,256,128]{3,2,1,0:T(8,128)(2,1)}, u32[]{:S(2)}, u32[]{:S(2)}) collective-permute-start(bf16[2,4,256,128]{3,2,1,0:T(8,128)(2,1)S(1)} %slice.18), channel_id=1, source_target_pairs={{0,12},{1,13},{2,14},{3,15},{4,0},{5,1},{6,2},{7,3},{8,4},{9,5},{1... | collective-permute-start | bytes 1572872 | tf_op jit(solution)/shard_map/ppermute | solution.py:328
Sparse Core Ops, SparseCore 0:
  10.8 93.7 all-gather.2

commit v2 on v0

v2 whole, which is shorter than its diff:
```python
import jax
import jax.numpy as jnp
from jax import lax
from jax.experimental import pallas as pl
from jax.experimental.pallas import tpu as pltpu
from jax.sharding import PartitionSpec as P


SLOT = 128
GROUP = 16
BLOCK = 256
MASKED = -1000000000.0
LOG2E = 1.4426950408889634
REACH = 60.0
PAIR = 4
XS, YS = 4, 4
PER_COL = 2
NEAR = 12 * PER_COL
FAR = 4 * PER_COL
NEAR_ROOM = NEAR * SLOT + BLOCK
FAR_ROOM = FAR * SLOT + BLOCK
ROOM = NEAR_ROOM + FAR_ROOM

NT = (((1,), (1,)), ((), ()))
TN = (((0,), (0,)), ((), ()))

SMEM = pl.BlockSpec(memory_space=pltpu.SMEM)
VMEM = pl.BlockSpec(memory_space=pltpu.VMEM)


def prep_kernel(valid_ref, pair_ref, bias_ref, normed_ref, biast_ref):
    pair = pair_ref[...].astype(jnp.float32)
    center = jnp.mean(pair, axis=-1, keepdims=True)
    spread = jnp.mean(jnp.square(pair - center), axis=-1, keepdims=True)
    normed_ref[...] = ((pair - center) * lax.rsqrt(spread + 1e-05)).astype(jnp.bfloat16)
    heads, queries, keys = bias_ref.shape
    valid = valid_ref[lax.axis_index("rows")]
    live = lax.broadcasted_iota(jnp.int32, (keys, queries), 0) < valid
    for head in range(heads):
        turned = jnp.transpose(bias_ref[head].astype(jnp.float32))
        biast_ref[head] = jnp.where(live, turned, MASKED).astype(jnp.bfloat16)


def prep(pair_rep, pair_bias, chain_valid):
    heads, queries, keys = pair_bias.shape
    return pl.pallas_call(
        prep_kernel,
        out_shape=(
            jax.ShapeDtypeStruct(pair_rep.shape, jnp.bfloat16),
            jax.ShapeDtypeStruct((heads, keys, queries), jnp.bfloat16),
        ),
        in_specs=[SMEM, VMEM, VMEM],
        out_specs=(VMEM, VMEM),
        name="prep",
    )(chain_valid, pair_rep, pair_bias)


def chart(valid_ref, table, places):
    col = lax.axis_index("cols")
    x, y = col >> 2, col & 3
    total = jnp.int32(0)
    for place in places:
        x_step = (0, 3, 1, 2)[place // (YS * PER_COL)]
        y_step = (0, 3, 1, 2)[place // PER_COL % YS]
        from_col = ((x + x_step) & (XS - 1)) * YS + ((y + y_step) & (YS - 1))
        chain = from_col * PER_COL + place % PER_COL
        table[0, place] = total
        table[1, place] = chain
        total = total + ((valid_ref[chain] + (GROUP - 1)) >> 4 << 4)
    table[2, places[0]] = total


def pack(table, places, refs, row, packed):
    sources = [
        (ref, piece, part)
        for ref in refs
        for piece in range(ref.shape[0])
        for part in range(PER_COL)
    ]
    total = table[2, places[0]]
    for (ref, piece, part), place in zip(sources, places):
        packed[pl.ds(pl.multiple_of(table[0, place], GROUP), SLOT), :] = ref[
            piece, row, part * SLOT : (part + 1) * SLOT, :
        ]
    packed[pl.ds(pl.multiple_of(total, GROUP), BLOCK), :] = jnp.zeros(
        (BLOCK, packed.shape[1]), jnp.bfloat16
    )


def project(packed, weight_ref, weight_t_ref, blocks, base, keys, values, peak):
    inner = weight_ref.shape[1] // 4
    heads, depth = values.shape[0], values.shape[1]
    head_size = inner // heads

    def step(block, peak):
        source = pl.ds(pl.multiple_of(block * BLOCK, BLOCK), BLOCK)
        place = pl.ds(pl.multiple_of(base + block * BLOCK, BLOCK), BLOCK)
        part = packed[source, :]
        key_part = jnp.dot(
            part, weight_ref[:, inner : 2 * inner], preferred_element_type=jnp.float32
        )
        turned = lax.dot_general(
            weight_t_ref[2 * inner : 3 * inner, :], part, NT, preferred_element_type=jnp.float32
        ).astype(jnp.bfloat16)
        keys[place, :] = key_part.astype(jnp.bfloat16)
        for h in range(heads):
            values[h, 0:head_size, place] = turned[h * head_size : (h + 1) * head_size]
            values[h, head_size:, place] = jnp.ones((depth - head_size, BLOCK), jnp.bfloat16)
        return jnp.maximum(
            peak, jnp.max(jnp.abs(key_part).reshape(BLOCK // 8, 8, inner), axis=0)
        )

    return lax.fori_loop(0, blocks, step, peak)


def near_kernel(
    valid_ref,
    own_ref,
    near_ref,
    left_ref,
    right_ref,
    weight_ref,
    weight_t_ref,
    keys_ref,
    values_ref,
    queries_ref,
    gates_ref,
    peaks_ref,
    packed,
    table,
):
    heads = queries_ref.shape[0]
    inner = queries_ref.shape[2]
    head_size = inner // heads
    own = own_ref[0]
    turned = lax.dot_general(weight_t_ref[0:inner, :], own, NT, preferred_element_type=jnp.float32)
    turned = (turned * head_size ** (-0.5)).astype(jnp.bfloat16)
    gate = jax.nn.sigmoid(
        lax.dot_general(
            weight_t_ref[3 * inner : 4 * inner, :], own, NT, preferred_element_type=jnp.float32
        )
    )
    queries_ref[...] = jnp.zeros_like(queries_ref)
    for h in range(heads):
        span = slice(h * head_size, (h + 1) * head_size)
        queries_ref[h, 0, span, :] = turned[span]
        gates_ref[h, 0] = gate[span]
    places = range(NEAR)

    @pl.when(pl.program_id(0) == 0)
    def _():
        chart(valid_ref, table, places)

    pack(table, places, (near_ref, left_ref, right_ref), 0, packed)
    blocks = (table[2, 0] + (BLOCK - 1)) >> 8
    peaks_ref[0] = project(
        packed,
        weight_ref,
        weight_t_ref,
        blocks,
        0,
        keys_ref.at[0],
        values_ref.at[0],
        jnp.zeros((8, inner), jnp.float32),
    )


def piece_spec(piece):
    count, _, cols, width = piece.shape
    return pl.BlockSpec((count, 1, cols, width), lambda i: (0, i, 0, 0))


def fixed(array):
    zeros = (0,) * array.ndim
    return pl.BlockSpec(array.shape, lambda i: zeros, pipeline_mode=pl.Buffered(1))


def project_near(chain_valid, normed, pieces, weight, weight_t, heads):
    rows, cols, width = normed.shape
    inner = weight.shape[1] // 4
    head_size = inner // heads
    depth = head_size + GROUP
    return pl.pallas_call(
        near_kernel,
        grid=(rows,),
        in_specs=[
            SMEM,
            pl.BlockSpec((1, cols, width), lambda i: (i, 0, 0)),
            *(piece_spec(piece) for piece in pieces),
            fixed(weight),
            fixed(weight_t),
        ],
        out_specs=(
            pl.BlockSpec((1, NEAR_ROOM, inner), lambda i: (i, 0, 0)),
            pl.BlockSpec((1, heads, depth, NEAR_ROOM), lambda i: (i, 0, 0, 0)),
            pl.BlockSpec((heads, 1, inner, cols), lambda i: (0, i, 0, 0)),
            pl.BlockSpec((heads, 1, head_size, cols), lambda i: (0, i, 0, 0)),
            pl.BlockSpec((1, 8, inner), lambda i: (i, 0, 0)),
        ),
        out_shape=(
            jax.ShapeDtypeStruct((rows, NEAR_ROOM, inner), jnp.bfloat16),
            jax.ShapeDtypeStruct((rows, heads, depth, NEAR_ROOM), jnp.bfloat16),
            jax.ShapeDtypeStruct((heads, rows, inner, cols), jnp.bfloat16),
            jax.ShapeDtypeStruct((heads, rows, head_size, cols), jnp.float32),
            jax.ShapeDtypeStruct((rows, 8, inner), jnp.float32),
        ),
        scratch_shapes=[
            pltpu.VMEM((NEAR * SLOT + BLOCK, width), jnp.bfloat16),
            pltpu.SMEM((3, NEAR + FAR), jnp.int32),
        ],
        name="near",
    )(chain_valid, normed, *pieces, weight, weight_t)


def attend_kernel(
    valid_ref,
    keys_hbm,
    values_hbm,
    low_ref,
    high_ref,
    weight_ref,
    weight_t_ref,
    queries,
    peaks_ref,
    gates,
    bias_ref,
    out_weight_ref,
    out_ref,
    keys,
    values,
    packed,
    gated,
    bias,
    shifted,
    sums,
    table,
    safe,
    sems,
):
    heads, rows, inner, cols = queries.shape
    head_size = inner // heads
    head = pl.program_id(0)
    half = bias_ref.shape[0]
    y_low = lax.axis_index("rows") >> 4
    spans = ((0, range(NEAR)), (NEAR_ROOM, range(NEAR, NEAR + FAR)))
    key_copy = pltpu.make_async_copy(keys_hbm, keys.at[:, pl.ds(0, NEAR_ROOM), :], sems.at[heads])

    def value_copy(h):
        return pltpu.make_async_copy(
            values_hbm.at[:, h], values.at[:, h, :, pl.ds(0, NEAR_ROOM)], sems.at[h]
        )

    @pl.when(head == 0)
    def _():
        key_copy.start()
        for h in range(heads):
            value_copy(h).start()
        for _, places in spans:
            chart(valid_ref, table, places)
        far = range(NEAR, NEAR + FAR)
        blocks = (table[2, NEAR] + (BLOCK - 1)) >> 8
        best = jnp.float32(0.0)
        for row in range(rows):
            pack(table, far, (low_ref, high_ref), row, packed)
            peak = project(
                packed,
                weight_ref,
                weight_t_ref,
                blocks,
                NEAR_ROOM,
                keys.at[row],
                values.at[row],
                peaks_ref[row],
            )
            peak = jnp.max(peak, axis=0, keepdims=True)
            peak = jnp.transpose(jnp.broadcast_to(peak, (inner, inner)))[:, 0:1]
            for h in range(heads):
                span = slice(h * head_size, (h + 1) * head_size)
                spread = jnp.abs(queries[h, row, span, :].astype(jnp.float32)) * peak[span]
                best = jnp.maximum(best, jnp.max(jnp.sum(spread, axis=0, keepdims=True)))
        safe[0] = (best < REACH).astype(jnp.int32)
        key_copy.wait()

    for h in range(heads):

        @pl.when(head == h)
        def _(h=h):
            value_copy(h).wait()

    top = jnp.full((GROUP, cols), MASKED, jnp.bfloat16)
    counts = []
    for base, places in spans:
        total = table[2, places[0]]

        def move(place, top, base=base):
            start, chain = table[0, place], table[1, place]
            piece = bias_ref[chain & (half - 1), (chain >> 4) ^ y_low, 0]
            bias[pl.ds(pl.multiple_of(base + start, GROUP), SLOT), :] = piece
            for group in range(0, SLOT, GROUP):
                top = jnp.maximum(top, piece[group : group + GROUP])
            return top

        top = lax.fori_loop(places[0], places[-1] + 1, move, top)
        bias[pl.ds(pl.multiple_of(base + total, GROUP), BLOCK), :] = jnp.full(
            (BLOCK, cols), MASKED, jnp.bfloat16
        )
        counts.append((total + (BLOCK - 1)) >> 8)
    near_blocks, blocks = counts[0], counts[0] + counts[1]
    top = jnp.max(top.astype(jnp.float32), axis=0, keepdims=True)
    sums[...] = jnp.zeros_like(sums)

    def place_of(block):
        block = jnp.where(block < near_blocks, block, block - near_blocks + NEAR_ROOM // BLOCK)
        return pl.ds(pl.multiple_of(block * BLOCK, BLOCK), BLOCK)

    @pl.when(safe[0] == 1)
    def _():
        def step(block, carry):
            place = place_of(block)
            shifted[...] = (bias[place, :].astype(jnp.float32) - top) * LOG2E
            for pair in range(0, rows, PAIR):
                members = range(pair, pair + PAIR)
                scores = [
                    jnp.dot(keys[row, place, :], queries[head, row], preferred_element_type=jnp.float32)
                    for row in members
                ]
                weights = [
                    jnp.exp2(part * LOG2E + shifted[...]).astype(jnp.bfloat16) for part in scores
                ]
                for row, part in zip(members, weights):
                    sums[row] += jnp.dot(
                        values[row, head, :, place], part, preferred_element_type=jnp.float32
                    )
            return carry

        lax.fori_loop(0, blocks, step, 0)

    @pl.when(safe[0] == 0)
    def _():
        def step(block, state):
            place = place_of(block)
            bias_block = bias[place, :].astype(jnp.float32)
            fresh = []
            for row in range(rows):
                scores = jnp.dot(
                    keys[row, place, :], queries[head, row], preferred_element_type=jnp.float32
                )
                scores = scores + bias_block
                new_max = jnp.maximum(state[row], jnp.max(scores, axis=0, keepdims=True))
                weights = jnp.exp(scores - new_max).astype(jnp.bfloat16)
                weighted = jnp.dot(
                    values[row, head, :, place], weights, preferred_element_type=jnp.float32
                )
                sums[row] = sums[row] * jnp.exp(state[row] - new_max) + weighted
                fresh.append(new_max)
            return tuple(fresh)

        lax.fori_loop(
            0,
            blocks,
            step,
            tuple(jnp.full((1, cols), -jnp.inf, jnp.float32) for _ in range(rows)),
        )

    for row in range(rows):
        total_row = sums[row]
        attended = total_row[0:head_size] / total_row[head_size : head_size + 1]
        gated[row, pl.ds(pl.multiple_of(head * head_size, head_size), head_size), :] = (
            attended * gates[0, row]
        ).astype(jnp.bfloat16)

    @pl.when(head == heads - 1)
    def _():
        for row in range(rows):
            out_ref[row] = lax.dot_general(
                gated[row], out_weight_ref[...], TN, preferred_element_type=jnp.float32
            ).astype(jnp.bfloat16)


def attend(
    chain_valid, keys, values, far, weight, weight_t, queries, peaks, gates, bias, output_weight
):
    heads, rows, inner, cols = queries.shape
    depth = values.shape[2]
    half, pair, _, slot, _ = bias.shape
    width = output_weight.shape[1]
    return pl.pallas_call(
        attend_kernel,
        grid=(heads,),
        in_specs=[
            SMEM,
            pl.BlockSpec(memory_space=pl.ANY),
            pl.BlockSpec(memory_space=pl.ANY),
            *(fixed(piece) for piece in far),
            fixed(weight),
            fixed(weight_t),
            fixed(queries),
            fixed(peaks),
            pl.BlockSpec((1, rows, inner // heads, cols), lambda h: (h, 0, 0, 0)),
            pl.BlockSpec((half, pair, 1, slot, cols), lambda h: (0, 0, h, 0, 0)),
            fixed(output_weight),
        ],
        out_specs=pl.BlockSpec((rows, cols, width), lambda h: (0, 0, 0)),
        scratch_shapes=[
            pltpu.VMEM((rows, ROOM, inner), jnp.bfloat16),
            pltpu.VMEM((rows, heads, depth, ROOM), jnp.bfloat16),
            pltpu.VMEM((FAR_ROOM, weight.shape[0]), jnp.bfloat16),
            pltpu.VMEM((rows, inner, cols), jnp.bfloat16),
            pltpu.VMEM((ROOM, cols), jnp.bfloat16),
            pltpu.VMEM((BLOCK, cols), jnp.float32),
            pltpu.VMEM((rows, depth, cols), jnp.float32),
            pltpu.SMEM((3, NEAR + FAR), jnp.int32),
            pltpu.SMEM((1,), jnp.int32),
            pltpu.SemaphoreType.DMA((heads + 1,)),
        ],
        out_shape=jax.ShapeDtypeStruct((rows, cols, width), jnp.bfloat16),
        name="attend",
    )(
        chain_valid,
        keys,
        values,
        *far,
        weight,
        weight_t,
        queries,
        peaks,
        gates,
        bias,
        output_weight,
    )


def shift(value, x_step, y_step):
    pairs = [
        (x * YS + y, (x + x_step) % XS * YS + (y + y_step) % YS)
        for x in range(XS)
        for y in range(YS)
    ]
    return lax.ppermute(value, "cols", pairs)


def gather_bias(bias_t):
    count = lax.axis_size("rows")
    half = count // 2
    swapped = lax.ppermute(bias_t, "rows", [(r, (r + half) % count) for r in range(count)])
    both = jnp.stack([bias_t, swapped])
    groups = [list(range(half)), list(range(half, count))]
    return lax.all_gather(both, "rows", axis_index_groups=groups)


def finish(chain_valid, normed, near, far, bias, project_weight, output_weight, heads):
    weight_t = project_weight.T
    keys, values, queries, gates, peaks = project_near(
        chain_valid, normed, near, project_weight, weight_t, heads
    )
    return attend(
        chain_valid,
        keys,
        values,
        far,
        project_weight,
        weight_t,
        queries,
        peaks,
        gates,
        bias,
        output_weight,
    )


def local(pair_rep, project_weight, output_weight, pair_bias, chain_valid):
    normed, bias_t = prep(pair_rep, pair_bias, chain_valid)
    bias = gather_bias(bias_t)
    above = shift(normed, 0, 1)
    below = shift(normed, 0, -1)
    across = shift(normed, 0, 2)
    near = jnp.stack([normed, above, below, across])
    left = shift(near, 1, 0)
    right = shift(near, -1, 0)
    far_low = shift(left[:2], 1, 0)
    far_high = shift(right[2:], -1, 0)
    return finish(
        chain_valid,
        normed,
        (near, left, right),
        (far_low, far_high),
        bias,
        project_weight,
        output_weight,
        pair_bias.shape[0],
    )


def solution(mesh):
    return jax.shard_map(
        local,
        mesh=mesh,
        in_specs=(P("rows", "cols", None), P(), P(), P(None, "cols", "rows"), P()),
        out_specs=P("rows", "cols", None),
        check_vma=False,
    )
```

time: 817 us -> 139 us (0.17)
  the two profiles are of different devices: /device:TPU:1 before, /device:TPU:136 now
where the time goes in v2:
time: 139 us; the launch traced here: 138 us
  waiting for transfers between devices  47.3 us (34%)
  Pallas kernels  41 us (29%)
  starting transfers between devices  31.2 us (22%)
  between operations  13.5 us (10%)
  other arithmetic  2.89 us (2%)
  local copies, waits for them, and re-layouts  2.52 us (2%)
    ppermute x7, waiting for transfers between devices, shift(): return lax.ppermute(value, 'cols', pairs)  39.5 us
    ppermute x7, starting transfers between devices, shift(): return lax.ppermute(value, 'cols', pairs)  28.9 us
    pallas_call x1, Pallas kernels, attend(): pl.pallas_call(attend_kernel, grid=(heads,), in_specs=[SMEM, pl.BlockSpec...  28.8 us
    pallas_call x1, Pallas kernels, project_near(): pl.pallas_call(near_kernel, grid=(rows,), in_specs=[SMEM, pl.BlockSpec((1...  9.94 us
    ppermute x1, waiting for transfers between devices, gather_bias(): lax.ppermute(bias_t, 'rows', [(r, (r + half) % count) for r in range(coun...  7.78 us
  transfers between devices with their start and end apart: 9, of which 4 were waited for; matrix products, arithmetic and copies ran while one was open for 3% of the time, Pallas kernels for 7%

profile of v2, /device:TPU:136, one launch (start us, length us, event | category | flops | bytes accessed | tf_op | source)
XLA Modules:
  0.0 138.4 jit_solution(12102885288863787064)
XLA Ops:
  6.5 2.2 %prep.1 = (bf16[4,256,128]{2,1,0:T(8,128)(2,1)}, bf16[4,128,256]{2,1,0:T(8,128)(2,1)}) custom-call(s32[32]{0:T(128)} %valid_ref.5, bf16[4,256,128]{2,1,0:T(8,128)(2,1)} %pair_ref.1, bf16[4,256,128]{2,1,0:T(8,128)(2,1)} %bias_ref.1), custom_call_target="tpu_custom_call" | custom-call | tf_op jit(solution)/shard_map/prep/pallas_call | solution.py:46
  8.8 2.3 %collective-permute-start.7 = (bf16[4,128,256]{2,1,0:T(8,128)(2,1)}, bf16[4,128,256]{2,1,0:T(8,128)(2,1)S(1)}, u32[]{:S(2)}, u32[]{:S(2)}) collective-permute-start(bf16[4,128,256]{2,1,0:T(8,128)(2,1)} %get-tuple-element.18), channel_id=1, source_target_pairs={{0,256},{16,272},{32,288},{48,304},{64,320},{80,336},{96,352},{112... | collective-permute-start | bytes 786440 | tf_op jit(solution)/shard_map/ppermute | solution.py:445
  11.1 7.8 %collective-permute-done.7 = bf16[4,128,256]{2,1,0:T(8,128)(2,1)S(1)} collective-permute-done((bf16[4,128,256]{2,1,0:T(8,128)(2,1)}, bf16[4,128,256]{2,1,0:T(8,128)(2,1)S(1)}, u32[]{:S(2)}, u32[]{:S(2)}) %collective-permute-start.7) | collective-permute-done | bytes 262176 | tf_op jit(solution)/shard_map/ppermute | solution.py:445
  18.9 1.8 %pad_maximum_fusion.1 = bf16[2,4,128,256]{3,2,1,0:T(8,128)(2,1)} fusion(bf16[1,4,128,256]{3,2,1,0:T(8,128)(2,1)S(1)} %bitcast.13, bf16[1,4,128,256]{3,2,1,0:T(8,128)(2,1)} %bitcast.12), kind=kLoop, calls=%fused_computation.1 | loop fusion | flops 262144 | bytes 1048576 | tf_op jit(solution)/shard_map/stack | solution.py:446
  20.7 0.0 all-gather.3.cloned.1.call-update
  20.7 4.5 %collective-permute-start = (bf16[4,256,128]{2,1,0:T(8,128)(2,1)}, bf16[4,256,128]{2,1,0:T(8,128)(2,1)S(1)}, u32[]{:S(2)}, u32[]{:S(2)}) collective-permute-start(bf16[4,256,128]{2,1,0:T(8,128)(2,1)} %get-tuple-element.12.own_ref), channel_id=1, source_target_pairs={{0,1},{1,2},{2,3},{3,0},{4,5},{5,6},{6,7},{7,4},{8,9},{9,10},{10,1... | collective-permute-start | bytes 786440 | tf_op jit(solution)/shard_map/ppermute | solution.py:439
  25.2 3.5 %collective-permute-start.1 = (bf16[4,256,128]{2,1,0:T(8,128)(2,1)}, bf16[4,256,128]{2,1,0:T(8,128)(2,1)S(1)}, u32[]{:S(2)}, u32[]{:S(2)}) collective-permute-start(bf16[4,256,128]{2,1,0:T(8,128)(2,1)} %get-tuple-element.12.own_ref), channel_id=1, source_target_pairs={{0,3},{1,0},{2,1},{3,2},{4,7},{5,4},{6,5},{7,6},{8,11},{9,8},{10,9... | collective-permute-start | bytes 786440 | tf_op jit(solution)/shard_map/ppermute | solution.py:439
  28.7 6.8 %collective-permute-start.2 = (bf16[4,256,128]{2,1,0:T(8,128)(2,1)}, bf16[4,256,128]{2,1,0:T(8,128)(2,1)S(1)}, u32[]{:S(2)}, u32[]{:S(2)}) collective-permute-start(bf16[4,256,128]{2,1,0:T(8,128)(2,1)} %get-tuple-element.12.own_ref), channel_id=1, source_target_pairs={{0,2},{1,3},{2,0},{3,1},{4,6},{5,7},{6,4},{7,5},{8,10},{9,11},{10,... | collective-permute-start | bytes 786440 | tf_op jit(solution)/shard_map/ppermute | solution.py:439
  35.5 3.9 %collective-permute-done = bf16[4,256,128]{2,1,0:T(8,128)(2,1)S(1)} collective-permute-done((bf16[4,256,128]{2,1,0:T(8,128)(2,1)}, bf16[4,256,128]{2,1,0:T(8,128)(2,1)S(1)}, u32[]{:S(2)}, u32[]{:S(2)}) %collective-permute-start) | collective-permute-done | bytes 262176 | tf_op jit(solution)/shard_map/ppermute | solution.py:439
  39.4 0.0 collective-permute-done.1
  39.4 15.9 %collective-permute-done.2 = bf16[4,256,128]{2,1,0:T(8,128)(2,1)S(1)} collective-permute-done((bf16[4,256,128]{2,1,0:T(8,128)(2,1)}, bf16[4,256,128]{2,1,0:T(8,128)(2,1)S(1)}, u32[]{:S(2)}, u32[]{:S(2)}) %collective-permute-start.2) | collective-permute-done | bytes 262176 | tf_op jit(solution)/shard_map/ppermute | solution.py:439
  55.3 1.1 pad_maximum_fusion.near_ref
  56.4 3.4 %collective-permute-start.3 = (bf16[4,4,256,128]{3,2,1,0:T(8,128)(2,1)S(1)}, bf16[4,4,256,128]{3,2,1,0:T(8,128)(2,1)S(1)}, u32[]{:S(2)}, u32[]{:S(2)}) collective-permute-start(bf16[4,4,256,128]{3,2,1,0:T(8,128)(2,1)S(1)} %pad_maximum_fusion.near_ref), channel_id=1, source_target_pairs={{0,4},{1,5},{2,6},{3,7},{4,8},{5,9},{6,10},{7,11},{8,12},{9,13},{1... | collective-permute-start | bytes 3145736 | tf_op jit(solution)/shard_map/ppermute | solution.py:439
  59.8 3.7 %collective-permute-start.4 = (bf16[4,4,256,128]{3,2,1,0:T(8,128)(2,1)S(1)}, bf16[4,4,256,128]{3,2,1,0:T(8,128)(2,1)S(1)}, u32[]{:S(2)}, u32[]{:S(2)}) collective-permute-start(bf16[4,4,256,128]{3,2,1,0:T(8,128)(2,1)S(1)} %pad_maximum_fusion.near_ref), channel_id=1, source_target_pairs={{0,12},{1,13},{2,14},{3,15},{4,0},{5,1},{6,2},{7,3},{8,4},{9,5},{1... | collective-permute-start | bytes 3145736 | tf_op jit(solution)/shard_map/ppermute | solution.py:439
  63.5 19.7 %collective-permute-done.3.left_ref = bf16[4,4,256,128]{3,2,1,0:T(8,128)(2,1)S(1)} collective-permute-done((bf16[4,4,256,128]{3,2,1,0:T(8,128)(2,1)S(1)}, bf16[4,4,256,128]{3,2,1,0:T(8,128)(2,1)S(1)}, u32[]{:S(2)}, u32[]{:S(2)}) %collective-permute-start.3) | collective-permute-done | bytes 1048608 | tf_op jit(solution)/shard_map/ppermute | solution.py:439
  83.2 0.9 slice.8
  84.0 2.2 %collective-permute-start.5 = (bf16[2,4,256,128]{3,2,1,0:T(8,128)(2,1)}, bf16[2,4,256,128]{3,2,1,0:T(8,128)(2,1)}, u32[]{:S(2)}, u32[]{:S(2)}) collective-permute-start(bf16[2,4,256,128]{3,2,1,0:T(8,128)(2,1)} %slice.8), channel_id=1, source_target_pairs={{0,4},{1,5},{2,6},{3,7},{4,8},{5,9},{6,10},{7,11},{8,12},{9,13},{1... | collective-permute-start | bytes 1572872 | tf_op jit(solution)/shard_map/ppermute | solution.py:439
  86.2 0.9 slice.9
  87.1 4.9 %collective-permute-start.6 = (bf16[2,4,256,128]{3,2,1,0:T(8,128)(2,1)}, bf16[2,4,256,128]{3,2,1,0:T(8,128)(2,1)}, u32[]{:S(2)}, u32[]{:S(2)}) collective-permute-start(bf16[2,4,256,128]{3,2,1,0:T(8,128)(2,1)} %slice.9), channel_id=1, source_target_pairs={{0,12},{1,13},{2,14},{3,15},{4,0},{5,1},{6,2},{7,3},{8,4},{9,5},{1... | collective-permute-start | bytes 1572872 | tf_op jit(solution)/shard_map/ppermute | solution.py:439
  92.0 0.7 copy.7
  92.8 9.9 %near.1 = (bf16[4,3328,128]{2,1,0:T(8,128)(2,1)}, bf16[4,4,48,3328]{3,2,1,0:T(8,128)(2,1)}, bf16[4,4,128,256]{3,2,1,0:T(8,128)(2,1)}, f32[4,4,32,256]{3,2,1,0:T(8,128)}, f32[4,8,128]{2,1,0:T(8,128)}) custom-call(s32[32]{0:T(128)} %valid_ref.5, bf16[4,256,128]{2,1,0:T(8,128)(2,1)} %get-tuple-element.12.own_ref, bf16[4,4,256,128]{3,2,1,0:T(8,128)(2,1)} %copy-done, ...), custom_call_target="tpu_custom_call" | custom-call | tf_op jit(solution)/shard_map/near/pallas_call | solution.py:183
  102.7 0.0 collective-permute-done.5.low_ref
  102.7 0.0 all-gather.3.cloned.1.call-done
  102.7 28.8 %attend.1 = bf16[4,256,128]{2,1,0:T(8,128)(2,1)} custom-call(s32[32]{0:T(128)} %valid_ref.5, bf16[4,3328,128]{2,1,0:T(8,128)(2,1)} %get-tuple-element.13.keys_hbm, bf16[4,4,48,3328]{3,2,1,0:T(8,128)(2,1)} %get-tuple-element.14.values_hbm, bf16[2,4,256,128]{3,2,1,0:T(8,128)(2,1)} %collective-permute-done.5.low_ref, ...), custom_call_target="tpu_custom_call" | custom-call | tf_op jit(solution)/shard_map/attend/pallas_call | solution.py:387
  (11 shorter events, 0.0 us)
Async XLA Ops:
  6.5 85.5 %copy-start.3 = (bf16[128,512]{1,0:T(8,128)(2,1)S(1)}, bf16[128,512]{1,0:T(8,128)(2,1)}, u32[]{:S(2)}) copy-start(bf16[128,512]{1,0:T(8,128)(2,1)} %weight_ref.3) | copy-start | bytes 393220
  6.5 96.2 %all-gather.3.cloned.1.call-start = ((), (), s32[]{:S(2)}) async-start(), calls=%async_computation | async-start | bytes 8912896 | tf_op jit(solution)/shard_map/all_gather | solution.py:448
  8.8 10.1 %collective-permute-start.7 = (bf16[4,128,256]{2,1,0:T(8,128)(2,1)}, bf16[4,128,256]{2,1,0:T(8,128)(2,1)S(1)}, u32[]{:S(2)}, u32[]{:S(2)}) collective-permute-start(bf16[4,128,256]{2,1,0:T(8,128)(2,1)} %get-tuple-element.18), channel_id=1, source_target_pairs={{0,256},{16,272},{32,288},{48,304},{64,320},{80,336},{96,352},{112... | collective-permute-start | bytes 786440 | tf_op jit(solution)/shard_map/ppermute | solution.py:445
  20.7 18.7 %collective-permute-start = (bf16[4,256,128]{2,1,0:T(8,128)(2,1)}, bf16[4,256,128]{2,1,0:T(8,128)(2,1)S(1)}, u32[]{:S(2)}, u32[]{:S(2)}) collective-permute-start(bf16[4,256,128]{2,1,0:T(8,128)(2,1)} %get-tuple-element.12.own_ref), channel_id=1, source_target_pairs={{0,1},{1,2},{2,3},{3,0},{4,5},{5,6},{6,7},{7,4},{8,9},{9,10},{10,1... | collective-permute-start | bytes 786440 | tf_op jit(solution)/shard_map/ppermute | solution.py:439
  25.2 14.2 %collective-permute-start.1 = (bf16[4,256,128]{2,1,0:T(8,128)(2,1)}, bf16[4,256,128]{2,1,0:T(8,128)(2,1)S(1)}, u32[]{:S(2)}, u32[]{:S(2)}) collective-permute-start(bf16[4,256,128]{2,1,0:T(8,128)(2,1)} %get-tuple-element.12.own_ref), channel_id=1, source_target_pairs={{0,3},{1,0},{2,1},{3,2},{4,7},{5,4},{6,5},{7,6},{8,11},{9,8},{10,9... | collective-permute-start | bytes 786440 | tf_op jit(solution)/shard_map/ppermute | solution.py:439
  28.7 26.6 %collective-permute-start.2 = (bf16[4,256,128]{2,1,0:T(8,128)(2,1)}, bf16[4,256,128]{2,1,0:T(8,128)(2,1)S(1)}, u32[]{:S(2)}, u32[]{:S(2)}) collective-permute-start(bf16[4,256,128]{2,1,0:T(8,128)(2,1)} %get-tuple-element.12.own_ref), channel_id=1, source_target_pairs={{0,2},{1,3},{2,0},{3,1},{4,6},{5,7},{6,4},{7,5},{8,10},{9,11},{10,... | collective-permute-start | bytes 786440 | tf_op jit(solution)/shard_map/ppermute | solution.py:439
  56.4 36.3 %copy-start = (bf16[4,4,256,128]{3,2,1,0:T(8,128)(2,1)}, bf16[4,4,256,128]{3,2,1,0:T(8,128)(2,1)S(1)}, u32[]{:S(2)}) copy-start(bf16[4,4,256,128]{3,2,1,0:T(8,128)(2,1)S(1)} %pad_maximum_fusion.near_ref) | copy-start | bytes 3145732
  56.4 26.7 %collective-permute-start.3 = (bf16[4,4,256,128]{3,2,1,0:T(8,128)(2,1)S(1)}, bf16[4,4,256,128]{3,2,1,0:T(8,128)(2,1)S(1)}, u32[]{:S(2)}, u32[]{:S(2)}) collective-permute-start(bf16[4,4,256,128]{3,2,1,0:T(8,128)(2,1)S(1)} %pad_maximum_fusion.near_ref), channel_id=1, source_target_pairs={{0,4},{1,5},{2,6},{3,7},{4,8},{5,9},{6,10},{7,11},{8,12},{9,13},{1... | collective-permute-start | bytes 3145736 | tf_op jit(solution)/shard_map/ppermute | solution.py:439
  59.8 26.4 %collective-permute-start.4 = (bf16[4,4,256,128]{3,2,1,0:T(8,128)(2,1)S(1)}, bf16[4,4,256,128]{3,2,1,0:T(8,128)(2,1)S(1)}, u32[]{:S(2)}, u32[]{:S(2)}) collective-permute-start(bf16[4,4,256,128]{3,2,1,0:T(8,128)(2,1)S(1)} %pad_maximum_fusion.near_ref), channel_id=1, source_target_pairs={{0,12},{1,13},{2,14},{3,15},{4,0},{5,1},{6,2},{7,3},{8,4},{9,5},{1... | collective-permute-start | bytes 3145736 | tf_op jit(solution)/shard_map/ppermute | solution.py:439
  83.2 9.6 %copy-start.1 = (bf16[4,4,256,128]{3,2,1,0:T(8,128)(2,1)}, bf16[4,4,256,128]{3,2,1,0:T(8,128)(2,1)S(1)}, u32[]{:S(2)}) copy-start(bf16[4,4,256,128]{3,2,1,0:T(8,128)(2,1)S(1)} %collective-permute-done.3.left_ref) | copy-start | bytes 3145732
  84.0 18.7 %collective-permute-start.5 = (bf16[2,4,256,128]{3,2,1,0:T(8,128)(2,1)}, bf16[2,4,256,128]{3,2,1,0:T(8,128)(2,1)}, u32[]{:S(2)}, u32[]{:S(2)}) collective-permute-start(bf16[2,4,256,128]{3,2,1,0:T(8,128)(2,1)} %slice.8), channel_id=1, source_target_pairs={{0,4},{1,5},{2,6},{3,7},{4,8},{5,9},{6,10},{7,11},{8,12},{9,13},{1... | collective-permute-start | bytes 1572872 | tf_op jit(solution)/shard_map/ppermute | solution.py:439
  86.2 6.5 %copy-start.2 = (bf16[4,4,256,128]{3,2,1,0:T(8,128)(2,1)}, bf16[4,4,256,128]{3,2,1,0:T(8,128)(2,1)S(1)}, u32[]{:S(2)}) copy-start(bf16[4,4,256,128]{3,2,1,0:T(8,128)(2,1)S(1)} %collective-permute-done.4.right_ref) | copy-start | bytes 3145732
  87.1 15.6 %collective-permute-start.6 = (bf16[2,4,256,128]{3,2,1,0:T(8,128)(2,1)}, bf16[2,4,256,128]{3,2,1,0:T(8,128)(2,1)}, u32[]{:S(2)}, u32[]{:S(2)}) collective-permute-start(bf16[2,4,256,128]{3,2,1,0:T(8,128)(2,1)} %slice.9), channel_id=1, source_target_pairs={{0,12},{1,13},{2,14},{3,15},{4,0},{5,1},{6,2},{7,3},{8,4},{9,5},{1... | collective-permute-start | bytes 1572872 | tf_op jit(solution)/shard_map/ppermute | solution.py:439
Sparse Core Ops, SparseCore 0:
  20.8 60.1 all-gather.2

commit v3 on v2

--- a/solution.py
+++ b/solution.py
@@ -12,7 +12,6 @@
 MASKED = -1000000000.0
 LOG2E = 1.4426950408889634
 REACH = 60.0
-PAIR = 4
 XS, YS = 4, 4
 PER_COL = 2
 NEAR = 12 * PER_COL
@@ -116,8 +115,10 @@
 def near_kernel(
     valid_ref,
     own_ref,
-    near_ref,
+    others_ref,
+    left_own_ref,
     left_ref,
+    right_own_ref,
     right_ref,
     weight_ref,
     weight_t_ref,
@@ -132,7 +133,7 @@
     heads = queries_ref.shape[0]
     inner = queries_ref.shape[2]
     head_size = inner // heads
-    own = own_ref[0]
+    own = own_ref[0, 0]
     turned = lax.dot_general(weight_t_ref[0:inner, :], own, NT, preferred_element_type=jnp.float32)
     turned = (turned * head_size ** (-0.5)).astype(jnp.bfloat16)
     gate = jax.nn.sigmoid(
@@ -151,7 +152,8 @@
     def _():
         chart(valid_ref, table, places)
 
-    pack(table, places, (near_ref, left_ref, right_ref), 0, packed)
+    refs = (own_ref, others_ref, left_own_ref, left_ref, right_own_ref, right_ref)
+    pack(table, places, refs, 0, packed)
     blocks = (table[2, 0] + (BLOCK - 1)) >> 8
     peaks_ref[0] = project(
         packed,
@@ -175,8 +177,8 @@
     return pl.BlockSpec(array.shape, lambda i: zeros, pipeline_mode=pl.Buffered(1))
 
 
-def project_near(chain_valid, normed, pieces, weight, weight_t, heads):
-    rows, cols, width = normed.shape
+def project_near(chain_valid, pieces, weight, weight_t, heads):
+    _, rows, cols, width = pieces[0].shape
     inner = weight.shape[1] // 4
     head_size = inner // heads
     depth = head_size + GROUP
@@ -185,7 +187,6 @@
         grid=(rows,),
         in_specs=[
             SMEM,
-            pl.BlockSpec((1, cols, width), lambda i: (i, 0, 0)),
             *(piece_spec(piece) for piece in pieces),
             fixed(weight),
             fixed(weight_t),
@@ -209,7 +210,7 @@
             pltpu.SMEM((3, NEAR + FAR), jnp.int32),
         ],
         name="near",
-    )(chain_valid, normed, *pieces, weight, weight_t)
+    )(chain_valid, *pieces, weight, weight_t)
 
 
 def attend_kernel(
@@ -315,25 +316,33 @@
 
     @pl.when(safe[0] == 1)
     def _():
-        def step(block, carry):
-            place = place_of(block)
-            shifted[...] = (bias[place, :].astype(jnp.float32) - top) * LOG2E
-            for pair in range(0, rows, PAIR):
-                members = range(pair, pair + PAIR)
+        def span(first, count):
+            parts = [place_of(first + n) for n in range(count)]
+            for n, place in enumerate(parts):
+                shifted[n] = (bias[place, :].astype(jnp.float32) - top) * LOG2E
+            weights = []
+            for n, place in enumerate(parts):
                 scores = [
-                    jnp.dot(keys[row, place, :], queries[head, row], preferred_element_type=jnp.float32)
-                    for row in members
+                    jnp.dot(keys[row, place, :], queries[head, row], preferred_element_type=jnp.float32) for row in range(rows)
                 ]
-                weights = [
-                    jnp.exp2(part * LOG2E + shifted[...]).astype(jnp.bfloat16) for part in scores
-                ]
-                for row, part in zip(members, weights):
+                weights.append(
+                    [jnp.exp2(part * LOG2E + shifted[n]).astype(jnp.bfloat16) for part in scores]
+                )
+            for n, place in enumerate(parts):
+                for row in range(rows):
                     sums[row] += jnp.dot(
-                        values[row, head, :, place], part, preferred_element_type=jnp.float32
+                        values[row, head, :, place], weights[n][row], preferred_element_type=jnp.float32
                     )
+
+        def double(pair, carry):
+            span(2 * pair, 2)
             return carry
 
-        lax.fori_loop(0, blocks, step, 0)
+        lax.fori_loop(0, blocks >> 1, double, 0)
+
+        @pl.when((blocks & 1) == 1)
+        def _():
+            span(blocks - 1, 1)
 
     @pl.when(safe[0] == 0)
     def _():
@@ -407,7 +416,7 @@
             pltpu.VMEM((FAR_ROOM, weight.shape[0]), jnp.bfloat16),
             pltpu.VMEM((rows, inner, cols), jnp.bfloat16),
             pltpu.VMEM((ROOM, cols), jnp.bfloat16),
-            pltpu.VMEM((BLOCK, cols), jnp.float32),
+            pltpu.VMEM((2, BLOCK, cols), jnp.float32),
             pltpu.VMEM((rows, depth, cols), jnp.float32),
             pltpu.SMEM((3, NEAR + FAR), jnp.int32),
             pltpu.SMEM((1,), jnp.int32),
@@ -448,10 +457,10 @@
     return lax.all_gather(both, "rows", axis_index_groups=groups)
 
 
-def finish(chain_valid, normed, near, far, bias, project_weight, output_weight, heads):
+def finish(chain_valid, near, far, bias, project_weight, output_weight, heads):
     weight_t = project_weight.T
     keys, values, queries, gates, peaks = project_near(
-        chain_valid, normed, near, project_weight, weight_t, heads
+        chain_valid, near, project_weight, weight_t, heads
     )
     return attend(
         chain_valid,
@@ -471,18 +480,20 @@
 def local(pair_rep, project_weight, output_weight, pair_bias, chain_valid):
     normed, bias_t = prep(pair_rep, pair_bias, chain_valid)
     bias = gather_bias(bias_t)
+    left_own = shift(normed, 1, 0)
+    right_own = shift(normed, -1, 0)
     above = shift(normed, 0, 1)
     below = shift(normed, 0, -1)
     across = shift(normed, 0, 2)
-    near = jnp.stack([normed, above, below, across])
-    left = shift(near, 1, 0)
-    right = shift(near, -1, 0)
-    far_low = shift(left[:2], 1, 0)
-    far_high = shift(right[2:], -1, 0)
+    others = jnp.stack([above, below, across])
+    left = shift(others, 1, 0)
+    right = shift(others, -1, 0)
+    far_low = shift(jnp.stack([left_own, left[0]]), 1, 0)
+    far_high = shift(right[1:], -1, 0)
+    near = (normed[None], others, left_own[None], left, right_own[None], right)
     return finish(
         chain_valid,
-        normed,
-        (near, left, right),
+        near,
         (far_low, far_high),
         bias,
         project_weight,

time: 139 us -> 149 us (1.072)
  the two profiles are of different devices: /device:TPU:136 before, /device:TPU:206 now
where the time goes in v3:
time: 149 us; the launch traced here: 148 us
  waiting for transfers between devices  58.3 us (39%)
  Pallas kernels  35.9 us (24%)
  starting transfers between devices  35.3 us (24%)
  between operations  13.6 us (9%)
  other arithmetic  2.79 us (2%)
  local copies, waits for them, and re-layouts  2.48 us (2%)
    ppermute x9, waiting for transfers between devices, shift(): return lax.ppermute(value, 'cols', pairs)  50.5 us
    ppermute x9, starting transfers between devices, shift(): return lax.ppermute(value, 'cols', pairs)  32.8 us
    pallas_call x1, Pallas kernels, attend(): pl.pallas_call(attend_kernel, grid=(heads,), in_specs=[SMEM, pl.BlockSpec...  23.5 us
    pallas_call x1, Pallas kernels, project_near(): pl.pallas_call(near_kernel, grid=(rows,), in_specs=[SMEM, *(piece_spec(pi...  10.2 us
    ppermute x1, waiting for transfers between devices, gather_bias(): lax.ppermute(bias_t, 'rows', [(r, (r + half) % count) for r in range(coun...  7.78 us
  transfers between devices with their start and end apart: 11, of which 6 were waited for; matrix products, arithmetic and copies ran while one was open for 2% of the time, Pallas kernels for 7%

profile of v3, /device:TPU:206, one launch (start us, length us, event | category | flops | bytes accessed | tf_op | source)
XLA Modules:
  0.0 148.3 jit_solution(2088191097806361859)
XLA Ops:
  6.5 2.2 %prep.1 = (bf16[4,256,128]{2,1,0:T(8,128)(2,1)}, bf16[4,128,256]{2,1,0:T(8,128)(2,1)}) custom-call(s32[32]{0:T(128)} %valid_ref.5, bf16[4,256,128]{2,1,0:T(8,128)(2,1)} %pair_ref.1, bf16[4,256,128]{2,1,0:T(8,128)(2,1)} %bias_ref.1), custom_call_target="tpu_custom_call" | custom-call | tf_op jit(solution)/shard_map/prep/pallas_call | solution.py:45
  8.8 2.5 %collective-permute-start.9 = (bf16[4,128,256]{2,1,0:T(8,128)(2,1)}, bf16[4,128,256]{2,1,0:T(8,128)(2,1)S(1)}, u32[]{:S(2)}, u32[]{:S(2)}) collective-permute-start(bf16[4,128,256]{2,1,0:T(8,128)(2,1)} %get-tuple-element.18), channel_id=1, source_target_pairs={{0,256},{16,272},{32,288},{48,304},{64,320},{80,336},{96,352},{112... | collective-permute-start | bytes 786440 | tf_op jit(solution)/shard_map/ppermute | solution.py:454
  11.2 7.8 %collective-permute-done.9 = bf16[4,128,256]{2,1,0:T(8,128)(2,1)S(1)} collective-permute-done((bf16[4,128,256]{2,1,0:T(8,128)(2,1)}, bf16[4,128,256]{2,1,0:T(8,128)(2,1)S(1)}, u32[]{:S(2)}, u32[]{:S(2)}) %collective-permute-start.9) | collective-permute-done | bytes 262176 | tf_op jit(solution)/shard_map/ppermute | solution.py:454
  19.0 1.8 %pad_maximum_fusion.2 = bf16[2,4,128,256]{3,2,1,0:T(8,128)(2,1)} fusion(bf16[1,4,128,256]{3,2,1,0:T(8,128)(2,1)S(1)} %bitcast.20, bf16[1,4,128,256]{3,2,1,0:T(8,128)(2,1)} %bitcast.19), kind=kLoop, calls=%fused_computation.2 | loop fusion | flops 262144 | bytes 1048576 | tf_op jit(solution)/shard_map/stack | solution.py:455
  20.8 4.5 %collective-permute-start = (bf16[4,256,128]{2,1,0:T(8,128)(2,1)}, bf16[4,256,128]{2,1,0:T(8,128)(2,1)S(1)}, u32[]{:S(2)}, u32[]{:S(2)}) collective-permute-start(bf16[4,256,128]{2,1,0:T(8,128)(2,1)} %get-tuple-element.12), channel_id=1, source_target_pairs={{0,1},{1,2},{2,3},{3,0},{4,5},{5,6},{6,7},{7,4},{8,9},{9,10},{10,1... | collective-permute-start | bytes 786440 | tf_op jit(solution)/shard_map/ppermute | solution.py:448
  25.3 3.5 %collective-permute-start.1 = (bf16[4,256,128]{2,1,0:T(8,128)(2,1)}, bf16[4,256,128]{2,1,0:T(8,128)(2,1)S(1)}, u32[]{:S(2)}, u32[]{:S(2)}) collective-permute-start(bf16[4,256,128]{2,1,0:T(8,128)(2,1)} %get-tuple-element.12), channel_id=1, source_target_pairs={{0,3},{1,0},{2,1},{3,2},{4,7},{5,4},{6,5},{7,6},{8,11},{9,8},{10,9... | collective-permute-start | bytes 786440 | tf_op jit(solution)/shard_map/ppermute | solution.py:448
  28.8 6.8 %collective-permute-start.2 = (bf16[4,256,128]{2,1,0:T(8,128)(2,1)}, bf16[4,256,128]{2,1,0:T(8,128)(2,1)S(1)}, u32[]{:S(2)}, u32[]{:S(2)}) collective-permute-start(bf16[4,256,128]{2,1,0:T(8,128)(2,1)} %get-tuple-element.12), channel_id=1, source_target_pairs={{0,2},{1,3},{2,0},{3,1},{4,6},{5,7},{6,4},{7,5},{8,10},{9,11},{10,... | collective-permute-start | bytes 786440 | tf_op jit(solution)/shard_map/ppermute | solution.py:448
  35.6 3.9 %collective-permute-done = bf16[4,256,128]{2,1,0:T(8,128)(2,1)S(1)} collective-permute-done((bf16[4,256,128]{2,1,0:T(8,128)(2,1)}, bf16[4,256,128]{2,1,0:T(8,128)(2,1)S(1)}, u32[]{:S(2)}, u32[]{:S(2)}) %collective-permute-start) | collective-permute-done | bytes 262176 | tf_op jit(solution)/shard_map/ppermute | solution.py:448
  39.5 15.9 %collective-permute-done.2 = bf16[4,256,128]{2,1,0:T(8,128)(2,1)S(1)} collective-permute-done((bf16[4,256,128]{2,1,0:T(8,128)(2,1)}, bf16[4,256,128]{2,1,0:T(8,128)(2,1)S(1)}, u32[]{:S(2)}, u32[]{:S(2)}) %collective-permute-start.2) | collective-permute-done | bytes 262176 | tf_op jit(solution)/shard_map/ppermute | solution.py:448
  55.5 2.4 %collective-permute-start.4 = (bf16[3,4,256,128]{3,2,1,0:T(8,128)(2,1)S(1)}, bf16[3,4,256,128]{3,2,1,0:T(8,128)(2,1)S(1)}, u32[]{:S(2)}, u32[]{:S(2)}) collective-permute-start(bf16[3,4,256,128]{3,2,1,0:T(8,128)(2,1)S(1)} %pad_maximum_fusion.others_ref), channel_id=1, source_target_pairs={{0,4},{1,5},{2,6},{3,7},{4,8},{5,9},{6,10},{7,11},{8,12},{9,13},{1... | collective-permute-start | bytes 2359304 | tf_op jit(solution)/shard_map/ppermute | solution.py:448
  57.9 3.5 %collective-permute-start.6 = (bf16[3,4,256,128]{3,2,1,0:T(8,128)(2,1)S(1)}, bf16[3,4,256,128]{3,2,1,0:T(8,128)(2,1)S(1)}, u32[]{:S(2)}, u32[]{:S(2)}) collective-permute-start(bf16[3,4,256,128]{3,2,1,0:T(8,128)(2,1)S(1)} %pad_maximum_fusion.others_ref), channel_id=1, source_target_pairs={{0,12},{1,13},{2,14},{3,15},{4,0},{5,1},{6,2},{7,3},{8,4},{9,5},{1... | collective-permute-start | bytes 2359304 | tf_op jit(solution)/shard_map/ppermute | solution.py:448
  61.4 3.6 %collective-permute-start.3 = (bf16[4,256,128]{2,1,0:T(8,128)(2,1)}, bf16[4,256,128]{2,1,0:T(8,128)(2,1)S(1)}, u32[]{:S(2)}, u32[]{:S(2)}) collective-permute-start(bf16[4,256,128]{2,1,0:T(8,128)(2,1)} %get-tuple-element.12), channel_id=1, source_target_pairs={{0,4},{1,5},{2,6},{3,7},{4,8},{5,9},{6,10},{7,11},{8,12},{9,13},{1... | collective-permute-start | bytes 786440 | tf_op jit(solution)/shard_map/ppermute | solution.py:448
  65.0 12.8 %collective-permute-done.4.left_ref = bf16[3,4,256,128]{3,2,1,0:T(8,128)(2,1)S(1)} collective-permute-done((bf16[3,4,256,128]{3,2,1,0:T(8,128)(2,1)S(1)}, bf16[3,4,256,128]{3,2,1,0:T(8,128)(2,1)S(1)}, u32[]{:S(2)}, u32[]{:S(2)}) %collective-permute-start.4) | collective-permute-done | bytes 786464 | tf_op jit(solution)/shard_map/ppermute | solution.py:448
  77.9 3.2 %collective-permute-done.3 = bf16[4,256,128]{2,1,0:T(8,128)(2,1)S(1)} collective-permute-done((bf16[4,256,128]{2,1,0:T(8,128)(2,1)}, bf16[4,256,128]{2,1,0:T(8,128)(2,1)S(1)}, u32[]{:S(2)}, u32[]{:S(2)}) %collective-permute-start.3) | collective-permute-done | bytes 262176 | tf_op jit(solution)/shard_map/ppermute | solution.py:448
  81.1 0.9 pad_maximum_fusion.1
  82.0 3.6 %collective-permute-start.7 = (bf16[2,4,256,128]{3,2,1,0:T(8,128)(2,1)}, bf16[2,4,256,128]{3,2,1,0:T(8,128)(2,1)S(1)}, u32[]{:S(2)}, u32[]{:S(2)}) collective-permute-start(bf16[2,4,256,128]{3,2,1,0:T(8,128)(2,1)} %pad_maximum_fusion.1), channel_id=1, source_target_pairs={{0,4},{1,5},{2,6},{3,7},{4,8},{5,9},{6,10},{7,11},{8,12},{9,13},{1... | collective-permute-start | bytes 1572872 | tf_op jit(solution)/shard_map/ppermute | solution.py:448
  85.6 0.9 slice.9
  86.5 2.2 %collective-permute-start.8 = (bf16[2,4,256,128]{3,2,1,0:T(8,128)(2,1)}, bf16[2,4,256,128]{3,2,1,0:T(8,128)(2,1)}, u32[]{:S(2)}, u32[]{:S(2)}) collective-permute-start(bf16[2,4,256,128]{3,2,1,0:T(8,128)(2,1)} %slice.9), channel_id=1, source_target_pairs={{0,12},{1,13},{2,14},{3,15},{4,0},{5,1},{6,2},{7,3},{8,4},{9,5},{1... | collective-permute-start | bytes 1572872 | tf_op jit(solution)/shard_map/ppermute | solution.py:448
  88.8 2.7 %collective-permute-start.5 = (bf16[4,256,128]{2,1,0:T(8,128)(2,1)S(1)}, bf16[4,256,128]{2,1,0:T(8,128)(2,1)}, u32[]{:S(2)}, u32[]{:S(2)}) collective-permute-start(bf16[4,256,128]{2,1,0:T(8,128)(2,1)S(1)} %copy-done.6), channel_id=1, source_target_pairs={{0,12},{1,13},{2,14},{3,15},{4,0},{5,1},{6,2},{7,3},{8,4},{9,5},{1... | collective-permute-start | bytes 786440 | tf_op jit(solution)/shard_map/ppermute | solution.py:448
  91.5 0.7 copy.7
  92.3 14.6 %collective-permute-done.5 = bf16[4,256,128]{2,1,0:T(8,128)(2,1)} collective-permute-done((bf16[4,256,128]{2,1,0:T(8,128)(2,1)S(1)}, bf16[4,256,128]{2,1,0:T(8,128)(2,1)}, u32[]{:S(2)}, u32[]{:S(2)}) %collective-permute-start.5) | collective-permute-done | bytes 262176 | tf_op jit(solution)/shard_map/ppermute | solution.py:448
  106.9 10.2 %near.1 = (bf16[4,3328,128]{2,1,0:T(8,128)(2,1)}, bf16[4,4,48,3328]{3,2,1,0:T(8,128)(2,1)}, bf16[4,4,128,256]{3,2,1,0:T(8,128)(2,1)}, f32[4,4,32,256]{3,2,1,0:T(8,128)}, f32[4,8,128]{2,1,0:T(8,128)}) custom-call(s32[32]{0:T(128)} %valid_ref.5, bf16[1,4,256,128]{3,2,1,0:T(8,128)(2,1)} %bitcast.15, bf16[3,4,256,128]{3,2,1,0:T(8,128)(2,1)} %copy-done, ...), custom_call_target="tpu_custom_call" | custom-call | tf_op jit(solution)/shard_map/near/pallas_call | solution.py:185
  117.2 0.8 copy-done.5
  118.0 23.5 %attend.1 = bf16[4,256,128]{2,1,0:T(8,128)(2,1)} custom-call(s32[32]{0:T(128)} %valid_ref.5, bf16[4,3328,128]{2,1,0:T(8,128)(2,1)} %get-tuple-element.13.keys_hbm, bf16[4,4,48,3328]{3,2,1,0:T(8,128)(2,1)} %get-tuple-element.14.values_hbm, bf16[2,4,256,128]{3,2,1,0:T(8,128)(2,1)} %copy-done.5, bf16[2,4,256,128]{3,2,1,0:T(8,128)(2,1)} %collective-permute-done.8.high_ref, ...), custom_call_target="tpu_custom_call" | custom-call | tf_op jit(solution)/shard_map/attend/pallas_call | solution.py:396
  (22 shorter events, 0.2 us)
Async XLA Ops:
  6.5 85.0 %copy-start.3 = (bf16[128,512]{1,0:T(8,128)(2,1)S(1)}, bf16[128,512]{1,0:T(8,128)(2,1)}, u32[]{:S(2)}) copy-start(bf16[128,512]{1,0:T(8,128)(2,1)} %weight_ref.3) | copy-start | bytes 393220
  6.5 110.6 %all-gather.3.cloned.1.call-start = ((), (), s32[]{:S(2)}) async-start(), calls=%async_computation | async-start | bytes 8912896 | tf_op jit(solution)/shard_map/all_gather | solution.py:457
  8.8 80.0 %copy-start.6 = (bf16[4,256,128]{2,1,0:T(8,128)(2,1)S(1)}, bf16[4,256,128]{2,1,0:T(8,128)(2,1)}, u32[]{:S(2)}) copy-start(bf16[4,256,128]{2,1,0:T(8,128)(2,1)} %get-tuple-element.12) | copy-start | bytes 786436
  8.8 10.3 %collective-permute-start.9 = (bf16[4,128,256]{2,1,0:T(8,128)(2,1)}, bf16[4,128,256]{2,1,0:T(8,128)(2,1)S(1)}, u32[]{:S(2)}, u32[]{:S(2)}) collective-permute-start(bf16[4,128,256]{2,1,0:T(8,128)(2,1)} %get-tuple-element.18), channel_id=1, source_target_pairs={{0,256},{16,272},{32,288},{48,304},{64,320},{80,336},{96,352},{112... | collective-permute-start | bytes 786440 | tf_op jit(solution)/shard_map/ppermute | solution.py:454
  20.8 18.7 %collective-permute-start = (bf16[4,256,128]{2,1,0:T(8,128)(2,1)}, bf16[4,256,128]{2,1,0:T(8,128)(2,1)S(1)}, u32[]{:S(2)}, u32[]{:S(2)}) collective-permute-start(bf16[4,256,128]{2,1,0:T(8,128)(2,1)} %get-tuple-element.12), channel_id=1, source_target_pairs={{0,1},{1,2},{2,3},{3,0},{4,5},{5,6},{6,7},{7,4},{8,9},{9,10},{10,1... | collective-permute-start | bytes 786440 | tf_op jit(solution)/shard_map/ppermute | solution.py:448
  25.3 14.2 %collective-permute-start.1 = (bf16[4,256,128]{2,1,0:T(8,128)(2,1)}, bf16[4,256,128]{2,1,0:T(8,128)(2,1)S(1)}, u32[]{:S(2)}, u32[]{:S(2)}) collective-permute-start(bf16[4,256,128]{2,1,0:T(8,128)(2,1)} %get-tuple-element.12), channel_id=1, source_target_pairs={{0,3},{1,0},{2,1},{3,2},{4,7},{5,4},{6,5},{7,6},{8,11},{9,8},{10,9... | collective-permute-start | bytes 786440 | tf_op jit(solution)/shard_map/ppermute | solution.py:448
  28.8 26.6 %collective-permute-start.2 = (bf16[4,256,128]{2,1,0:T(8,128)(2,1)}, bf16[4,256,128]{2,1,0:T(8,128)(2,1)S(1)}, u32[]{:S(2)}, u32[]{:S(2)}) collective-permute-start(bf16[4,256,128]{2,1,0:T(8,128)(2,1)} %get-tuple-element.12), channel_id=1, source_target_pairs={{0,2},{1,3},{2,0},{3,1},{4,6},{5,7},{6,4},{7,5},{8,10},{9,11},{10,... | collective-permute-start | bytes 786440 | tf_op jit(solution)/shard_map/ppermute | solution.py:448
  55.5 51.4 %copy-start = (bf16[3,4,256,128]{3,2,1,0:T(8,128)(2,1)}, bf16[3,4,256,128]{3,2,1,0:T(8,128)(2,1)S(1)}, u32[]{:S(2)}) copy-start(bf16[3,4,256,128]{3,2,1,0:T(8,128)(2,1)S(1)} %pad_maximum_fusion.others_ref) | copy-start | bytes 2359300
  55.5 22.3 %collective-permute-start.4 = (bf16[3,4,256,128]{3,2,1,0:T(8,128)(2,1)S(1)}, bf16[3,4,256,128]{3,2,1,0:T(8,128)(2,1)S(1)}, u32[]{:S(2)}, u32[]{:S(2)}) collective-permute-start(bf16[3,4,256,128]{3,2,1,0:T(8,128)(2,1)S(1)} %pad_maximum_fusion.others_ref), channel_id=1, source_target_pairs={{0,4},{1,5},{2,6},{3,7},{4,8},{5,9},{6,10},{7,11},{8,12},{9,13},{1... | collective-permute-start | bytes 2359304 | tf_op jit(solution)/shard_map/ppermute | solution.py:448
  57.9 27.6 %collective-permute-start.6 = (bf16[3,4,256,128]{3,2,1,0:T(8,128)(2,1)S(1)}, bf16[3,4,256,128]{3,2,1,0:T(8,128)(2,1)S(1)}, u32[]{:S(2)}, u32[]{:S(2)}) collective-permute-start(bf16[3,4,256,128]{3,2,1,0:T(8,128)(2,1)S(1)} %pad_maximum_fusion.others_ref), channel_id=1, source_target_pairs={{0,12},{1,13},{2,14},{3,15},{4,0},{5,1},{6,2},{7,3},{8,4},{9,5},{1... | collective-permute-start | bytes 2359304 | tf_op jit(solution)/shard_map/ppermute | solution.py:448
  61.4 19.7 %collective-permute-start.3 = (bf16[4,256,128]{2,1,0:T(8,128)(2,1)}, bf16[4,256,128]{2,1,0:T(8,128)(2,1)S(1)}, u32[]{:S(2)}, u32[]{:S(2)}) collective-permute-start(bf16[4,256,128]{2,1,0:T(8,128)(2,1)} %get-tuple-element.12), channel_id=1, source_target_pairs={{0,4},{1,5},{2,6},{3,7},{4,8},{5,9},{6,10},{7,11},{8,12},{9,13},{1... | collective-permute-start | bytes 786440 | tf_op jit(solution)/shard_map/ppermute | solution.py:448
  77.9 29.0 %copy-start.2 = (bf16[3,4,256,128]{3,2,1,0:T(8,128)(2,1)}, bf16[3,4,256,128]{3,2,1,0:T(8,128)(2,1)S(1)}, u32[]{:S(2)}) copy-start(bf16[3,4,256,128]{3,2,1,0:T(8,128)(2,1)S(1)} %collective-permute-done.4.left_ref) | copy-start | bytes 2359300
  81.1 25.8 %copy-start.4 = (bf16[4,256,128]{2,1,0:T(8,128)(2,1)}, bf16[4,256,128]{2,1,0:T(8,128)(2,1)S(1)}, u32[]{:S(2)}) copy-start(bf16[4,256,128]{2,1,0:T(8,128)(2,1)S(1)} %collective-permute-done.3) | copy-start | bytes 786436
  82.0 35.1 %collective-permute-start.7 = (bf16[2,4,256,128]{3,2,1,0:T(8,128)(2,1)}, bf16[2,4,256,128]{3,2,1,0:T(8,128)(2,1)S(1)}, u32[]{:S(2)}, u32[]{:S(2)}) collective-permute-start(bf16[2,4,256,128]{3,2,1,0:T(8,128)(2,1)} %pad_maximum_fusion.1), channel_id=1, source_target_pairs={{0,4},{1,5},{2,6},{3,7},{4,8},{5,9},{6,10},{7,11},{8,12},{9,13},{1... | collective-permute-start | bytes 1572872 | tf_op jit(solution)/shard_map/ppermute | solution.py:448
  85.6 21.3 %copy-start.1 = (bf16[3,4,256,128]{3,2,1,0:T(8,128)(2,1)}, bf16[3,4,256,128]{3,2,1,0:T(8,128)(2,1)S(1)}, u32[]{:S(2)}) copy-start(bf16[3,4,256,128]{3,2,1,0:T(8,128)(2,1)S(1)} %collective-permute-done.6.right_ref) | copy-start | bytes 2359300
  86.5 30.6 %collective-permute-start.8 = (bf16[2,4,256,128]{3,2,1,0:T(8,128)(2,1)}, bf16[2,4,256,128]{3,2,1,0:T(8,128)(2,1)}, u32[]{:S(2)}, u32[]{:S(2)}) collective-permute-start(bf16[2,4,256,128]{3,2,1,0:T(8,128)(2,1)} %slice.9), channel_id=1, source_target_pairs={{0,12},{1,13},{2,14},{3,15},{4,0},{5,1},{6,2},{7,3},{8,4},{9,5},{1... | collective-permute-start | bytes 1572872 | tf_op jit(solution)/shard_map/ppermute | solution.py:448
  88.8 18.1 %collective-permute-start.5 = (bf16[4,256,128]{2,1,0:T(8,128)(2,1)S(1)}, bf16[4,256,128]{2,1,0:T(8,128)(2,1)}, u32[]{:S(2)}, u32[]{:S(2)}) collective-permute-start(bf16[4,256,128]{2,1,0:T(8,128)(2,1)S(1)} %copy-done.6), channel_id=1, source_target_pairs={{0,12},{1,13},{2,14},{3,15},{4,0},{5,1},{6,2},{7,3},{8,4},{9,5},{1... | collective-permute-start | bytes 786440 | tf_op jit(solution)/shard_map/ppermute | solution.py:448
  117.1 0.8 copy-start.5
Sparse Core Ops, SparseCore 0:
  21.0 60.4 all-gather.2

commit v4 on v3

--- a/solution.py
+++ b/solution.py
@@ -115,11 +115,14 @@
 def near_kernel(
     valid_ref,
     own_ref,
-    others_ref,
+    sides_ref,
+    across_ref,
     left_own_ref,
-    left_ref,
+    left_sides_ref,
+    left_across_ref,
     right_own_ref,
-    right_ref,
+    right_sides_ref,
+    right_across_ref,
     weight_ref,
     weight_t_ref,
     keys_ref,
@@ -152,7 +155,17 @@
     def _():
         chart(valid_ref, table, places)
 
-    refs = (own_ref, others_ref, left_own_ref, left_ref, right_own_ref, right_ref)
+    refs = (
+        own_ref,
+        sides_ref,
+        across_ref,
+        left_own_ref,
+        left_sides_ref,
+        left_across_ref,
+        right_own_ref,
+        right_sides_ref,
+        right_across_ref,
+    )
     pack(table, places, refs, 0, packed)
     blocks = (table[2, 0] + (BLOCK - 1)) >> 8
     peaks_ref[0] = project(
@@ -485,12 +498,24 @@
     above = shift(normed, 0, 1)
     below = shift(normed, 0, -1)
     across = shift(normed, 0, 2)
-    others = jnp.stack([above, below, across])
-    left = shift(others, 1, 0)
-    right = shift(others, -1, 0)
-    far_low = shift(jnp.stack([left_own, left[0]]), 1, 0)
-    far_high = shift(right[1:], -1, 0)
-    near = (normed[None], others, left_own[None], left, right_own[None], right)
+    sides = jnp.stack([above, below])
+    left_sides = shift(sides, 1, 0)
+    right_sides = shift(sides, -1, 0)
+    left_across = shift(across, 1, 0)
+    right_across = shift(across, -1, 0)
+    far_low = shift(jnp.stack([left_own, left_sides[0]]), 1, 0)
+    far_high = shift(jnp.stack([right_sides[1], right_across]), -1, 0)
+    near = (
+        normed[None],
+        sides,
+        across[None],
+        left_own[None],
+        left_sides,
+        left_across[None],
+        right_own[None],
+        right_sides,
+        right_across[None],
+    )
     return finish(
         chain_valid,
         near,

time: 149 us -> 144 us (0.966)
  the two profiles are of different devices: /device:TPU:206 before, /device:TPU:208 now
where the time goes in v4:
time: 144 us
  waiting for transfers between devices  49.2 us (34%)
  starting transfers between devices  39.7 us (28%)
  Pallas kernels  35.8 us (25%)
  between operations  13.7 us (10%)
  other arithmetic  3.73 us (3%)
  local copies, waits for them, and re-layouts  1.76 us (1%)
    ppermute x11, waiting for transfers between devices, shift(): return lax.ppermute(value, 'cols', pairs)  42.5 us
    ppermute x11, starting transfers between devices, shift(): return lax.ppermute(value, 'cols', pairs)  36.1 us
    pallas_call x1, Pallas kernels, attend(): pl.pallas_call(attend_kernel, grid=(heads,), in_specs=[SMEM, pl.BlockSpec...  23.5 us
    pallas_call x1, Pallas kernels, project_near(): pl.pallas_call(near_kernel, grid=(rows,), in_specs=[SMEM, *(piece_spec(pi...  10.1 us
    ppermute x1, waiting for transfers between devices, gather_bias(): lax.ppermute(bias_t, 'rows', [(r, (r + half) % count) for r in range(coun...  6.66 us
    ppermute x1, starting transfers between devices, gather_bias(): lax.ppermute(bias_t, 'rows', [(r, (r + half) % count) for r in range(coun...  3.6 us
  transfers between devices with their start and end apart: 13, of which 7 were waited for; matrix products, arithmetic and copies ran while one was open for 2% of the time, Pallas kernels for 7%

profile of v4, /device:TPU:208, one launch (start us, length us, event | category | flops | bytes accessed | tf_op | source)
XLA Modules:
  0.0 143.9 jit_solution(13099807027751083210)
XLA Ops:
  6.5 2.2 %prep.1 = (bf16[4,256,128]{2,1,0:T(8,128)(2,1)}, bf16[4,128,256]{2,1,0:T(8,128)(2,1)}) custom-call(s32[32]{0:T(128)} %valid_ref.5, bf16[4,256,128]{2,1,0:T(8,128)(2,1)} %pair_ref.1, bf16[4,256,128]{2,1,0:T(8,128)(2,1)} %bias_ref.1), custom_call_target="tpu_custom_call" | custom-call | tf_op jit(solution)/shard_map/prep/pallas_call | solution.py:45
  8.8 3.6 %collective-permute-start.11 = (bf16[4,128,256]{2,1,0:T(8,128)(2,1)}, bf16[4,128,256]{2,1,0:T(8,128)(2,1)S(1)}, u32[]{:S(2)}, u32[]{:S(2)}) collective-permute-start(bf16[4,128,256]{2,1,0:T(8,128)(2,1)} %get-tuple-element.18), channel_id=1, source_target_pairs={{0,256},{16,272},{32,288},{48,304},{64,320},{80,336},{96,352},{112... | collective-permute-start | bytes 786440 | tf_op jit(solution)/shard_map/ppermute | solution.py:467
  12.4 6.7 %collective-permute-done.11 = bf16[4,128,256]{2,1,0:T(8,128)(2,1)S(1)} collective-permute-done((bf16[4,128,256]{2,1,0:T(8,128)(2,1)}, bf16[4,128,256]{2,1,0:T(8,128)(2,1)S(1)}, u32[]{:S(2)}, u32[]{:S(2)}) %collective-permute-start.11) | collective-permute-done | bytes 262176 | tf_op jit(solution)/shard_map/ppermute | solution.py:467
  19.0 1.8 %pad_maximum_fusion.3 = bf16[2,4,128,256]{3,2,1,0:T(8,128)(2,1)} fusion(bf16[1,4,128,256]{3,2,1,0:T(8,128)(2,1)S(1)} %bitcast.23, bf16[1,4,128,256]{3,2,1,0:T(8,128)(2,1)} %bitcast.21), kind=kLoop, calls=%fused_computation.3 | loop fusion | flops 262144 | bytes 1048576 | tf_op jit(solution)/shard_map/stack | solution.py:468
  20.9 5.7 %collective-permute-start = (bf16[4,256,128]{2,1,0:T(8,128)(2,1)}, bf16[4,256,128]{2,1,0:T(8,128)(2,1)S(1)}, u32[]{:S(2)}, u32[]{:S(2)}) collective-permute-start(bf16[4,256,128]{2,1,0:T(8,128)(2,1)} %get-tuple-element.12), channel_id=1, source_target_pairs={{0,1},{1,2},{2,3},{3,0},{4,5},{5,6},{6,7},{7,4},{8,9},{9,10},{10,1... | collective-permute-start | bytes 786440 | tf_op jit(solution)/shard_map/ppermute | solution.py:461
  26.6 1.9 %collective-permute-start.1 = (bf16[4,256,128]{2,1,0:T(8,128)(2,1)}, bf16[4,256,128]{2,1,0:T(8,128)(2,1)S(1)}, u32[]{:S(2)}, u32[]{:S(2)}) collective-permute-start(bf16[4,256,128]{2,1,0:T(8,128)(2,1)} %get-tuple-element.12), channel_id=1, source_target_pairs={{0,3},{1,0},{2,1},{3,2},{4,7},{5,4},{6,5},{7,6},{8,11},{9,8},{10,9... | collective-permute-start | bytes 786440 | tf_op jit(solution)/shard_map/ppermute | solution.py:461
  28.5 8.5 %collective-permute-done = bf16[4,256,128]{2,1,0:T(8,128)(2,1)S(1)} collective-permute-done((bf16[4,256,128]{2,1,0:T(8,128)(2,1)}, bf16[4,256,128]{2,1,0:T(8,128)(2,1)S(1)}, u32[]{:S(2)}, u32[]{:S(2)}) %collective-permute-start) | collective-permute-done | bytes 262176 | tf_op jit(solution)/shard_map/ppermute | solution.py:461
  37.1 5.5 %collective-permute-done.1 = bf16[4,256,128]{2,1,0:T(8,128)(2,1)S(1)} collective-permute-done((bf16[4,256,128]{2,1,0:T(8,128)(2,1)}, bf16[4,256,128]{2,1,0:T(8,128)(2,1)S(1)}, u32[]{:S(2)}, u32[]{:S(2)}) %collective-permute-start.1) | collective-permute-done | bytes 262176 | tf_op jit(solution)/shard_map/ppermute | solution.py:461
  42.6 4.7 %collective-permute-start.7 = (bf16[2,4,256,128]{3,2,1,0:T(8,128)(2,1)S(1)}, bf16[2,4,256,128]{3,2,1,0:T(8,128)(2,1)S(1)}, u32[]{:S(2)}, u32[]{:S(2)}) collective-permute-start(bf16[2,4,256,128]{3,2,1,0:T(8,128)(2,1)S(1)} %pad_maximum_fusion.sides_ref), channel_id=1, source_target_pairs={{0,12},{1,13},{2,14},{3,15},{4,0},{5,1},{6,2},{7,3},{8,4},{9,5},{1... | collective-permute-start | bytes 1572872 | tf_op jit(solution)/shard_map/ppermute | solution.py:461
  47.3 3.2 %collective-permute-start.2 = (bf16[4,256,128]{2,1,0:T(8,128)(2,1)}, bf16[4,256,128]{2,1,0:T(8,128)(2,1)}, u32[]{:S(2)}, u32[]{:S(2)}) collective-permute-start(bf16[4,256,128]{2,1,0:T(8,128)(2,1)} %get-tuple-element.12), channel_id=1, source_target_pairs={{0,2},{1,3},{2,0},{3,1},{4,6},{5,7},{6,4},{7,5},{8,10},{9,11},{10,... | collective-permute-start | bytes 786440 | tf_op jit(solution)/shard_map/ppermute | solution.py:461
  50.5 1.9 %collective-permute-start.4 = (bf16[2,4,256,128]{3,2,1,0:T(8,128)(2,1)S(1)}, bf16[2,4,256,128]{3,2,1,0:T(8,128)(2,1)S(1)}, u32[]{:S(2)}, u32[]{:S(2)}) collective-permute-start(bf16[2,4,256,128]{3,2,1,0:T(8,128)(2,1)S(1)} %pad_maximum_fusion.sides_ref), channel_id=1, source_target_pairs={{0,4},{1,5},{2,6},{3,7},{4,8},{5,9},{6,10},{7,11},{8,12},{9,13},{1... | collective-permute-start | bytes 1572872 | tf_op jit(solution)/shard_map/ppermute | solution.py:461
  52.4 13.8 %collective-permute-done.2 = bf16[4,256,128]{2,1,0:T(8,128)(2,1)} collective-permute-done((bf16[4,256,128]{2,1,0:T(8,128)(2,1)}, bf16[4,256,128]{2,1,0:T(8,128)(2,1)}, u32[]{:S(2)}, u32[]{:S(2)}) %collective-permute-start.2) | collective-permute-done | bytes 262176 | tf_op jit(solution)/shard_map/ppermute | solution.py:461
  66.2 2.7 %collective-permute-start.8 = (bf16[4,256,128]{2,1,0:T(8,128)(2,1)}, bf16[4,256,128]{2,1,0:T(8,128)(2,1)S(1)}, u32[]{:S(2)}, u32[]{:S(2)}) collective-permute-start(bf16[4,256,128]{2,1,0:T(8,128)(2,1)} %collective-permute-done.2), channel_id=1, source_target_pairs={{0,12},{1,13},{2,14},{3,15},{4,0},{5,1},{6,2},{7,3},{8,4},{9,5},{1... | collective-permute-start | bytes 786440 | tf_op jit(solution)/shard_map/ppermute | solution.py:461
  69.0 3.1 %collective-permute-start.3 = (bf16[4,256,128]{2,1,0:T(8,128)(2,1)}, bf16[4,256,128]{2,1,0:T(8,128)(2,1)S(1)}, u32[]{:S(2)}, u32[]{:S(2)}) collective-permute-start(bf16[4,256,128]{2,1,0:T(8,128)(2,1)} %get-tuple-element.12), channel_id=1, source_target_pairs={{0,4},{1,5},{2,6},{3,7},{4,8},{5,9},{6,10},{7,11},{8,12},{9,13},{1... | collective-permute-start | bytes 786440 | tf_op jit(solution)/shard_map/ppermute | solution.py:461
  72.1 3.5 %collective-permute-done.8 = bf16[4,256,128]{2,1,0:T(8,128)(2,1)S(1)} collective-permute-done((bf16[4,256,128]{2,1,0:T(8,128)(2,1)}, bf16[4,256,128]{2,1,0:T(8,128)(2,1)S(1)}, u32[]{:S(2)}, u32[]{:S(2)}) %collective-permute-start.8) | collective-permute-done | bytes 262176 | tf_op jit(solution)/shard_map/ppermute | solution.py:461
  76.5 3.9 %collective-permute-start.10 = (bf16[2,4,256,128]{3,2,1,0:T(8,128)(2,1)}, bf16[2,4,256,128]{3,2,1,0:T(8,128)(2,1)S(1)}, u32[]{:S(2)}, u32[]{:S(2)}) collective-permute-start(bf16[2,4,256,128]{3,2,1,0:T(8,128)(2,1)} %pad_maximum_fusion.2), channel_id=1, source_target_pairs={{0,12},{1,13},{2,14},{3,15},{4,0},{5,1},{6,2},{7,3},{8,4},{9,5},{1... | collective-permute-start | bytes 1572872 | tf_op jit(solution)/shard_map/ppermute | solution.py:461
  80.5 0.9 pad_maximum_fusion.1
  81.5 1.9 %collective-permute-start.9 = (bf16[2,4,256,128]{3,2,1,0:T(8,128)(2,1)}, bf16[2,4,256,128]{3,2,1,0:T(8,128)(2,1)S(1)}, u32[]{:S(2)}, u32[]{:S(2)}) collective-permute-start(bf16[2,4,256,128]{3,2,1,0:T(8,128)(2,1)} %pad_maximum_fusion.1), channel_id=1, source_target_pairs={{0,4},{1,5},{2,6},{3,7},{4,8},{5,9},{6,10},{7,11},{8,12},{9,13},{1... | collective-permute-start | bytes 1572872 | tf_op jit(solution)/shard_map/ppermute | solution.py:461
  83.4 5.1 %collective-permute-start.6 = (bf16[4,256,128]{2,1,0:T(8,128)(2,1)S(1)}, bf16[4,256,128]{2,1,0:T(8,128)(2,1)}, u32[]{:S(2)}, u32[]{:S(2)}) collective-permute-start(bf16[4,256,128]{2,1,0:T(8,128)(2,1)S(1)} %copy-done.8), channel_id=1, source_target_pairs={{0,12},{1,13},{2,14},{3,15},{4,0},{5,1},{6,2},{7,3},{8,4},{9,5},{1... | collective-permute-start | bytes 786440 | tf_op jit(solution)/shard_map/ppermute | solution.py:461
  88.5 1.9 %collective-permute-start.5 = (bf16[4,256,128]{2,1,0:T(8,128)(2,1)}, bf16[4,256,128]{2,1,0:T(8,128)(2,1)}, u32[]{:S(2)}, u32[]{:S(2)}) collective-permute-start(bf16[4,256,128]{2,1,0:T(8,128)(2,1)} %collective-permute-done.2), channel_id=1, source_target_pairs={{0,4},{1,5},{2,6},{3,7},{4,8},{5,9},{6,10},{7,11},{8,12},{9,13},{1... | collective-permute-start | bytes 786440 | tf_op jit(solution)/shard_map/ppermute | solution.py:461
  91.2 5.2 %collective-permute-done.6 = bf16[4,256,128]{2,1,0:T(8,128)(2,1)} collective-permute-done((bf16[4,256,128]{2,1,0:T(8,128)(2,1)S(1)}, bf16[4,256,128]{2,1,0:T(8,128)(2,1)}, u32[]{:S(2)}, u32[]{:S(2)}) %collective-permute-start.6) | collective-permute-done | bytes 262176 | tf_op jit(solution)/shard_map/ppermute | solution.py:461
  96.5 5.9 %collective-permute-done.5 = bf16[4,256,128]{2,1,0:T(8,128)(2,1)} collective-permute-done((bf16[4,256,128]{2,1,0:T(8,128)(2,1)}, bf16[4,256,128]{2,1,0:T(8,128)(2,1)}, u32[]{:S(2)}, u32[]{:S(2)}) %collective-permute-start.5) | collective-permute-done | bytes 262176 | tf_op jit(solution)/shard_map/ppermute | solution.py:461
  102.4 10.1 %near.1 = (bf16[4,3328,128]{2,1,0:T(8,128)(2,1)}, bf16[4,4,48,3328]{3,2,1,0:T(8,128)(2,1)}, bf16[4,4,128,256]{3,2,1,0:T(8,128)(2,1)}, f32[4,4,32,256]{3,2,1,0:T(8,128)}, f32[4,8,128]{2,1,0:T(8,128)}) custom-call(s32[32]{0:T(128)} %valid_ref.5, bf16[1,4,256,128]{3,2,1,0:T(8,128)(2,1)} %bitcast.19, bf16[2,4,256,128]{3,2,1,0:T(8,128)(2,1)} %copy-done, ...), custom_call_target="tpu_custom_call" | custom-call | tf_op jit(solution)/shard_map/near/pallas_call | solution.py:198
  113.5 23.5 %attend.1 = bf16[4,256,128]{2,1,0:T(8,128)(2,1)} custom-call(s32[32]{0:T(128)} %valid_ref.5, bf16[4,3328,128]{2,1,0:T(8,128)(2,1)} %get-tuple-element.13.keys_hbm, bf16[4,4,48,3328]{3,2,1,0:T(8,128)(2,1)} %get-tuple-element.14.values_hbm, bf16[2,4,256,128]{3,2,1,0:T(8,128)(2,1)} %copy-done.7, bf16[2,4,256,128]{3,2,1,0:T(8,128)(2,1)} %copy-done.6, ...), custom_call_target="tpu_custom_call" | custom-call | tf_op jit(solution)/shard_map/attend/pallas_call | solution.py:409
  (31 shorter events, 2.8 us)
Async XLA Ops:
  6.5 83.9 %copy-start.1 = (bf16[128,512]{1,0:T(8,128)(2,1)S(1)}, bf16[128,512]{1,0:T(8,128)(2,1)}, u32[]{:S(2)}) copy-start(bf16[128,512]{1,0:T(8,128)(2,1)} %weight_ref.3) | copy-start | bytes 393220
  6.5 106.0 %all-gather.3.cloned.1.call-start = ((), (), s32[]{:S(2)}) async-start(), calls=%async_computation | async-start | bytes 8912896 | tf_op jit(solution)/shard_map/all_gather | solution.py:470
  8.8 74.6 %copy-start.8 = (bf16[4,256,128]{2,1,0:T(8,128)(2,1)S(1)}, bf16[4,256,128]{2,1,0:T(8,128)(2,1)}, u32[]{:S(2)}) copy-start(bf16[4,256,128]{2,1,0:T(8,128)(2,1)} %get-tuple-element.12) | copy-start | bytes 786436
  8.8 10.3 %collective-permute-start.11 = (bf16[4,128,256]{2,1,0:T(8,128)(2,1)}, bf16[4,128,256]{2,1,0:T(8,128)(2,1)S(1)}, u32[]{:S(2)}, u32[]{:S(2)}) collective-permute-start(bf16[4,128,256]{2,1,0:T(8,128)(2,1)} %get-tuple-element.18), channel_id=1, source_target_pairs={{0,256},{16,272},{32,288},{48,304},{64,320},{80,336},{96,352},{112... | collective-permute-start | bytes 786440 | tf_op jit(solution)/shard_map/ppermute | solution.py:467
  20.9 16.2 %collective-permute-start = (bf16[4,256,128]{2,1,0:T(8,128)(2,1)}, bf16[4,256,128]{2,1,0:T(8,128)(2,1)S(1)}, u32[]{:S(2)}, u32[]{:S(2)}) collective-permute-start(bf16[4,256,128]{2,1,0:T(8,128)(2,1)} %get-tuple-element.12), channel_id=1, source_target_pairs={{0,1},{1,2},{2,3},{3,0},{4,5},{5,6},{6,7},{7,4},{8,9},{9,10},{10,1... | collective-permute-start | bytes 786440 | tf_op jit(solution)/shard_map/ppermute | solution.py:461
  26.6 16.0 %collective-permute-start.1 = (bf16[4,256,128]{2,1,0:T(8,128)(2,1)}, bf16[4,256,128]{2,1,0:T(8,128)(2,1)S(1)}, u32[]{:S(2)}, u32[]{:S(2)}) collective-permute-start(bf16[4,256,128]{2,1,0:T(8,128)(2,1)} %get-tuple-element.12), channel_id=1, source_target_pairs={{0,3},{1,0},{2,1},{3,2},{4,7},{5,4},{6,5},{7,6},{8,11},{9,8},{10,9... | collective-permute-start | bytes 786440 | tf_op jit(solution)/shard_map/ppermute | solution.py:461
  42.6 59.8 %copy-start = (bf16[2,4,256,128]{3,2,1,0:T(8,128)(2,1)}, bf16[2,4,256,128]{3,2,1,0:T(8,128)(2,1)S(1)}, u32[]{:S(2)}) copy-start(bf16[2,4,256,128]{3,2,1,0:T(8,128)(2,1)S(1)} %pad_maximum_fusion.sides_ref) | copy-start | bytes 1572868
  42.6 29.5 %collective-permute-start.7 = (bf16[2,4,256,128]{3,2,1,0:T(8,128)(2,1)S(1)}, bf16[2,4,256,128]{3,2,1,0:T(8,128)(2,1)S(1)}, u32[]{:S(2)}, u32[]{:S(2)}) collective-permute-start(bf16[2,4,256,128]{3,2,1,0:T(8,128)(2,1)S(1)} %pad_maximum_fusion.sides_ref), channel_id=1, source_target_pairs={{0,12},{1,13},{2,14},{3,15},{4,0},{5,1},{6,2},{7,3},{8,4},{9,5},{1... | collective-permute-start | bytes 1572872 | tf_op jit(solution)/shard_map/ppermute | solution.py:461
  47.3 18.9 %collective-permute-start.2 = (bf16[4,256,128]{2,1,0:T(8,128)(2,1)}, bf16[4,256,128]{2,1,0:T(8,128)(2,1)}, u32[]{:S(2)}, u32[]{:S(2)}) collective-permute-start(bf16[4,256,128]{2,1,0:T(8,128)(2,1)} %get-tuple-element.12), channel_id=1, source_target_pairs={{0,2},{1,3},{2,0},{3,1},{4,6},{5,7},{6,4},{7,5},{8,10},{9,11},{10,... | collective-permute-start | bytes 786440 | tf_op jit(solution)/shard_map/ppermute | solution.py:461
  50.5 30.0 %collective-permute-start.4 = (bf16[2,4,256,128]{3,2,1,0:T(8,128)(2,1)S(1)}, bf16[2,4,256,128]{3,2,1,0:T(8,128)(2,1)S(1)}, u32[]{:S(2)}, u32[]{:S(2)}) collective-permute-start(bf16[2,4,256,128]{3,2,1,0:T(8,128)(2,1)S(1)} %pad_maximum_fusion.sides_ref), channel_id=1, source_target_pairs={{0,4},{1,5},{2,6},{3,7},{4,8},{5,9},{6,10},{7,11},{8,12},{9,13},{1... | collective-permute-start | bytes 1572872 | tf_op jit(solution)/shard_map/ppermute | solution.py:461
  66.2 9.4 %collective-permute-start.8 = (bf16[4,256,128]{2,1,0:T(8,128)(2,1)}, bf16[4,256,128]{2,1,0:T(8,128)(2,1)S(1)}, u32[]{:S(2)}, u32[]{:S(2)}) collective-permute-start(bf16[4,256,128]{2,1,0:T(8,128)(2,1)} %collective-permute-done.2), channel_id=1, source_target_pairs={{0,12},{1,13},{2,14},{3,15},{4,0},{5,1},{6,2},{7,3},{8,4},{9,5},{1... | collective-permute-start | bytes 786440 | tf_op jit(solution)/shard_map/ppermute | solution.py:461
  69.0 11.6 %collective-permute-start.3 = (bf16[4,256,128]{2,1,0:T(8,128)(2,1)}, bf16[4,256,128]{2,1,0:T(8,128)(2,1)S(1)}, u32[]{:S(2)}, u32[]{:S(2)}) collective-permute-start(bf16[4,256,128]{2,1,0:T(8,128)(2,1)} %get-tuple-element.12), channel_id=1, source_target_pairs={{0,4},{1,5},{2,6},{3,7},{4,8},{5,9},{6,10},{7,11},{8,12},{9,13},{1... | collective-permute-start | bytes 786440 | tf_op jit(solution)/shard_map/ppermute | solution.py:461
  72.1 30.3 %copy-start.2 = (bf16[2,4,256,128]{3,2,1,0:T(8,128)(2,1)}, bf16[2,4,256,128]{3,2,1,0:T(8,128)(2,1)S(1)}, u32[]{:S(2)}) copy-start(bf16[2,4,256,128]{3,2,1,0:T(8,128)(2,1)S(1)} %collective-permute-done.7.right_sides_ref) | copy-start | bytes 1572868
  75.6 26.8 %copy-start.4 = (bf16[4,256,128]{2,1,0:T(8,128)(2,1)}, bf16[4,256,128]{2,1,0:T(8,128)(2,1)S(1)}, u32[]{:S(2)}) copy-start(bf16[4,256,128]{2,1,0:T(8,128)(2,1)S(1)} %collective-permute-done.8) | copy-start | bytes 786436
  76.5 36.0 %collective-permute-start.10 = (bf16[2,4,256,128]{3,2,1,0:T(8,128)(2,1)}, bf16[2,4,256,128]{3,2,1,0:T(8,128)(2,1)S(1)}, u32[]{:S(2)}, u32[]{:S(2)}) collective-permute-start(bf16[2,4,256,128]{3,2,1,0:T(8,128)(2,1)} %pad_maximum_fusion.2), channel_id=1, source_target_pairs={{0,12},{1,13},{2,14},{3,15},{4,0},{5,1},{6,2},{7,3},{8,4},{9,5},{1... | collective-permute-start | bytes 1572872 | tf_op jit(solution)/shard_map/ppermute | solution.py:461
  80.5 21.9 %copy-start.3 = (bf16[2,4,256,128]{3,2,1,0:T(8,128)(2,1)}, bf16[2,4,256,128]{3,2,1,0:T(8,128)(2,1)S(1)}, u32[]{:S(2)}) copy-start(bf16[2,4,256,128]{3,2,1,0:T(8,128)(2,1)S(1)} %collective-permute-done.4.left_sides_ref) | copy-start | bytes 1572868
  80.5 21.9 %copy-start.5 = (bf16[4,256,128]{2,1,0:T(8,128)(2,1)}, bf16[4,256,128]{2,1,0:T(8,128)(2,1)S(1)}, u32[]{:S(2)}) copy-start(bf16[4,256,128]{2,1,0:T(8,128)(2,1)S(1)} %collective-permute-done.3) | copy-start | bytes 786436
  81.5 31.1 %collective-permute-start.9 = (bf16[2,4,256,128]{3,2,1,0:T(8,128)(2,1)}, bf16[2,4,256,128]{3,2,1,0:T(8,128)(2,1)S(1)}, u32[]{:S(2)}, u32[]{:S(2)}) collective-permute-start(bf16[2,4,256,128]{3,2,1,0:T(8,128)(2,1)} %pad_maximum_fusion.1), channel_id=1, source_target_pairs={{0,4},{1,5},{2,6},{3,7},{4,8},{5,9},{6,10},{7,11},{8,12},{9,13},{1... | collective-permute-start | bytes 1572872 | tf_op jit(solution)/shard_map/ppermute | solution.py:461
  83.4 13.1 %collective-permute-start.6 = (bf16[4,256,128]{2,1,0:T(8,128)(2,1)S(1)}, bf16[4,256,128]{2,1,0:T(8,128)(2,1)}, u32[]{:S(2)}, u32[]{:S(2)}) collective-permute-start(bf16[4,256,128]{2,1,0:T(8,128)(2,1)S(1)} %copy-done.8), channel_id=1, source_target_pairs={{0,12},{1,13},{2,14},{3,15},{4,0},{5,1},{6,2},{7,3},{8,4},{9,5},{1... | collective-permute-start | bytes 786440 | tf_op jit(solution)/shard_map/ppermute | solution.py:461
  88.5 13.8 %collective-permute-start.5 = (bf16[4,256,128]{2,1,0:T(8,128)(2,1)}, bf16[4,256,128]{2,1,0:T(8,128)(2,1)}, u32[]{:S(2)}, u32[]{:S(2)}) collective-permute-start(bf16[4,256,128]{2,1,0:T(8,128)(2,1)} %collective-permute-done.2), channel_id=1, source_target_pairs={{0,4},{1,5},{2,6},{3,7},{4,8},{5,9},{6,10},{7,11},{8,12},{9,13},{1... | collective-permute-start | bytes 786440 | tf_op jit(solution)/shard_map/ppermute | solution.py:461
  112.5 0.8 copy-start.6
  112.5 1.0 copy-start.7
Sparse Core Ops, SparseCore 0:
  21.0 60.3 all-gather.2

commit v5 on v4

--- a/solution.py
+++ b/solution.py
@@ -178,6 +178,54 @@
         values_ref.at[0],
         jnp.zeros((8, inner), jnp.float32),
     )
+
+
+def far_kernel(
+    valid_ref,
+    low_ref,
+    high_ref,
+    weight_ref,
+    weight_t_ref,
+    queries_ref,
+    peaks_ref,
+    keys_ref,
+    values_ref,
+    safe_ref,
+    packed,
+    table,
+    reach,
+):
+    row = pl.program_id(0)
+    heads, _, inner, _ = queries_ref.shape
+    head_size = inner // heads
+    places = range(NEAR, NEAR + FAR)
+
+    @pl.when(row == 0)
+    def _():
+        chart(valid_ref, table, places)
+        reach[0] = jnp.float32(0.0)
+
+    pack(table, places, (low_ref, high_ref), 0, packed)
+    blocks = (table[2, NEAR] + (BLOCK - 1)) >> 8
+    peak = project(
+        packed,
+        weight_ref,
+        weight_t_ref,
+        blocks,
+        0,
+        keys_ref.at[0],
+        values_ref.at[0],
+        peaks_ref[0],
+    )
+    peak = jnp.max(peak, axis=0, keepdims=True)
+    peak = jnp.transpose(jnp.broadcast_to(peak, (inner, inner)))[:, 0:1]
+    best = reach[0]
+    for h in range(heads):
+        span = slice(h * head_size, (h + 1) * head_size)
+        spread = jnp.abs(queries_ref[h, 0, span, :].astype(jnp.float32)) * peak[span]
+        best = jnp.maximum(best, jnp.max(jnp.sum(spread, axis=0, keepdims=True)))
+    reach[0] = best
+    safe_ref[0] = (best < REACH).astype(jnp.int32)
 
 
 def piece_spec(piece):
@@ -226,29 +274,58 @@
     )(chain_valid, *pieces, weight, weight_t)
 
 
+def project_far(chain_valid, pieces, weight, weight_t, queries, peaks, depth):
+    heads, rows, inner, cols = queries.shape
+    width = weight.shape[0]
+    return pl.pallas_call(
+        far_kernel,
+        grid=(rows,),
+        in_specs=[
+            SMEM,
+            *(piece_spec(piece) for piece in pieces),
+            fixed(weight),
+            fixed(weight_t),
+            pl.BlockSpec((heads, 1, inner, cols), lambda i: (0, i, 0, 0)),
+            pl.BlockSpec((1, 8, inner), lambda i: (i, 0, 0)),
+        ],
+        out_specs=(
+            pl.BlockSpec((1, FAR_ROOM, inner), lambda i: (i, 0, 0)),
+            pl.BlockSpec((1, heads, depth, FAR_ROOM), lambda i: (i, 0, 0, 0)),
+            SMEM,
+        ),
+        out_shape=(
+            jax.ShapeDtypeStruct((rows, FAR_ROOM, inner), jnp.bfloat16),
+            jax.ShapeDtypeStruct((rows, heads, depth, FAR_ROOM), jnp.bfloat16),
+            jax.ShapeDtypeStruct((1,), jnp.int32),
+        ),
+        scratch_shapes=[
+            pltpu.VMEM((FAR_ROOM, width), jnp.bfloat16),
+            pltpu.SMEM((3, NEAR + FAR), jnp.int32),
+            pltpu.SMEM((1,), jnp.float32),
+        ],
+        name="far",
+    )(chain_valid, *pieces, weight, weight_t, queries, peaks)
+
+
 def attend_kernel(
     valid_ref,
-    keys_hbm,
-    values_hbm,
-    low_ref,
-    high_ref,
-    weight_ref,
-    weight_t_ref,
+    safe,
+    near_keys,
+    near_values,
+    far_keys,
+    far_values,
     queries,
-    peaks_ref,
     gates,
     bias_ref,
     out_weight_ref,
     out_ref,
     keys,
     values,
-    packed,
     gated,
     bias,
     shifted,
     sums,
     table,
-    safe,
     sems,
 ):
     heads, rows, inner, cols = queries.shape
@@ -257,49 +334,26 @@
     half = bias_ref.shape[0]
     y_low = lax.axis_index("rows") >> 4
     spans = ((0, range(NEAR)), (NEAR_ROOM, range(NEAR, NEAR + FAR)))
-    key_copy = pltpu.make_async_copy(keys_hbm, keys.at[:, pl.ds(0, NEAR_ROOM), :], sems.at[heads])
-
-    def value_copy(h):
-        return pltpu.make_async_copy(
-            values_hbm.at[:, h], values.at[:, h, :, pl.ds(0, NEAR_ROOM)], sems.at[h]
+    near_room, far_room = pl.ds(0, NEAR_ROOM), pl.ds(NEAR_ROOM, FAR_ROOM)
+    key_copies = (
+        pltpu.make_async_copy(near_keys, keys.at[:, near_room, :], sems.at[0, heads]),
+        pltpu.make_async_copy(far_keys, keys.at[:, far_room, :], sems.at[1, heads]),
+    )
+
+    def value_copies(h):
+        return (
+            pltpu.make_async_copy(
+                near_values.at[:, h], values.at[:, h, :, near_room], sems.at[0, h]
+            ),
+            pltpu.make_async_copy(far_values.at[:, h], values.at[:, h, :, far_room], sems.at[1, h]),
         )
 
     @pl.when(head == 0)
     def _():
-        key_copy.start()
-        for h in range(heads):
-            value_copy(h).start()
+        for copy in key_copies + value_copies(0):
+            copy.start()
         for _, places in spans:
             chart(valid_ref, table, places)
-        far = range(NEAR, NEAR + FAR)
-        blocks = (table[2, NEAR] + (BLOCK - 1)) >> 8
-        best = jnp.float32(0.0)
-        for row in range(rows):
-            pack(table, far, (low_ref, high_ref), row, packed)
-            peak = project(
-                packed,
-                weight_ref,
-                weight_t_ref,
-                blocks,
-                NEAR_ROOM,
-                keys.at[row],
-                values.at[row],
-                peaks_ref[row],
-            )
-            peak = jnp.max(peak, axis=0, keepdims=True)
-            peak = jnp.transpose(jnp.broadcast_to(peak, (inner, inner)))[:, 0:1]
-            for h in range(heads):
-                span = slice(h * head_size, (h + 1) * head_size)
-                spread = jnp.abs(queries[h, row, span, :].astype(jnp.float32)) * peak[span]
-                best = jnp.maximum(best, jnp.max(jnp.sum(spread, axis=0, keepdims=True)))
-        safe[0] = (best < REACH).astype(jnp.int32)
-        key_copy.wait()
-
-    for h in range(heads):
-
-        @pl.when(head == h)
-        def _(h=h):
-            value_copy(h).wait()
 
     top = jnp.full((GROUP, cols), MASKED, jnp.bfloat16)
     counts = []
@@ -314,11 +368,27 @@
                 top = jnp.maximum(top, piece[group : group + GROUP])
             return top
 
-        top = lax.fori_loop(places[0], places[-1] + 1, move, top)
+        top = lax.fori_loop(places[0], places[-1] + 1, move, top, unroll=4)
         bias[pl.ds(pl.multiple_of(base + total, GROUP), BLOCK), :] = jnp.full(
             (BLOCK, cols), MASKED, jnp.bfloat16
         )
         counts.append((total + (BLOCK - 1)) >> 8)
+
+    @pl.when(head == 0)
+    def _():
+        for copy in key_copies:
+            copy.wait()
+        for h in range(1, heads):
+            for copy in value_copies(h):
+                copy.start()
+
+    for h in range(heads):
+
+        @pl.when(head == h)
+        def _(h=h):
+            for copy in value_copies(h):
+                copy.wait()
+
     near_blocks, blocks = counts[0], counts[0] + counts[1]
     top = jnp.max(top.astype(jnp.float32), axis=0, keepdims=True)
     sums[...] = jnp.zeros_like(sums)
@@ -400,10 +470,19 @@
 
 
 def attend(
-    chain_valid, keys, values, far, weight, weight_t, queries, peaks, gates, bias, output_weight
+    chain_valid,
+    safe,
+    near_keys,
+    near_values,
+    far_keys,
+    far_values,
+    queries,
+    gates,
+    bias,
+    output_weight,
 ):
     heads, rows, inner, cols = queries.shape
-    depth = values.shape[2]
+    depth = near_values.shape[2]
     half, pair, _, slot, _ = bias.shape
     width = output_weight.shape[1]
     return pl.pallas_call(
@@ -411,13 +490,9 @@
         grid=(heads,),
         in_specs=[
             SMEM,
-            pl.BlockSpec(memory_space=pl.ANY),
-            pl.BlockSpec(memory_space=pl.ANY),
-            *(fixed(piece) for piece in far),
-            fixed(weight),
-            fixed(weight_t),
+            SMEM,
+            *[pl.BlockSpec(memory_space=pl.ANY)] * 4,
             fixed(queries),
-            fixed(peaks),
             pl.BlockSpec((1, rows, inner // heads, cols), lambda h: (h, 0, 0, 0)),
             pl.BlockSpec((half, pair, 1, slot, cols), lambda h: (0, 0, h, 0, 0)),
             fixed(output_weight),
@@ -426,26 +501,23 @@
         scratch_shapes=[
             pltpu.VMEM((rows, ROOM, inner), jnp.bfloat16),
             pltpu.VMEM((rows, heads, depth, ROOM), jnp.bfloat16),
-            pltpu.VMEM((FAR_ROOM, weight.shape[0]), jnp.bfloat16),
             pltpu.VMEM((rows, inner, cols), jnp.bfloat16),
             pltpu.VMEM((ROOM, cols), jnp.bfloat16),
             pltpu.VMEM((2, BLOCK, cols), jnp.float32),
             pltpu.VMEM((rows, depth, cols), jnp.float32),
             pltpu.SMEM((3, NEAR + FAR), jnp.int32),
-            pltpu.SMEM((1,), jnp.int32),
-            pltpu.SemaphoreType.DMA((heads + 1,)),
+            pltpu.SemaphoreType.DMA((2, heads + 1)),
         ],
         out_shape=jax.ShapeDtypeStruct((rows, cols, width), jnp.bfloat16),
         name="attend",
     )(
         chain_valid,
-        keys,
-        values,
-        *far,
-        weight,
-        weight_t,
+        safe,
+        near_keys,
+        near_values,
+        far_keys,
+        far_values,
         queries,
-        peaks,
         gates,
         bias,
         output_weight,
@@ -475,15 +547,17 @@
     keys, values, queries, gates, peaks = project_near(
         chain_valid, near, project_weight, weight_t, heads
     )
+    far_keys, far_values, safe = project_far(
+        chain_valid, far, project_weight, weight_t, queries, peaks, values.shape[2]
+    )
     return attend(
         chain_valid,
+        safe,
         keys,
         values,
-        far,
-        project_weight,
-        weight_t,
+        far_keys,
+        far_values,
         queries,
-        peaks,
         gates,
         bias,
         output_weight,
@@ -497,7 +571,10 @@
     right_own = shift(normed, -1, 0)
     above = shift(normed, 0, 1)
     below = shift(normed, 0, -1)
-    across = shift(normed, 0, 2)
+    half = normed.shape[0] // 2
+    across_low = shift(above[:half], 0, 1)
+    across_high = shift(below[half:], 0, -1)
+    across = jnp.concatenate([across_low, across_high])
     sides = jnp.stack([above, below])
     left_sides = shift(sides, 1, 0)
     right_sides = shift(sides, -1, 0)

time: 144 us -> 138 us (0.958)
  the two profiles are of different devices: /device:TPU:208 before, /device:TPU:1 now
where the time goes in v5:
time: 138 us; the launch traced here: 136 us
  starting transfers between devices  47.6 us (34%)
  Pallas kernels  40.1 us (29%)
  waiting for transfers between devices  31.4 us (23%)
  between operations  13.7 us (10%)
  other arithmetic  1.98 us (1%)
    ppermute x12, starting transfers between devices, shift(): return lax.ppermute(value, 'cols', pairs)  43.5 us
    ppermute x12, waiting for transfers between devices, shift(): return lax.ppermute(value, 'cols', pairs)  27.5 us
    pallas_call x1, Pallas kernels, attend(): pl.pallas_call(attend_kernel, grid=(heads,), in_specs=[SMEM, SMEM, *[pl.B...  22 us
    pallas_call x1, Pallas kernels, project_near(): pl.pallas_call(near_kernel, grid=(rows,), in_specs=[SMEM, *(piece_spec(pi...  10.1 us
    pallas_call x1, Pallas kernels, project_far(): pl.pallas_call(far_kernel, grid=(rows,), in_specs=[SMEM, *(piece_spec(pie...  5.76 us
    ppermute x1, starting transfers between devices, gather_bias(): lax.ppermute(bias_t, 'rows', [(r, (r + half) % count) for r in range(coun...  4.14 us
    ppermute x1, waiting for transfers between devices, gather_bias(): lax.ppermute(bias_t, 'rows', [(r, (r + half) % count) for r in range(coun...  3.96 us
  transfers between devices with their start and end apart: 14, of which 8 were waited for; matrix products, arithmetic and copies ran while one was open for 1% of the time, Pallas kernels for 12%

profile of v5, /device:TPU:1, one launch (start us, length us, event | category | flops | bytes accessed | tf_op | source)
XLA Modules:
  0.0 135.6 jit_solution(57439412722922751)
XLA Ops:
  6.5 2.2 %prep.1 = (bf16[4,256,128]{2,1,0:T(8,128)(2,1)}, bf16[4,128,256]{2,1,0:T(8,128)(2,1)}) custom-call(s32[32]{0:T(128)} %valid_ref.7, bf16[4,256,128]{2,1,0:T(8,128)(2,1)} %pair_ref.1, bf16[4,256,128]{2,1,0:T(8,128)(2,1)} %bias_ref.1), custom_call_target="tpu_custom_call" | custom-call | tf_op jit(solution)/shard_map/prep/pallas_call | solution.py:45
  8.7 4.1 %collective-permute-start.12 = (bf16[4,128,256]{2,1,0:T(8,128)(2,1)}, bf16[4,128,256]{2,1,0:T(8,128)(2,1)S(1)}, u32[]{:S(2)}, u32[]{:S(2)}) collective-permute-start(bf16[4,128,256]{2,1,0:T(8,128)(2,1)} %get-tuple-element.24), channel_id=1, source_target_pairs={{0,256},{16,272},{32,288},{48,304},{64,320},{80,336},{96,352},{112... | collective-permute-start | bytes 786440 | tf_op jit(solution)/shard_map/ppermute | solution.py:539
  12.9 4.0 %collective-permute-done.12 = bf16[4,128,256]{2,1,0:T(8,128)(2,1)S(1)} collective-permute-done((bf16[4,128,256]{2,1,0:T(8,128)(2,1)}, bf16[4,128,256]{2,1,0:T(8,128)(2,1)S(1)}, u32[]{:S(2)}, u32[]{:S(2)}) %collective-permute-start.12) | collective-permute-done | bytes 262176 | tf_op jit(solution)/shard_map/ppermute | solution.py:539
  18.7 6.3 %collective-permute-start.1 = (bf16[4,256,128]{2,1,0:T(8,128)(2,1)}, bf16[4,256,128]{2,1,0:T(8,128)(2,1)S(1)}, u32[]{:S(2)}, u32[]{:S(2)}) collective-permute-start(bf16[4,256,128]{2,1,0:T(8,128)(2,1)} %get-tuple-element.15), channel_id=1, source_target_pairs={{0,1},{1,2},{2,3},{3,0},{4,5},{5,6},{6,7},{7,4},{8,9},{9,10},{10,1... | collective-permute-start | bytes 786440 | tf_op jit(solution)/shard_map/ppermute | solution.py:533
  25.0 3.6 %collective-permute-start.2 = (bf16[4,256,128]{2,1,0:T(8,128)(2,1)}, bf16[4,256,128]{2,1,0:T(8,128)(2,1)S(1)}, u32[]{:S(2)}, u32[]{:S(2)}) collective-permute-start(bf16[4,256,128]{2,1,0:T(8,128)(2,1)} %get-tuple-element.15), channel_id=1, source_target_pairs={{0,3},{1,0},{2,1},{3,2},{4,7},{5,4},{6,5},{7,6},{8,11},{9,8},{10,9... | collective-permute-start | bytes 786440 | tf_op jit(solution)/shard_map/ppermute | solution.py:533
  28.6 3.0 %collective-permute-done.1 = bf16[4,256,128]{2,1,0:T(8,128)(2,1)S(1)} collective-permute-done((bf16[4,256,128]{2,1,0:T(8,128)(2,1)}, bf16[4,256,128]{2,1,0:T(8,128)(2,1)S(1)}, u32[]{:S(2)}, u32[]{:S(2)}) %collective-permute-start.1) | collective-permute-done | bytes 262176 | tf_op jit(solution)/shard_map/ppermute | solution.py:533
  31.6 6.9 %collective-permute-start.6 = (bf16[2,256,128]{2,1,0:T(8,128)(2,1)S(1)}, bf16[2,256,128]{2,1,0:T(8,128)(2,1)S(1)}, u32[]{:S(2)}, u32[]{:S(2)}) collective-permute-start(bf16[2,256,128]{2,1,0:T(8,128)(2,1)S(1)} %slice.18), channel_id=1, source_target_pairs={{0,1},{1,2},{2,3},{3,0},{4,5},{5,6},{6,7},{7,4},{8,9},{9,10},{10,1... | collective-permute-start | bytes 393224 | tf_op jit(solution)/shard_map/ppermute | solution.py:533
  38.5 4.5 %collective-permute-done.2 = bf16[4,256,128]{2,1,0:T(8,128)(2,1)S(1)} collective-permute-done((bf16[4,256,128]{2,1,0:T(8,128)(2,1)}, bf16[4,256,128]{2,1,0:T(8,128)(2,1)S(1)}, u32[]{:S(2)}, u32[]{:S(2)}) %collective-permute-start.2) | collective-permute-done | bytes 262176 | tf_op jit(solution)/shard_map/ppermute | solution.py:533
  43.0 4.3 %collective-permute-start.5 = (bf16[2,4,256,128]{3,2,1,0:T(8,128)(2,1)S(1)}, bf16[2,4,256,128]{3,2,1,0:T(8,128)(2,1)S(1)}, u32[]{:S(2)}, u32[]{:S(2)}) collective-permute-start(bf16[2,4,256,128]{3,2,1,0:T(8,128)(2,1)S(1)} %pad_maximum_fusion.sides_ref), channel_id=1, source_target_pairs={{0,12},{1,13},{2,14},{3,15},{4,0},{5,1},{6,2},{7,3},{8,4},{9,5},{1... | collective-permute-start | bytes 1572872 | tf_op jit(solution)/shard_map/ppermute | solution.py:533
  47.4 3.0 %collective-permute-start.7 = (bf16[2,256,128]{2,1,0:T(8,128)(2,1)S(1)}, bf16[2,256,128]{2,1,0:T(8,128)(2,1)S(1)}, u32[]{:S(2)}, u32[]{:S(2)}) collective-permute-start(bf16[2,256,128]{2,1,0:T(8,128)(2,1)S(1)} %slice.19), channel_id=1, source_target_pairs={{0,3},{1,0},{2,1},{3,2},{4,7},{5,4},{6,5},{7,6},{8,11},{9,8},{10,9... | collective-permute-start | bytes 393224 | tf_op jit(solution)/shard_map/ppermute | solution.py:533
  52.4 4.4 %collective-permute-done.7 = bf16[2,256,128]{2,1,0:T(8,128)(2,1)S(1)} collective-permute-done((bf16[2,256,128]{2,1,0:T(8,128)(2,1)S(1)}, bf16[2,256,128]{2,1,0:T(8,128)(2,1)S(1)}, u32[]{:S(2)}, u32[]{:S(2)}) %collective-permute-start.7) | collective-permute-done | bytes 131104 | tf_op jit(solution)/shard_map/ppermute | solution.py:533
  56.8 2.5 %collective-permute-start.8 = (bf16[4,256,128]{2,1,0:T(8,128)(2,1)S(1)}, bf16[4,256,128]{2,1,0:T(8,128)(2,1)S(1)}, u32[]{:S(2)}, u32[]{:S(2)}) collective-permute-start(bf16[4,256,128]{2,1,0:T(8,128)(2,1)S(1)} %constant_dynamic-update-slice_fusion), channel_id=1, source_target_pairs={{0,12},{1,13},{2,14},{3,15},{4,0},{5,1},{6,2},{7,3},{8,4},{9,5},{1... | collective-permute-start | bytes 786440 | tf_op jit(solution)/shard_map/ppermute | solution.py:533
  59.3 2.8 %collective-permute-start = (bf16[4,256,128]{2,1,0:T(8,128)(2,1)S(1)}, bf16[4,256,128]{2,1,0:T(8,128)(2,1)S(1)}, u32[]{:S(2)}, u32[]{:S(2)}) collective-permute-start(bf16[4,256,128]{2,1,0:T(8,128)(2,1)S(1)} %copy-done.7), channel_id=1, source_target_pairs={{0,4},{1,5},{2,6},{3,7},{4,8},{5,9},{6,10},{7,11},{8,12},{9,13},{1... | collective-permute-start | bytes 786440 | tf_op jit(solution)/shard_map/ppermute | solution.py:533
  62.2 2.6 %collective-permute-done.8 = bf16[4,256,128]{2,1,0:T(8,128)(2,1)S(1)} collective-permute-done((bf16[4,256,128]{2,1,0:T(8,128)(2,1)S(1)}, bf16[4,256,128]{2,1,0:T(8,128)(2,1)S(1)}, u32[]{:S(2)}, u32[]{:S(2)}) %collective-permute-start.8) | collective-permute-done | bytes 262176 | tf_op jit(solution)/shard_map/ppermute | solution.py:533
  64.8 3.7 %collective-permute-start.9 = (bf16[2,4,256,128]{3,2,1,0:T(8,128)(2,1)S(1)}, bf16[2,4,256,128]{3,2,1,0:T(8,128)(2,1)}, u32[]{:S(2)}, u32[]{:S(2)}) collective-permute-start(bf16[2,4,256,128]{3,2,1,0:T(8,128)(2,1)S(1)} %pad_maximum_fusion.2), channel_id=1, source_target_pairs={{0,12},{1,13},{2,14},{3,15},{4,0},{5,1},{6,2},{7,3},{8,4},{9,5},{1... | collective-permute-start | bytes 1572872 | tf_op jit(solution)/shard_map/ppermute | solution.py:533
  68.5 2.5 %collective-permute-done = bf16[4,256,128]{2,1,0:T(8,128)(2,1)S(1)} collective-permute-done((bf16[4,256,128]{2,1,0:T(8,128)(2,1)S(1)}, bf16[4,256,128]{2,1,0:T(8,128)(2,1)S(1)}, u32[]{:S(2)}, u32[]{:S(2)}) %collective-permute-start) | collective-permute-done | bytes 262176 | tf_op jit(solution)/shard_map/ppermute | solution.py:533
  71.0 1.9 %collective-permute-start.4 = (bf16[2,4,256,128]{3,2,1,0:T(8,128)(2,1)S(1)}, bf16[2,4,256,128]{3,2,1,0:T(8,128)(2,1)}, u32[]{:S(2)}, u32[]{:S(2)}) collective-permute-start(bf16[2,4,256,128]{3,2,1,0:T(8,128)(2,1)S(1)} %pad_maximum_fusion.1), channel_id=1, source_target_pairs={{0,4},{1,5},{2,6},{3,7},{4,8},{5,9},{6,10},{7,11},{8,12},{9,13},{1... | collective-permute-start | bytes 1572872 | tf_op jit(solution)/shard_map/ppermute | solution.py:533
  73.0 4.6 %collective-permute-start.11 = (bf16[4,256,128]{2,1,0:T(8,128)(2,1)}, bf16[4,256,128]{2,1,0:T(8,128)(2,1)}, u32[]{:S(2)}, u32[]{:S(2)}) collective-permute-start(bf16[4,256,128]{2,1,0:T(8,128)(2,1)} %get-tuple-element.15), channel_id=1, source_target_pairs={{0,12},{1,13},{2,14},{3,15},{4,0},{5,1},{6,2},{7,3},{8,4},{9,5},{1... | collective-permute-start | bytes 786440 | tf_op jit(solution)/shard_map/ppermute | solution.py:533
  77.5 1.9 %collective-permute-start.10 = (bf16[4,256,128]{2,1,0:T(8,128)(2,1)S(1)}, bf16[4,256,128]{2,1,0:T(8,128)(2,1)}, u32[]{:S(2)}, u32[]{:S(2)}) collective-permute-start(bf16[4,256,128]{2,1,0:T(8,128)(2,1)S(1)} %constant_dynamic-update-slice_fusion), channel_id=1, source_target_pairs={{0,4},{1,5},{2,6},{3,7},{4,8},{5,9},{6,10},{7,11},{8,12},{9,13},{1... | collective-permute-start | bytes 786440 | tf_op jit(solution)/shard_map/ppermute | solution.py:533
  80.2 3.7 %collective-permute-done.11 = bf16[4,256,128]{2,1,0:T(8,128)(2,1)} collective-permute-done((bf16[4,256,128]{2,1,0:T(8,128)(2,1)}, bf16[4,256,128]{2,1,0:T(8,128)(2,1)}, u32[]{:S(2)}, u32[]{:S(2)}) %collective-permute-start.11) | collective-permute-done | bytes 262176 | tf_op jit(solution)/shard_map/ppermute | solution.py:533
  84.0 6.9 %collective-permute-done.10 = bf16[4,256,128]{2,1,0:T(8,128)(2,1)} collective-permute-done((bf16[4,256,128]{2,1,0:T(8,128)(2,1)S(1)}, bf16[4,256,128]{2,1,0:T(8,128)(2,1)}, u32[]{:S(2)}, u32[]{:S(2)}) %collective-permute-start.10) | collective-permute-done | bytes 262176 | tf_op jit(solution)/shard_map/ppermute | solution.py:533
  90.9 10.1 %near.1 = (bf16[4,3328,128]{2,1,0:T(8,128)(2,1)}, bf16[4,4,48,3328]{3,2,1,0:T(8,128)(2,1)}, bf16[4,4,128,256]{3,2,1,0:T(8,128)(2,1)}, f32[4,4,32,256]{3,2,1,0:T(8,128)}, f32[4,8,128]{2,1,0:T(8,128)}) custom-call(s32[32]{0:T(128)} %valid_ref.7, bf16[1,4,256,128]{3,2,1,0:T(8,128)(2,1)} %bitcast.22, bf16[2,4,256,128]{3,2,1,0:T(8,128)(2,1)} %copy-done, ...), custom_call_target="tpu_custom_call" | custom-call | tf_op jit(solution)/shard_map/near/pallas_call | solution.py:246
  101.0 5.8 %far.1 = (bf16[4,1280,128]{2,1,0:T(8,128)(2,1)}, bf16[4,4,48,1280]{3,2,1,0:T(8,128)(2,1)}, s32[1]{0:T(128)}) custom-call(s32[32]{0:T(128)} %valid_ref.7, bf16[2,4,256,128]{3,2,1,0:T(8,128)(2,1)} %collective-permute-done.4.low_ref, bf16[2,4,256,128]{3,2,1,0:T(8,128)(2,1)} %collective-permute-done.9.high_ref, bf16[128,512]{1,0:T(8,128)(2,1)} %weight_ref.3, ...), custom_call_target="tpu_custom_call" | custom-call | tf_op jit(solution)/shard_map/far/pallas_call | solution.py:280
  106.7 22.0 %attend.1 = bf16[4,256,128]{2,1,0:T(8,128)(2,1)} custom-call(s32[32]{0:T(128)} %valid_ref.7, s32[1]{0:T(128)} %get-tuple-element.18.safe, bf16[4,3328,128]{2,1,0:T(8,128)(2,1)} %get-tuple-element.19.near_keys, bf16[4,4,48,3328]{3,2,1,0:T(8,128)(2,1)} %get-tuple-element.20.near_values, bf16[4,1280,128]{2,1,0:T(8,128)(2,1)} %get-tuple-element.21.far_keys, ...), custom_call_target="tpu_custom_call" | custom-call | tf_op jit(solution)/shard_map/attend/pallas_call | solution.py:488
  (36 shorter events, 4.8 us)
Async XLA Ops:
  6.5 100.2 %all-gather.3.cloned.1.call-start = ((), (), s32[]{:S(2)}) async-start(), calls=%async_computation | async-start | bytes 8912896 | tf_op jit(solution)/shard_map/all_gather | solution.py:542
  8.7 50.5 %copy-start.7 = (bf16[4,256,128]{2,1,0:T(8,128)(2,1)S(1)}, bf16[4,256,128]{2,1,0:T(8,128)(2,1)}, u32[]{:S(2)}) copy-start(bf16[4,256,128]{2,1,0:T(8,128)(2,1)} %get-tuple-element.15) | copy-start | bytes 786436
  8.7 8.1 %collective-permute-start.12 = (bf16[4,128,256]{2,1,0:T(8,128)(2,1)}, bf16[4,128,256]{2,1,0:T(8,128)(2,1)S(1)}, u32[]{:S(2)}, u32[]{:S(2)}) collective-permute-start(bf16[4,128,256]{2,1,0:T(8,128)(2,1)} %get-tuple-element.24), channel_id=1, source_target_pairs={{0,256},{16,272},{32,288},{48,304},{64,320},{80,336},{96,352},{112... | collective-permute-start | bytes 786440 | tf_op jit(solution)/shard_map/ppermute | solution.py:539
  16.8 62.6 %copy-start.3 = (bf16[128,512]{1,0:T(8,128)(2,1)S(1)}, bf16[128,512]{1,0:T(8,128)(2,1)}, u32[]{:S(2)}) copy-start(bf16[128,512]{1,0:T(8,128)(2,1)} %weight_ref.3) | copy-start | bytes 393220
  18.7 12.9 %collective-permute-start.1 = (bf16[4,256,128]{2,1,0:T(8,128)(2,1)}, bf16[4,256,128]{2,1,0:T(8,128)(2,1)S(1)}, u32[]{:S(2)}, u32[]{:S(2)}) collective-permute-start(bf16[4,256,128]{2,1,0:T(8,128)(2,1)} %get-tuple-element.15), channel_id=1, source_target_pairs={{0,1},{1,2},{2,3},{3,0},{4,5},{5,6},{6,7},{7,4},{8,9},{9,10},{10,1... | collective-permute-start | bytes 786440 | tf_op jit(solution)/shard_map/ppermute | solution.py:533
  25.0 17.9 %collective-permute-start.2 = (bf16[4,256,128]{2,1,0:T(8,128)(2,1)}, bf16[4,256,128]{2,1,0:T(8,128)(2,1)S(1)}, u32[]{:S(2)}, u32[]{:S(2)}) collective-permute-start(bf16[4,256,128]{2,1,0:T(8,128)(2,1)} %get-tuple-element.15), channel_id=1, source_target_pairs={{0,3},{1,0},{2,1},{3,2},{4,7},{5,4},{6,5},{7,6},{8,11},{9,8},{10,9... | collective-permute-start | bytes 786440 | tf_op jit(solution)/shard_map/ppermute | solution.py:533
  31.6 20.8 %collective-permute-start.6 = (bf16[2,256,128]{2,1,0:T(8,128)(2,1)S(1)}, bf16[2,256,128]{2,1,0:T(8,128)(2,1)S(1)}, u32[]{:S(2)}, u32[]{:S(2)}) collective-permute-start(bf16[2,256,128]{2,1,0:T(8,128)(2,1)S(1)} %slice.18), channel_id=1, source_target_pairs={{0,1},{1,2},{2,3},{3,0},{4,5},{5,6},{6,7},{7,4},{8,9},{9,10},{10,1... | collective-permute-start | bytes 393224 | tf_op jit(solution)/shard_map/ppermute | solution.py:533
  43.0 47.8 %copy-start = (bf16[2,4,256,128]{3,2,1,0:T(8,128)(2,1)}, bf16[2,4,256,128]{3,2,1,0:T(8,128)(2,1)S(1)}, u32[]{:S(2)}) copy-start(bf16[2,4,256,128]{3,2,1,0:T(8,128)(2,1)S(1)} %pad_maximum_fusion.sides_ref) | copy-start | bytes 1572868
  43.0 19.1 %collective-permute-start.5 = (bf16[2,4,256,128]{3,2,1,0:T(8,128)(2,1)S(1)}, bf16[2,4,256,128]{3,2,1,0:T(8,128)(2,1)S(1)}, u32[]{:S(2)}, u32[]{:S(2)}) collective-permute-start(bf16[2,4,256,128]{3,2,1,0:T(8,128)(2,1)S(1)} %pad_maximum_fusion.sides_ref), channel_id=1, source_target_pairs={{0,12},{1,13},{2,14},{3,15},{4,0},{5,1},{6,2},{7,3},{8,4},{9,5},{1... | collective-permute-start | bytes 1572872 | tf_op jit(solution)/shard_map/ppermute | solution.py:533
  47.4 9.4 %collective-permute-start.7 = (bf16[2,256,128]{2,1,0:T(8,128)(2,1)S(1)}, bf16[2,256,128]{2,1,0:T(8,128)(2,1)S(1)}, u32[]{:S(2)}, u32[]{:S(2)}) collective-permute-start(bf16[2,256,128]{2,1,0:T(8,128)(2,1)S(1)} %slice.19), channel_id=1, source_target_pairs={{0,3},{1,0},{2,1},{3,2},{4,7},{5,4},{6,5},{7,6},{8,11},{9,8},{10,9... | collective-permute-start | bytes 393224 | tf_op jit(solution)/shard_map/ppermute | solution.py:533
  50.4 18.0 %collective-permute-start.3 = (bf16[2,4,256,128]{3,2,1,0:T(8,128)(2,1)S(1)}, bf16[2,4,256,128]{3,2,1,0:T(8,128)(2,1)S(1)}, u32[]{:S(2)}, u32[]{:S(2)}) collective-permute-start(bf16[2,4,256,128]{3,2,1,0:T(8,128)(2,1)S(1)} %pad_maximum_fusion.sides_ref), channel_id=1, source_target_pairs={{0,4},{1,5},{2,6},{3,7},{4,8},{5,9},{6,10},{7,11},{8,12},{9,13},{1... | collective-permute-start | bytes 1572872 | tf_op jit(solution)/shard_map/ppermute | solution.py:533
  56.8 34.0 %copy-start.6 = (bf16[4,256,128]{2,1,0:T(8,128)(2,1)}, bf16[4,256,128]{2,1,0:T(8,128)(2,1)S(1)}, u32[]{:S(2)}) copy-start(bf16[4,256,128]{2,1,0:T(8,128)(2,1)S(1)} %constant_dynamic-update-slice_fusion) | copy-start | bytes 786436
  56.8 7.9 %collective-permute-start.8 = (bf16[4,256,128]{2,1,0:T(8,128)(2,1)S(1)}, bf16[4,256,128]{2,1,0:T(8,128)(2,1)S(1)}, u32[]{:S(2)}, u32[]{:S(2)}) collective-permute-start(bf16[4,256,128]{2,1,0:T(8,128)(2,1)S(1)} %constant_dynamic-update-slice_fusion), channel_id=1, source_target_pairs={{0,12},{1,13},{2,14},{3,15},{4,0},{5,1},{6,2},{7,3},{8,4},{9,5},{1... | collective-permute-start | bytes 786440 | tf_op jit(solution)/shard_map/ppermute | solution.py:533
  59.3 11.7 %collective-permute-start = (bf16[4,256,128]{2,1,0:T(8,128)(2,1)S(1)}, bf16[4,256,128]{2,1,0:T(8,128)(2,1)S(1)}, u32[]{:S(2)}, u32[]{:S(2)}) collective-permute-start(bf16[4,256,128]{2,1,0:T(8,128)(2,1)S(1)} %copy-done.7), channel_id=1, source_target_pairs={{0,4},{1,5},{2,6},{3,7},{4,8},{5,9},{6,10},{7,11},{8,12},{9,13},{1... | collective-permute-start | bytes 786440 | tf_op jit(solution)/shard_map/ppermute | solution.py:533
  62.1 28.7 %copy-start.1 = (bf16[2,4,256,128]{3,2,1,0:T(8,128)(2,1)}, bf16[2,4,256,128]{3,2,1,0:T(8,128)(2,1)S(1)}, u32[]{:S(2)}) copy-start(bf16[2,4,256,128]{3,2,1,0:T(8,128)(2,1)S(1)} %collective-permute-done.5.right_sides_ref) | copy-start | bytes 1572868
  64.7 26.1 %copy-start.4 = (bf16[4,256,128]{2,1,0:T(8,128)(2,1)}, bf16[4,256,128]{2,1,0:T(8,128)(2,1)S(1)}, u32[]{:S(2)}) copy-start(bf16[4,256,128]{2,1,0:T(8,128)(2,1)S(1)} %collective-permute-done.8) | copy-start | bytes 786436
  64.8 36.1 %collective-permute-start.9 = (bf16[2,4,256,128]{3,2,1,0:T(8,128)(2,1)S(1)}, bf16[2,4,256,128]{3,2,1,0:T(8,128)(2,1)}, u32[]{:S(2)}, u32[]{:S(2)}) collective-permute-start(bf16[2,4,256,128]{3,2,1,0:T(8,128)(2,1)S(1)} %pad_maximum_fusion.2), channel_id=1, source_target_pairs={{0,12},{1,13},{2,14},{3,15},{4,0},{5,1},{6,2},{7,3},{8,4},{9,5},{1... | collective-permute-start | bytes 1572872 | tf_op jit(solution)/shard_map/ppermute | solution.py:533
  68.5 22.3 %copy-start.2 = (bf16[2,4,256,128]{3,2,1,0:T(8,128)(2,1)}, bf16[2,4,256,128]{3,2,1,0:T(8,128)(2,1)S(1)}, u32[]{:S(2)}) copy-start(bf16[2,4,256,128]{3,2,1,0:T(8,128)(2,1)S(1)} %collective-permute-done.3.left_sides_ref) | copy-start | bytes 1572868
  71.0 19.9 %copy-start.5 = (bf16[4,256,128]{2,1,0:T(8,128)(2,1)}, bf16[4,256,128]{2,1,0:T(8,128)(2,1)S(1)}, u32[]{:S(2)}) copy-start(bf16[4,256,128]{2,1,0:T(8,128)(2,1)S(1)} %collective-permute-done) | copy-start | bytes 786436
  71.0 29.9 %collective-permute-start.4 = (bf16[2,4,256,128]{3,2,1,0:T(8,128)(2,1)S(1)}, bf16[2,4,256,128]{3,2,1,0:T(8,128)(2,1)}, u32[]{:S(2)}, u32[]{:S(2)}) collective-permute-start(bf16[2,4,256,128]{3,2,1,0:T(8,128)(2,1)S(1)} %pad_maximum_fusion.1), channel_id=1, source_target_pairs={{0,4},{1,5},{2,6},{3,7},{4,8},{5,9},{6,10},{7,11},{8,12},{9,13},{1... | collective-permute-start | bytes 1572872 | tf_op jit(solution)/shard_map/ppermute | solution.py:533
  73.0 11.0 %collective-permute-start.11 = (bf16[4,256,128]{2,1,0:T(8,128)(2,1)}, bf16[4,256,128]{2,1,0:T(8,128)(2,1)}, u32[]{:S(2)}, u32[]{:S(2)}) collective-permute-start(bf16[4,256,128]{2,1,0:T(8,128)(2,1)} %get-tuple-element.15), channel_id=1, source_target_pairs={{0,12},{1,13},{2,14},{3,15},{4,0},{5,1},{6,2},{7,3},{8,4},{9,5},{1... | collective-permute-start | bytes 786440 | tf_op jit(solution)/shard_map/ppermute | solution.py:533
  77.5 13.3 %collective-permute-start.10 = (bf16[4,256,128]{2,1,0:T(8,128)(2,1)S(1)}, bf16[4,256,128]{2,1,0:T(8,128)(2,1)}, u32[]{:S(2)}, u32[]{:S(2)}) collective-permute-start(bf16[4,256,128]{2,1,0:T(8,128)(2,1)S(1)} %constant_dynamic-update-slice_fusion), channel_id=1, source_target_pairs={{0,4},{1,5},{2,6},{3,7},{4,8},{5,9},{6,10},{7,11},{8,12},{9,13},{1... | collective-permute-start | bytes 786440 | tf_op jit(solution)/shard_map/ppermute | solution.py:533
Sparse Core Ops, SparseCore 0:
  18.8 67.3 all-gather.2

commit v6 on v4

--- a/solution.py
+++ b/solution.py
@@ -314,7 +314,7 @@
                 top = jnp.maximum(top, piece[group : group + GROUP])
             return top
 
-        top = lax.fori_loop(places[0], places[-1] + 1, move, top)
+        top = lax.fori_loop(places[0], places[-1] + 1, move, top, unroll=4)
         bias[pl.ds(pl.multiple_of(base + total, GROUP), BLOCK), :] = jnp.full(
             (BLOCK, cols), MASKED, jnp.bfloat16
         )
@@ -497,7 +497,10 @@
     right_own = shift(normed, -1, 0)
     above = shift(normed, 0, 1)
     below = shift(normed, 0, -1)
-    across = shift(normed, 0, 2)
+    half = normed.shape[0] // 2
+    across_low = shift(above[:half], 0, 1)
+    across_high = shift(below[half:], 0, -1)
+    across = jnp.concatenate([across_low, across_high])
     sides = jnp.stack([above, below])
     left_sides = shift(sides, 1, 0)
     right_sides = shift(sides, -1, 0)

time: 144 us -> 135 us (0.938)
  the two profiles are of different devices: /device:TPU:208 before, /device:TPU:448 now
where the time goes in v6:
time: 135 us; the launch traced here: 134 us
  starting transfers between devices  46.7 us (35%)
  Pallas kernels  34.9 us (26%)
  waiting for transfers between devices  33.7 us (25%)
  between operations  13.7 us (10%)
  other arithmetic  3.68 us (3%)
  local copies, waits for them, and re-layouts  1.82 us (1%)
    ppermute x12, starting transfers between devices, shift(): return lax.ppermute(value, 'cols', pairs)  43.2 us
    ppermute x12, waiting for transfers between devices, shift(): return lax.ppermute(value, 'cols', pairs)  27 us
    pallas_call x1, Pallas kernels, attend(): pl.pallas_call(attend_kernel, grid=(heads,), in_specs=[SMEM, pl.BlockSpec...  22.5 us
    pallas_call x1, Pallas kernels, project_near(): pl.pallas_call(near_kernel, grid=(rows,), in_specs=[SMEM, *(piece_spec(pi...  10.1 us
    ppermute x1, waiting for transfers between devices, gather_bias(): lax.ppermute(bias_t, 'rows', [(r, (r + half) % count) for r in range(coun...  6.66 us
    ppermute x1, starting transfers between devices, gather_bias(): lax.ppermute(bias_t, 'rows', [(r, (r + half) % count) for r in range(coun...  3.47 us
  transfers between devices with their start and end apart: 14, of which 8 were waited for; matrix products, arithmetic and copies ran while one was open for 2% of the time, Pallas kernels for 8%

profile of v6, /device:TPU:448, one launch (start us, length us, event | category | flops | bytes accessed | tf_op | source)
XLA Modules:
  0.0 134.4 jit_solution(11134996701102918028)
XLA Ops:
  6.5 2.2 %prep.1 = (bf16[4,256,128]{2,1,0:T(8,128)(2,1)}, bf16[4,128,256]{2,1,0:T(8,128)(2,1)}) custom-call(s32[32]{0:T(128)} %valid_ref.5, bf16[4,256,128]{2,1,0:T(8,128)(2,1)} %pair_ref.1, bf16[4,256,128]{2,1,0:T(8,128)(2,1)} %bias_ref.1), custom_call_target="tpu_custom_call" | custom-call | tf_op jit(solution)/shard_map/prep/pallas_call | solution.py:45
  8.8 3.5 %collective-permute-start.12 = (bf16[4,128,256]{2,1,0:T(8,128)(2,1)}, bf16[4,128,256]{2,1,0:T(8,128)(2,1)S(1)}, u32[]{:S(2)}, u32[]{:S(2)}) collective-permute-start(bf16[4,128,256]{2,1,0:T(8,128)(2,1)} %get-tuple-element.18), channel_id=1, source_target_pairs={{0,256},{16,272},{32,288},{48,304},{64,320},{80,336},{96,352},{112... | collective-permute-start | bytes 786440 | tf_op jit(solution)/shard_map/ppermute | solution.py:467
  12.2 6.7 %collective-permute-done.12 = bf16[4,128,256]{2,1,0:T(8,128)(2,1)S(1)} collective-permute-done((bf16[4,128,256]{2,1,0:T(8,128)(2,1)}, bf16[4,128,256]{2,1,0:T(8,128)(2,1)S(1)}, u32[]{:S(2)}, u32[]{:S(2)}) %collective-permute-start.12) | collective-permute-done | bytes 262176 | tf_op jit(solution)/shard_map/ppermute | solution.py:467
  18.9 1.8 %pad_maximum_fusion.3 = bf16[2,4,128,256]{3,2,1,0:T(8,128)(2,1)} fusion(bf16[1,4,128,256]{3,2,1,0:T(8,128)(2,1)S(1)} %bitcast.23, bf16[1,4,128,256]{3,2,1,0:T(8,128)(2,1)} %bitcast.22), kind=kLoop, calls=%fused_computation.3 | loop fusion | flops 262144 | bytes 1048576 | tf_op jit(solution)/shard_map/stack | solution.py:468
  20.7 4.5 %collective-permute-start = (bf16[4,256,128]{2,1,0:T(8,128)(2,1)}, bf16[4,256,128]{2,1,0:T(8,128)(2,1)S(1)}, u32[]{:S(2)}, u32[]{:S(2)}) collective-permute-start(bf16[4,256,128]{2,1,0:T(8,128)(2,1)} %get-tuple-element.12), channel_id=1, source_target_pairs={{0,1},{1,2},{2,3},{3,0},{4,5},{5,6},{6,7},{7,4},{8,9},{9,10},{10,1... | collective-permute-start | bytes 786440 | tf_op jit(solution)/shard_map/ppermute | solution.py:461
  25.2 3.6 %collective-permute-start.1 = (bf16[4,256,128]{2,1,0:T(8,128)(2,1)}, bf16[4,256,128]{2,1,0:T(8,128)(2,1)S(1)}, u32[]{:S(2)}, u32[]{:S(2)}) collective-permute-start(bf16[4,256,128]{2,1,0:T(8,128)(2,1)} %get-tuple-element.12), channel_id=1, source_target_pairs={{0,3},{1,0},{2,1},{3,2},{4,7},{5,4},{6,5},{7,6},{8,11},{9,8},{10,9... | collective-permute-start | bytes 786440 | tf_op jit(solution)/shard_map/ppermute | solution.py:461
  28.8 6.7 %collective-permute-done = bf16[4,256,128]{2,1,0:T(8,128)(2,1)S(1)} collective-permute-done((bf16[4,256,128]{2,1,0:T(8,128)(2,1)}, bf16[4,256,128]{2,1,0:T(8,128)(2,1)S(1)}, u32[]{:S(2)}, u32[]{:S(2)}) %collective-permute-start) | collective-permute-done | bytes 262176 | tf_op jit(solution)/shard_map/ppermute | solution.py:461
  35.5 5.9 %collective-permute-start.2 = (bf16[2,256,128]{2,1,0:T(8,128)(2,1)S(1)}, bf16[2,256,128]{2,1,0:T(8,128)(2,1)S(1)}, u32[]{:S(2)}, u32[]{:S(2)}) collective-permute-start(bf16[2,256,128]{2,1,0:T(8,128)(2,1)S(1)} %slice.16), channel_id=1, source_target_pairs={{0,1},{1,2},{2,3},{3,0},{4,5},{5,6},{6,7},{7,4},{8,9},{9,10},{10,1... | collective-permute-start | bytes 393224 | tf_op jit(solution)/shard_map/ppermute | solution.py:461
  42.0 4.7 %collective-permute-start.8 = (bf16[2,4,256,128]{3,2,1,0:T(8,128)(2,1)S(1)}, bf16[2,4,256,128]{3,2,1,0:T(8,128)(2,1)S(1)}, u32[]{:S(2)}, u32[]{:S(2)}) collective-permute-start(bf16[2,4,256,128]{3,2,1,0:T(8,128)(2,1)S(1)} %pad_maximum_fusion.sides_ref), channel_id=1, source_target_pairs={{0,12},{1,13},{2,14},{3,15},{4,0},{5,1},{6,2},{7,3},{8,4},{9,5},{1... | collective-permute-start | bytes 1572872 | tf_op jit(solution)/shard_map/ppermute | solution.py:461
  46.7 3.9 %collective-permute-start.3 = (bf16[2,256,128]{2,1,0:T(8,128)(2,1)S(1)}, bf16[2,256,128]{2,1,0:T(8,128)(2,1)S(1)}, u32[]{:S(2)}, u32[]{:S(2)}) collective-permute-start(bf16[2,256,128]{2,1,0:T(8,128)(2,1)S(1)} %slice.17), channel_id=1, source_target_pairs={{0,3},{1,0},{2,1},{3,2},{4,7},{5,4},{6,5},{7,6},{8,11},{9,8},{10,9... | collective-permute-start | bytes 393224 | tf_op jit(solution)/shard_map/ppermute | solution.py:461
  50.6 1.9 %collective-permute-start.5 = (bf16[2,4,256,128]{3,2,1,0:T(8,128)(2,1)S(1)}, bf16[2,4,256,128]{3,2,1,0:T(8,128)(2,1)S(1)}, u32[]{:S(2)}, u32[]{:S(2)}) collective-permute-start(bf16[2,4,256,128]{3,2,1,0:T(8,128)(2,1)S(1)} %pad_maximum_fusion.sides_ref), channel_id=1, source_target_pairs={{0,4},{1,5},{2,6},{3,7},{4,8},{5,9},{6,10},{7,11},{8,12},{9,13},{1... | collective-permute-start | bytes 1572872 | tf_op jit(solution)/shard_map/ppermute | solution.py:461
  52.6 4.6 %collective-permute-done.3 = bf16[2,256,128]{2,1,0:T(8,128)(2,1)S(1)} collective-permute-done((bf16[2,256,128]{2,1,0:T(8,128)(2,1)S(1)}, bf16[2,256,128]{2,1,0:T(8,128)(2,1)S(1)}, u32[]{:S(2)}, u32[]{:S(2)}) %collective-permute-start.3) | collective-permute-done | bytes 131104 | tf_op jit(solution)/shard_map/ppermute | solution.py:461
  57.2 2.7 %collective-permute-start.9 = (bf16[4,256,128]{2,1,0:T(8,128)(2,1)S(1)}, bf16[4,256,128]{2,1,0:T(8,128)(2,1)S(1)}, u32[]{:S(2)}, u32[]{:S(2)}) collective-permute-start(bf16[4,256,128]{2,1,0:T(8,128)(2,1)S(1)} %constant_dynamic-update-slice_fusion), channel_id=1, source_target_pairs={{0,12},{1,13},{2,14},{3,15},{4,0},{5,1},{6,2},{7,3},{8,4},{9,5},{1... | collective-permute-start | bytes 786440 | tf_op jit(solution)/shard_map/ppermute | solution.py:461
  59.9 3.1 %collective-permute-start.4 = (bf16[4,256,128]{2,1,0:T(8,128)(2,1)}, bf16[4,256,128]{2,1,0:T(8,128)(2,1)S(1)}, u32[]{:S(2)}, u32[]{:S(2)}) collective-permute-start(bf16[4,256,128]{2,1,0:T(8,128)(2,1)} %get-tuple-element.12), channel_id=1, source_target_pairs={{0,4},{1,5},{2,6},{3,7},{4,8},{5,9},{6,10},{7,11},{8,12},{9,13},{1... | collective-permute-start | bytes 786440 | tf_op jit(solution)/shard_map/ppermute | solution.py:461
  63.1 3.0 %collective-permute-done.9 = bf16[4,256,128]{2,1,0:T(8,128)(2,1)S(1)} collective-permute-done((bf16[4,256,128]{2,1,0:T(8,128)(2,1)S(1)}, bf16[4,256,128]{2,1,0:T(8,128)(2,1)S(1)}, u32[]{:S(2)}, u32[]{:S(2)}) %collective-permute-start.9) | collective-permute-done | bytes 262176 | tf_op jit(solution)/shard_map/ppermute | solution.py:461
  66.0 0.9 pad_maximum_fusion.2
  67.0 3.9 %collective-permute-start.11 = (bf16[2,4,256,128]{3,2,1,0:T(8,128)(2,1)}, bf16[2,4,256,128]{3,2,1,0:T(8,128)(2,1)S(1)}, u32[]{:S(2)}, u32[]{:S(2)}) collective-permute-start(bf16[2,4,256,128]{3,2,1,0:T(8,128)(2,1)} %pad_maximum_fusion.2), channel_id=1, source_target_pairs={{0,12},{1,13},{2,14},{3,15},{4,0},{5,1},{6,2},{7,3},{8,4},{9,5},{1... | collective-permute-start | bytes 1572872 | tf_op jit(solution)/shard_map/ppermute | solution.py:461
  72.8 1.9 %collective-permute-start.10 = (bf16[2,4,256,128]{3,2,1,0:T(8,128)(2,1)}, bf16[2,4,256,128]{3,2,1,0:T(8,128)(2,1)S(1)}, u32[]{:S(2)}, u32[]{:S(2)}) collective-permute-start(bf16[2,4,256,128]{3,2,1,0:T(8,128)(2,1)} %pad_maximum_fusion.1), channel_id=1, source_target_pairs={{0,4},{1,5},{2,6},{3,7},{4,8},{5,9},{6,10},{7,11},{8,12},{9,13},{1... | collective-permute-start | bytes 1572872 | tf_op jit(solution)/shard_map/ppermute | solution.py:461
  74.7 5.1 %collective-permute-start.7 = (bf16[4,256,128]{2,1,0:T(8,128)(2,1)}, bf16[4,256,128]{2,1,0:T(8,128)(2,1)}, u32[]{:S(2)}, u32[]{:S(2)}) collective-permute-start(bf16[4,256,128]{2,1,0:T(8,128)(2,1)} %get-tuple-element.12), channel_id=1, source_target_pairs={{0,12},{1,13},{2,14},{3,15},{4,0},{5,1},{6,2},{7,3},{8,4},{9,5},{1... | collective-permute-start | bytes 786440 | tf_op jit(solution)/shard_map/ppermute | solution.py:461
  79.8 1.9 %collective-permute-start.6 = (bf16[4,256,128]{2,1,0:T(8,128)(2,1)S(1)}, bf16[4,256,128]{2,1,0:T(8,128)(2,1)}, u32[]{:S(2)}, u32[]{:S(2)}) collective-permute-start(bf16[4,256,128]{2,1,0:T(8,128)(2,1)S(1)} %constant_dynamic-update-slice_fusion), channel_id=1, source_target_pairs={{0,4},{1,5},{2,6},{3,7},{4,8},{5,9},{6,10},{7,11},{8,12},{9,13},{1... | collective-permute-start | bytes 786440 | tf_op jit(solution)/shard_map/ppermute | solution.py:461
  82.5 4.1 %collective-permute-done.7 = bf16[4,256,128]{2,1,0:T(8,128)(2,1)} collective-permute-done((bf16[4,256,128]{2,1,0:T(8,128)(2,1)}, bf16[4,256,128]{2,1,0:T(8,128)(2,1)}, u32[]{:S(2)}, u32[]{:S(2)}) %collective-permute-start.7) | collective-permute-done | bytes 262176 | tf_op jit(solution)/shard_map/ppermute | solution.py:461
  86.6 7.2 %collective-permute-done.6 = bf16[4,256,128]{2,1,0:T(8,128)(2,1)} collective-permute-done((bf16[4,256,128]{2,1,0:T(8,128)(2,1)S(1)}, bf16[4,256,128]{2,1,0:T(8,128)(2,1)}, u32[]{:S(2)}, u32[]{:S(2)}) %collective-permute-start.6) | collective-permute-done | bytes 262176 | tf_op jit(solution)/shard_map/ppermute | solution.py:461
  93.9 10.1 %near.1 = (bf16[4,3328,128]{2,1,0:T(8,128)(2,1)}, bf16[4,4,48,3328]{3,2,1,0:T(8,128)(2,1)}, bf16[4,4,128,256]{3,2,1,0:T(8,128)(2,1)}, f32[4,4,32,256]{3,2,1,0:T(8,128)}, f32[4,8,128]{2,1,0:T(8,128)}) custom-call(s32[32]{0:T(128)} %valid_ref.5, bf16[1,4,256,128]{3,2,1,0:T(8,128)(2,1)} %bitcast.own_ref, bf16[2,4,256,128]{3,2,1,0:T(8,128)(2,1)} %copy-done, ...), custom_call_target="tpu_custom_call" | custom-call | tf_op jit(solution)/shard_map/near/pallas_call | solution.py:198
  105.1 22.5 %attend.1 = bf16[4,256,128]{2,1,0:T(8,128)(2,1)} custom-call(s32[32]{0:T(128)} %valid_ref.5, bf16[4,3328,128]{2,1,0:T(8,128)(2,1)} %get-tuple-element.13.keys_hbm, bf16[4,4,48,3328]{3,2,1,0:T(8,128)(2,1)} %get-tuple-element.14.values_hbm, bf16[2,4,256,128]{3,2,1,0:T(8,128)(2,1)} %copy-done.8, bf16[2,4,256,128]{3,2,1,0:T(8,128)(2,1)} %copy-done.7, ...), custom_call_target="tpu_custom_call" | custom-call | tf_op jit(solution)/shard_map/attend/pallas_call | solution.py:409
  (37 shorter events, 4.2 us)
Async XLA Ops:
  6.5 75.2 %copy-start.1 = (bf16[128,512]{1,0:T(8,128)(2,1)S(1)}, bf16[128,512]{1,0:T(8,128)(2,1)}, u32[]{:S(2)}) copy-start(bf16[128,512]{1,0:T(8,128)(2,1)} %weight_ref.3) | copy-start | bytes 393220
  6.5 97.6 %all-gather.3.cloned.1.call-start = ((), (), s32[]{:S(2)}) async-start(), calls=%async_computation | async-start | bytes 8912896 | tf_op jit(solution)/shard_map/all_gather | solution.py:470
  8.8 10.1 %collective-permute-start.12 = (bf16[4,128,256]{2,1,0:T(8,128)(2,1)}, bf16[4,128,256]{2,1,0:T(8,128)(2,1)S(1)}, u32[]{:S(2)}, u32[]{:S(2)}) collective-permute-start(bf16[4,128,256]{2,1,0:T(8,128)(2,1)} %get-tuple-element.18), channel_id=1, source_target_pairs={{0,256},{16,272},{32,288},{48,304},{64,320},{80,336},{96,352},{112... | collective-permute-start | bytes 786440 | tf_op jit(solution)/shard_map/ppermute | solution.py:467
  20.7 14.8 %collective-permute-start = (bf16[4,256,128]{2,1,0:T(8,128)(2,1)}, bf16[4,256,128]{2,1,0:T(8,128)(2,1)S(1)}, u32[]{:S(2)}, u32[]{:S(2)}) collective-permute-start(bf16[4,256,128]{2,1,0:T(8,128)(2,1)} %get-tuple-element.12), channel_id=1, source_target_pairs={{0,1},{1,2},{2,3},{3,0},{4,5},{5,6},{6,7},{7,4},{8,9},{9,10},{10,1... | collective-permute-start | bytes 786440 | tf_op jit(solution)/shard_map/ppermute | solution.py:461
  25.2 16.7 %collective-permute-start.1 = (bf16[4,256,128]{2,1,0:T(8,128)(2,1)}, bf16[4,256,128]{2,1,0:T(8,128)(2,1)S(1)}, u32[]{:S(2)}, u32[]{:S(2)}) collective-permute-start(bf16[4,256,128]{2,1,0:T(8,128)(2,1)} %get-tuple-element.12), channel_id=1, source_target_pairs={{0,3},{1,0},{2,1},{3,2},{4,7},{5,4},{6,5},{7,6},{8,11},{9,8},{10,9... | collective-permute-start | bytes 786440 | tf_op jit(solution)/shard_map/ppermute | solution.py:461
  35.5 17.0 %collective-permute-start.2 = (bf16[2,256,128]{2,1,0:T(8,128)(2,1)S(1)}, bf16[2,256,128]{2,1,0:T(8,128)(2,1)S(1)}, u32[]{:S(2)}, u32[]{:S(2)}) collective-permute-start(bf16[2,256,128]{2,1,0:T(8,128)(2,1)S(1)} %slice.16), channel_id=1, source_target_pairs={{0,1},{1,2},{2,3},{3,0},{4,5},{5,6},{6,7},{7,4},{8,9},{9,10},{10,1... | collective-permute-start | bytes 393224 | tf_op jit(solution)/shard_map/ppermute | solution.py:461
  42.0 51.9 %copy-start = (bf16[2,4,256,128]{3,2,1,0:T(8,128)(2,1)}, bf16[2,4,256,128]{3,2,1,0:T(8,128)(2,1)S(1)}, u32[]{:S(2)}) copy-start(bf16[2,4,256,128]{3,2,1,0:T(8,128)(2,1)S(1)} %pad_maximum_fusion.sides_ref) | copy-start | bytes 1572868
  42.0 21.0 %collective-permute-start.8 = (bf16[2,4,256,128]{3,2,1,0:T(8,128)(2,1)S(1)}, bf16[2,4,256,128]{3,2,1,0:T(8,128)(2,1)S(1)}, u32[]{:S(2)}, u32[]{:S(2)}) collective-permute-start(bf16[2,4,256,128]{3,2,1,0:T(8,128)(2,1)S(1)} %pad_maximum_fusion.sides_ref), channel_id=1, source_target_pairs={{0,12},{1,13},{2,14},{3,15},{4,0},{5,1},{6,2},{7,3},{8,4},{9,5},{1... | collective-permute-start | bytes 1572872 | tf_op jit(solution)/shard_map/ppermute | solution.py:461
  46.7 10.4 %collective-permute-start.3 = (bf16[2,256,128]{2,1,0:T(8,128)(2,1)S(1)}, bf16[2,256,128]{2,1,0:T(8,128)(2,1)S(1)}, u32[]{:S(2)}, u32[]{:S(2)}) collective-permute-start(bf16[2,256,128]{2,1,0:T(8,128)(2,1)S(1)} %slice.17), channel_id=1, source_target_pairs={{0,3},{1,0},{2,1},{3,2},{4,7},{5,4},{6,5},{7,6},{8,11},{9,8},{10,9... | collective-permute-start | bytes 393224 | tf_op jit(solution)/shard_map/ppermute | solution.py:461
  50.6 20.3 %collective-permute-start.5 = (bf16[2,4,256,128]{3,2,1,0:T(8,128)(2,1)S(1)}, bf16[2,4,256,128]{3,2,1,0:T(8,128)(2,1)S(1)}, u32[]{:S(2)}, u32[]{:S(2)}) collective-permute-start(bf16[2,4,256,128]{3,2,1,0:T(8,128)(2,1)S(1)} %pad_maximum_fusion.sides_ref), channel_id=1, source_target_pairs={{0,4},{1,5},{2,6},{3,7},{4,8},{5,9},{6,10},{7,11},{8,12},{9,13},{1... | collective-permute-start | bytes 1572872 | tf_op jit(solution)/shard_map/ppermute | solution.py:461
  57.1 36.7 %copy-start.6 = (bf16[4,256,128]{2,1,0:T(8,128)(2,1)}, bf16[4,256,128]{2,1,0:T(8,128)(2,1)S(1)}, u32[]{:S(2)}) copy-start(bf16[4,256,128]{2,1,0:T(8,128)(2,1)S(1)} %constant_dynamic-update-slice_fusion) | copy-start | bytes 786436
  57.2 8.9 %collective-permute-start.9 = (bf16[4,256,128]{2,1,0:T(8,128)(2,1)S(1)}, bf16[4,256,128]{2,1,0:T(8,128)(2,1)S(1)}, u32[]{:S(2)}, u32[]{:S(2)}) collective-permute-start(bf16[4,256,128]{2,1,0:T(8,128)(2,1)S(1)} %constant_dynamic-update-slice_fusion), channel_id=1, source_target_pairs={{0,12},{1,13},{2,14},{3,15},{4,0},{5,1},{6,2},{7,3},{8,4},{9,5},{1... | collective-permute-start | bytes 786440 | tf_op jit(solution)/shard_map/ppermute | solution.py:461
  59.9 12.0 %collective-permute-start.4 = (bf16[4,256,128]{2,1,0:T(8,128)(2,1)}, bf16[4,256,128]{2,1,0:T(8,128)(2,1)S(1)}, u32[]{:S(2)}, u32[]{:S(2)}) collective-permute-start(bf16[4,256,128]{2,1,0:T(8,128)(2,1)} %get-tuple-element.12), channel_id=1, source_target_pairs={{0,4},{1,5},{2,6},{3,7},{4,8},{5,9},{6,10},{7,11},{8,12},{9,13},{1... | collective-permute-start | bytes 786440 | tf_op jit(solution)/shard_map/ppermute | solution.py:461
  63.0 30.9 %copy-start.2 = (bf16[2,4,256,128]{3,2,1,0:T(8,128)(2,1)}, bf16[2,4,256,128]{3,2,1,0:T(8,128)(2,1)S(1)}, u32[]{:S(2)}) copy-start(bf16[2,4,256,128]{3,2,1,0:T(8,128)(2,1)S(1)} %collective-permute-done.8.right_sides_ref) | copy-start | bytes 1572868
  66.0 27.9 %copy-start.4 = (bf16[4,256,128]{2,1,0:T(8,128)(2,1)}, bf16[4,256,128]{2,1,0:T(8,128)(2,1)S(1)}, u32[]{:S(2)}) copy-start(bf16[4,256,128]{2,1,0:T(8,128)(2,1)S(1)} %collective-permute-done.9) | copy-start | bytes 786436
  67.0 37.1 %collective-permute-start.11 = (bf16[2,4,256,128]{3,2,1,0:T(8,128)(2,1)}, bf16[2,4,256,128]{3,2,1,0:T(8,128)(2,1)S(1)}, u32[]{:S(2)}, u32[]{:S(2)}) collective-permute-start(bf16[2,4,256,128]{3,2,1,0:T(8,128)(2,1)} %pad_maximum_fusion.2), channel_id=1, source_target_pairs={{0,12},{1,13},{2,14},{3,15},{4,0},{5,1},{6,2},{7,3},{8,4},{9,5},{1... | collective-permute-start | bytes 1572872 | tf_op jit(solution)/shard_map/ppermute | solution.py:461
  70.9 23.0 %copy-start.3 = (bf16[2,4,256,128]{3,2,1,0:T(8,128)(2,1)}, bf16[2,4,256,128]{3,2,1,0:T(8,128)(2,1)S(1)}, u32[]{:S(2)}) copy-start(bf16[2,4,256,128]{3,2,1,0:T(8,128)(2,1)S(1)} %collective-permute-done.5.left_sides_ref) | copy-start | bytes 1572868
  71.9 22.0 %copy-start.5 = (bf16[4,256,128]{2,1,0:T(8,128)(2,1)}, bf16[4,256,128]{2,1,0:T(8,128)(2,1)S(1)}, u32[]{:S(2)}) copy-start(bf16[4,256,128]{2,1,0:T(8,128)(2,1)S(1)} %collective-permute-done.4) | copy-start | bytes 786436
  72.8 31.3 %collective-permute-start.10 = (bf16[2,4,256,128]{3,2,1,0:T(8,128)(2,1)}, bf16[2,4,256,128]{3,2,1,0:T(8,128)(2,1)S(1)}, u32[]{:S(2)}, u32[]{:S(2)}) collective-permute-start(bf16[2,4,256,128]{3,2,1,0:T(8,128)(2,1)} %pad_maximum_fusion.1), channel_id=1, source_target_pairs={{0,4},{1,5},{2,6},{3,7},{4,8},{5,9},{6,10},{7,11},{8,12},{9,13},{1... | collective-permute-start | bytes 1572872 | tf_op jit(solution)/shard_map/ppermute | solution.py:461
  74.7 11.9 %collective-permute-start.7 = (bf16[4,256,128]{2,1,0:T(8,128)(2,1)}, bf16[4,256,128]{2,1,0:T(8,128)(2,1)}, u32[]{:S(2)}, u32[]{:S(2)}) collective-permute-start(bf16[4,256,128]{2,1,0:T(8,128)(2,1)} %get-tuple-element.12), channel_id=1, source_target_pairs={{0,12},{1,13},{2,14},{3,15},{4,0},{5,1},{6,2},{7,3},{8,4},{9,5},{1... | collective-permute-start | bytes 786440 | tf_op jit(solution)/shard_map/ppermute | solution.py:461
  79.8 14.0 %collective-permute-start.6 = (bf16[4,256,128]{2,1,0:T(8,128)(2,1)S(1)}, bf16[4,256,128]{2,1,0:T(8,128)(2,1)}, u32[]{:S(2)}, u32[]{:S(2)}) collective-permute-start(bf16[4,256,128]{2,1,0:T(8,128)(2,1)S(1)} %constant_dynamic-update-slice_fusion), channel_id=1, source_target_pairs={{0,4},{1,5},{2,6},{3,7},{4,8},{5,9},{6,10},{7,11},{8,12},{9,13},{1... | collective-permute-start | bytes 786440 | tf_op jit(solution)/shard_map/ppermute | solution.py:461
  104.1 0.8 copy-start.7
  104.1 1.0 copy-start.8
Sparse Core Ops, SparseCore 0:
  20.8 56.1 all-gather.2

commit v7 on v6

--- a/solution.py
+++ b/solution.py
@@ -333,19 +333,28 @@
             parts = [place_of(first + n) for n in range(count)]
             for n, place in enumerate(parts):
                 shifted[n] = (bias[place, :].astype(jnp.float32) - top) * LOG2E
-            weights = []
-            for n, place in enumerate(parts):
-                scores = [
-                    jnp.dot(keys[row, place, :], queries[head, row], preferred_element_type=jnp.float32) for row in range(rows)
+
+            def score(place):
+                return [
+                    jnp.dot(
+                        keys[row, place, :], queries[head, row], preferred_element_type=jnp.float32
+                    )
+                    for row in range(rows)
                 ]
-                weights.append(
-                    [jnp.exp2(part * LOG2E + shifted[n]).astype(jnp.bfloat16) for part in scores]
-                )
-            for n, place in enumerate(parts):
-                for row in range(rows):
-                    sums[row] += jnp.dot(
+
+            def weigh(n, scores):
+                return [
+                    jnp.exp2(part * LOG2E + shifted[n]).astype(jnp.bfloat16) for part in scores
+                ]
+
+            weights = [weigh(n, score(place)) for n, place in enumerate(parts)]
+            for row in range(rows):
+                fresh = sums[row]
+                for n, place in enumerate(parts):
+                    fresh += jnp.dot(
                         values[row, head, :, place], weights[n][row], preferred_element_type=jnp.float32
                     )
+                sums[row] = fresh
 
         def double(pair, carry):
             span(2 * pair, 2)
@@ -413,7 +422,7 @@
             SMEM,
             pl.BlockSpec(memory_space=pl.ANY),
             pl.BlockSpec(memory_space=pl.ANY),
-            *(fixed(piece) for piece in far),
+            *[VMEM] * len(far),
             fixed(weight),
             fixed(weight_t),
             fixed(queries),

time: 135 us -> 135 us (level)
  no operation moved by 1% of the time
where the time goes in v7:
time: 135 us; the launch traced here: 134 us
  starting transfers between devices  46.7 us (35%)
  Pallas kernels  34.8 us (26%)
  waiting for transfers between devices  33.7 us (25%)
  between operations  13.7 us (10%)
  other arithmetic  3.68 us (3%)
  local copies, waits for them, and re-layouts  1.82 us (1%)
    ppermute x12, starting transfers between devices, shift(): return lax.ppermute(value, 'cols', pairs)  43.2 us
    ppermute x12, waiting for transfers between devices, shift(): return lax.ppermute(value, 'cols', pairs)  27 us
    pallas_call x1, Pallas kernels, attend(): pl.pallas_call(attend_kernel, grid=(heads,), in_specs=[SMEM, pl.BlockSpec...  22.5 us
    pallas_call x1, Pallas kernels, project_near(): pl.pallas_call(near_kernel, grid=(rows,), in_specs=[SMEM, *(piece_spec(pi...  10.1 us
    ppermute x1, waiting for transfers between devices, gather_bias(): lax.ppermute(bias_t, 'rows', [(r, (r + half) % count) for r in range(coun...  6.66 us
    ppermute x1, starting transfers between devices, gather_bias(): lax.ppermute(bias_t, 'rows', [(r, (r + half) % count) for r in range(coun...  3.47 us
  transfers between devices with their start and end apart: 14, of which 8 were waited for; matrix products, arithmetic and copies ran while one was open for 2% of the time, Pallas kernels for 8%

profile of v7, /device:TPU:448, one launch (start us, length us, event | category | flops | bytes accessed | tf_op | source)
XLA Modules:
  0.0 134.4 jit_solution(18339429711256297527)
XLA Ops:
  6.5 2.2 %prep.1 = (bf16[4,256,128]{2,1,0:T(8,128)(2,1)}, bf16[4,128,256]{2,1,0:T(8,128)(2,1)}) custom-call(s32[32]{0:T(128)} %valid_ref.5, bf16[4,256,128]{2,1,0:T(8,128)(2,1)} %pair_ref.1, bf16[4,256,128]{2,1,0:T(8,128)(2,1)} %bias_ref.1), custom_call_target="tpu_custom_call" | custom-call | tf_op jit(solution)/shard_map/prep/pallas_call | solution.py:45
  8.8 3.5 %collective-permute-start.12 = (bf16[4,128,256]{2,1,0:T(8,128)(2,1)}, bf16[4,128,256]{2,1,0:T(8,128)(2,1)S(1)}, u32[]{:S(2)}, u32[]{:S(2)}) collective-permute-start(bf16[4,128,256]{2,1,0:T(8,128)(2,1)} %get-tuple-element.18), channel_id=1, source_target_pairs={{0,256},{16,272},{32,288},{48,304},{64,320},{80,336},{96,352},{112... | collective-permute-start | bytes 786440 | tf_op jit(solution)/shard_map/ppermute | solution.py:476
  12.2 6.7 %collective-permute-done.12 = bf16[4,128,256]{2,1,0:T(8,128)(2,1)S(1)} collective-permute-done((bf16[4,128,256]{2,1,0:T(8,128)(2,1)}, bf16[4,128,256]{2,1,0:T(8,128)(2,1)S(1)}, u32[]{:S(2)}, u32[]{:S(2)}) %collective-permute-start.12) | collective-permute-done | bytes 262176 | tf_op jit(solution)/shard_map/ppermute | solution.py:476
  18.9 1.8 %pad_maximum_fusion.3 = bf16[2,4,128,256]{3,2,1,0:T(8,128)(2,1)} fusion(bf16[1,4,128,256]{3,2,1,0:T(8,128)(2,1)S(1)} %bitcast.23, bf16[1,4,128,256]{3,2,1,0:T(8,128)(2,1)} %bitcast.22), kind=kLoop, calls=%fused_computation.3 | loop fusion | flops 262144 | bytes 1048576 | tf_op jit(solution)/shard_map/stack | solution.py:477
  20.7 4.5 %collective-permute-start = (bf16[4,256,128]{2,1,0:T(8,128)(2,1)}, bf16[4,256,128]{2,1,0:T(8,128)(2,1)S(1)}, u32[]{:S(2)}, u32[]{:S(2)}) collective-permute-start(bf16[4,256,128]{2,1,0:T(8,128)(2,1)} %get-tuple-element.12), channel_id=1, source_target_pairs={{0,1},{1,2},{2,3},{3,0},{4,5},{5,6},{6,7},{7,4},{8,9},{9,10},{10,1... | collective-permute-start | bytes 786440 | tf_op jit(solution)/shard_map/ppermute | solution.py:470
  25.2 3.6 %collective-permute-start.1 = (bf16[4,256,128]{2,1,0:T(8,128)(2,1)}, bf16[4,256,128]{2,1,0:T(8,128)(2,1)S(1)}, u32[]{:S(2)}, u32[]{:S(2)}) collective-permute-start(bf16[4,256,128]{2,1,0:T(8,128)(2,1)} %get-tuple-element.12), channel_id=1, source_target_pairs={{0,3},{1,0},{2,1},{3,2},{4,7},{5,4},{6,5},{7,6},{8,11},{9,8},{10,9... | collective-permute-start | bytes 786440 | tf_op jit(solution)/shard_map/ppermute | solution.py:470
  28.8 6.7 %collective-permute-done = bf16[4,256,128]{2,1,0:T(8,128)(2,1)S(1)} collective-permute-done((bf16[4,256,128]{2,1,0:T(8,128)(2,1)}, bf16[4,256,128]{2,1,0:T(8,128)(2,1)S(1)}, u32[]{:S(2)}, u32[]{:S(2)}) %collective-permute-start) | collective-permute-done | bytes 262176 | tf_op jit(solution)/shard_map/ppermute | solution.py:470
  35.5 5.9 %collective-permute-start.2 = (bf16[2,256,128]{2,1,0:T(8,128)(2,1)S(1)}, bf16[2,256,128]{2,1,0:T(8,128)(2,1)S(1)}, u32[]{:S(2)}, u32[]{:S(2)}) collective-permute-start(bf16[2,256,128]{2,1,0:T(8,128)(2,1)S(1)} %slice.16), channel_id=1, source_target_pairs={{0,1},{1,2},{2,3},{3,0},{4,5},{5,6},{6,7},{7,4},{8,9},{9,10},{10,1... | collective-permute-start | bytes 393224 | tf_op jit(solution)/shard_map/ppermute | solution.py:470
  42.0 4.7 %collective-permute-start.8 = (bf16[2,4,256,128]{3,2,1,0:T(8,128)(2,1)S(1)}, bf16[2,4,256,128]{3,2,1,0:T(8,128)(2,1)S(1)}, u32[]{:S(2)}, u32[]{:S(2)}) collective-permute-start(bf16[2,4,256,128]{3,2,1,0:T(8,128)(2,1)S(1)} %pad_maximum_fusion.sides_ref), channel_id=1, source_target_pairs={{0,12},{1,13},{2,14},{3,15},{4,0},{5,1},{6,2},{7,3},{8,4},{9,5},{1... | collective-permute-start | bytes 1572872 | tf_op jit(solution)/shard_map/ppermute | solution.py:470
  46.7 3.9 %collective-permute-start.3 = (bf16[2,256,128]{2,1,0:T(8,128)(2,1)S(1)}, bf16[2,256,128]{2,1,0:T(8,128)(2,1)S(1)}, u32[]{:S(2)}, u32[]{:S(2)}) collective-permute-start(bf16[2,256,128]{2,1,0:T(8,128)(2,1)S(1)} %slice.17), channel_id=1, source_target_pairs={{0,3},{1,0},{2,1},{3,2},{4,7},{5,4},{6,5},{7,6},{8,11},{9,8},{10,9... | collective-permute-start | bytes 393224 | tf_op jit(solution)/shard_map/ppermute | solution.py:470
  50.6 1.9 %collective-permute-start.5 = (bf16[2,4,256,128]{3,2,1,0:T(8,128)(2,1)S(1)}, bf16[2,4,256,128]{3,2,1,0:T(8,128)(2,1)S(1)}, u32[]{:S(2)}, u32[]{:S(2)}) collective-permute-start(bf16[2,4,256,128]{3,2,1,0:T(8,128)(2,1)S(1)} %pad_maximum_fusion.sides_ref), channel_id=1, source_target_pairs={{0,4},{1,5},{2,6},{3,7},{4,8},{5,9},{6,10},{7,11},{8,12},{9,13},{1... | collective-permute-start | bytes 1572872 | tf_op jit(solution)/shard_map/ppermute | solution.py:470
  52.6 4.6 %collective-permute-done.3 = bf16[2,256,128]{2,1,0:T(8,128)(2,1)S(1)} collective-permute-done((bf16[2,256,128]{2,1,0:T(8,128)(2,1)S(1)}, bf16[2,256,128]{2,1,0:T(8,128)(2,1)S(1)}, u32[]{:S(2)}, u32[]{:S(2)}) %collective-permute-start.3) | collective-permute-done | bytes 131104 | tf_op jit(solution)/shard_map/ppermute | solution.py:470
  57.2 2.7 %collective-permute-start.9 = (bf16[4,256,128]{2,1,0:T(8,128)(2,1)S(1)}, bf16[4,256,128]{2,1,0:T(8,128)(2,1)S(1)}, u32[]{:S(2)}, u32[]{:S(2)}) collective-permute-start(bf16[4,256,128]{2,1,0:T(8,128)(2,1)S(1)} %constant_dynamic-update-slice_fusion), channel_id=1, source_target_pairs={{0,12},{1,13},{2,14},{3,15},{4,0},{5,1},{6,2},{7,3},{8,4},{9,5},{1... | collective-permute-start | bytes 786440 | tf_op jit(solution)/shard_map/ppermute | solution.py:470
  59.9 3.1 %collective-permute-start.4 = (bf16[4,256,128]{2,1,0:T(8,128)(2,1)}, bf16[4,256,128]{2,1,0:T(8,128)(2,1)S(1)}, u32[]{:S(2)}, u32[]{:S(2)}) collective-permute-start(bf16[4,256,128]{2,1,0:T(8,128)(2,1)} %get-tuple-element.12), channel_id=1, source_target_pairs={{0,4},{1,5},{2,6},{3,7},{4,8},{5,9},{6,10},{7,11},{8,12},{9,13},{1... | collective-permute-start | bytes 786440 | tf_op jit(solution)/shard_map/ppermute | solution.py:470
  63.1 3.0 %collective-permute-done.9 = bf16[4,256,128]{2,1,0:T(8,128)(2,1)S(1)} collective-permute-done((bf16[4,256,128]{2,1,0:T(8,128)(2,1)S(1)}, bf16[4,256,128]{2,1,0:T(8,128)(2,1)S(1)}, u32[]{:S(2)}, u32[]{:S(2)}) %collective-permute-start.9) | collective-permute-done | bytes 262176 | tf_op jit(solution)/shard_map/ppermute | solution.py:470
  66.0 0.9 pad_maximum_fusion.2
  67.0 3.9 %collective-permute-start.11 = (bf16[2,4,256,128]{3,2,1,0:T(8,128)(2,1)}, bf16[2,4,256,128]{3,2,1,0:T(8,128)(2,1)S(1)}, u32[]{:S(2)}, u32[]{:S(2)}) collective-permute-start(bf16[2,4,256,128]{3,2,1,0:T(8,128)(2,1)} %pad_maximum_fusion.2), channel_id=1, source_target_pairs={{0,12},{1,13},{2,14},{3,15},{4,0},{5,1},{6,2},{7,3},{8,4},{9,5},{1... | collective-permute-start | bytes 1572872 | tf_op jit(solution)/shard_map/ppermute | solution.py:470
  72.8 1.9 %collective-permute-start.10 = (bf16[2,4,256,128]{3,2,1,0:T(8,128)(2,1)}, bf16[2,4,256,128]{3,2,1,0:T(8,128)(2,1)S(1)}, u32[]{:S(2)}, u32[]{:S(2)}) collective-permute-start(bf16[2,4,256,128]{3,2,1,0:T(8,128)(2,1)} %pad_maximum_fusion.1), channel_id=1, source_target_pairs={{0,4},{1,5},{2,6},{3,7},{4,8},{5,9},{6,10},{7,11},{8,12},{9,13},{1... | collective-permute-start | bytes 1572872 | tf_op jit(solution)/shard_map/ppermute | solution.py:470
  74.7 5.1 %collective-permute-start.7 = (bf16[4,256,128]{2,1,0:T(8,128)(2,1)}, bf16[4,256,128]{2,1,0:T(8,128)(2,1)}, u32[]{:S(2)}, u32[]{:S(2)}) collective-permute-start(bf16[4,256,128]{2,1,0:T(8,128)(2,1)} %get-tuple-element.12), channel_id=1, source_target_pairs={{0,12},{1,13},{2,14},{3,15},{4,0},{5,1},{6,2},{7,3},{8,4},{9,5},{1... | collective-permute-start | bytes 786440 | tf_op jit(solution)/shard_map/ppermute | solution.py:470
  79.8 1.9 %collective-permute-start.6 = (bf16[4,256,128]{2,1,0:T(8,128)(2,1)S(1)}, bf16[4,256,128]{2,1,0:T(8,128)(2,1)}, u32[]{:S(2)}, u32[]{:S(2)}) collective-permute-start(bf16[4,256,128]{2,1,0:T(8,128)(2,1)S(1)} %constant_dynamic-update-slice_fusion), channel_id=1, source_target_pairs={{0,4},{1,5},{2,6},{3,7},{4,8},{5,9},{6,10},{7,11},{8,12},{9,13},{1... | collective-permute-start | bytes 786440 | tf_op jit(solution)/shard_map/ppermute | solution.py:470
  82.5 4.1 %collective-permute-done.7 = bf16[4,256,128]{2,1,0:T(8,128)(2,1)} collective-permute-done((bf16[4,256,128]{2,1,0:T(8,128)(2,1)}, bf16[4,256,128]{2,1,0:T(8,128)(2,1)}, u32[]{:S(2)}, u32[]{:S(2)}) %collective-permute-start.7) | collective-permute-done | bytes 262176 | tf_op jit(solution)/shard_map/ppermute | solution.py:470
  86.6 7.2 %collective-permute-done.6 = bf16[4,256,128]{2,1,0:T(8,128)(2,1)} collective-permute-done((bf16[4,256,128]{2,1,0:T(8,128)(2,1)S(1)}, bf16[4,256,128]{2,1,0:T(8,128)(2,1)}, u32[]{:S(2)}, u32[]{:S(2)}) %collective-permute-start.6) | collective-permute-done | bytes 262176 | tf_op jit(solution)/shard_map/ppermute | solution.py:470
  93.9 10.1 %near.1 = (bf16[4,3328,128]{2,1,0:T(8,128)(2,1)}, bf16[4,4,48,3328]{3,2,1,0:T(8,128)(2,1)}, bf16[4,4,128,256]{3,2,1,0:T(8,128)(2,1)}, f32[4,4,32,256]{3,2,1,0:T(8,128)}, f32[4,8,128]{2,1,0:T(8,128)}) custom-call(s32[32]{0:T(128)} %valid_ref.5, bf16[1,4,256,128]{3,2,1,0:T(8,128)(2,1)} %bitcast.own_ref, bf16[2,4,256,128]{3,2,1,0:T(8,128)(2,1)} %copy-done, ...), custom_call_target="tpu_custom_call" | custom-call | tf_op jit(solution)/shard_map/near/pallas_call | solution.py:198
  105.1 22.5 %attend.1 = bf16[4,256,128]{2,1,0:T(8,128)(2,1)} custom-call(s32[32]{0:T(128)} %valid_ref.5, bf16[4,3328,128]{2,1,0:T(8,128)(2,1)} %get-tuple-element.13.keys_hbm, bf16[4,4,48,3328]{3,2,1,0:T(8,128)(2,1)} %get-tuple-element.14.values_hbm, bf16[2,4,256,128]{3,2,1,0:T(8,128)(2,1)} %copy-done.8, bf16[2,4,256,128]{3,2,1,0:T(8,128)(2,1)} %copy-done.7, ...), custom_call_target="tpu_custom_call" | custom-call | tf_op jit(solution)/shard_map/attend/pallas_call | solution.py:418
  (37 shorter events, 4.2 us)
Async XLA Ops:
  6.5 75.2 %copy-start.1 = (bf16[128,512]{1,0:T(8,128)(2,1)S(1)}, bf16[128,512]{1,0:T(8,128)(2,1)}, u32[]{:S(2)}) copy-start(bf16[128,512]{1,0:T(8,128)(2,1)} %weight_ref.3) | copy-start | bytes 393220
  6.5 97.6 %all-gather.3.cloned.1.call-start = ((), (), s32[]{:S(2)}) async-start(), calls=%async_computation | async-start | bytes 8912896 | tf_op jit(solution)/shard_map/all_gather | solution.py:479
  8.8 10.1 %collective-permute-start.12 = (bf16[4,128,256]{2,1,0:T(8,128)(2,1)}, bf16[4,128,256]{2,1,0:T(8,128)(2,1)S(1)}, u32[]{:S(2)}, u32[]{:S(2)}) collective-permute-start(bf16[4,128,256]{2,1,0:T(8,128)(2,1)} %get-tuple-element.18), channel_id=1, source_target_pairs={{0,256},{16,272},{32,288},{48,304},{64,320},{80,336},{96,352},{112... | collective-permute-start | bytes 786440 | tf_op jit(solution)/shard_map/ppermute | solution.py:476
  20.7 14.8 %collective-permute-start = (bf16[4,256,128]{2,1,0:T(8,128)(2,1)}, bf16[4,256,128]{2,1,0:T(8,128)(2,1)S(1)}, u32[]{:S(2)}, u32[]{:S(2)}) collective-permute-start(bf16[4,256,128]{2,1,0:T(8,128)(2,1)} %get-tuple-element.12), channel_id=1, source_target_pairs={{0,1},{1,2},{2,3},{3,0},{4,5},{5,6},{6,7},{7,4},{8,9},{9,10},{10,1... | collective-permute-start | bytes 786440 | tf_op jit(solution)/shard_map/ppermute | solution.py:470
  25.2 16.7 %collective-permute-start.1 = (bf16[4,256,128]{2,1,0:T(8,128)(2,1)}, bf16[4,256,128]{2,1,0:T(8,128)(2,1)S(1)}, u32[]{:S(2)}, u32[]{:S(2)}) collective-permute-start(bf16[4,256,128]{2,1,0:T(8,128)(2,1)} %get-tuple-element.12), channel_id=1, source_target_pairs={{0,3},{1,0},{2,1},{3,2},{4,7},{5,4},{6,5},{7,6},{8,11},{9,8},{10,9... | collective-permute-start | bytes 786440 | tf_op jit(solution)/shard_map/ppermute | solution.py:470
  35.5 17.0 %collective-permute-start.2 = (bf16[2,256,128]{2,1,0:T(8,128)(2,1)S(1)}, bf16[2,256,128]{2,1,0:T(8,128)(2,1)S(1)}, u32[]{:S(2)}, u32[]{:S(2)}) collective-permute-start(bf16[2,256,128]{2,1,0:T(8,128)(2,1)S(1)} %slice.16), channel_id=1, source_target_pairs={{0,1},{1,2},{2,3},{3,0},{4,5},{5,6},{6,7},{7,4},{8,9},{9,10},{10,1... | collective-permute-start | bytes 393224 | tf_op jit(solution)/shard_map/ppermute | solution.py:470
  42.0 51.9 %copy-start = (bf16[2,4,256,128]{3,2,1,0:T(8,128)(2,1)}, bf16[2,4,256,128]{3,2,1,0:T(8,128)(2,1)S(1)}, u32[]{:S(2)}) copy-start(bf16[2,4,256,128]{3,2,1,0:T(8,128)(2,1)S(1)} %pad_maximum_fusion.sides_ref) | copy-start | bytes 1572868
  42.0 21.0 %collective-permute-start.8 = (bf16[2,4,256,128]{3,2,1,0:T(8,128)(2,1)S(1)}, bf16[2,4,256,128]{3,2,1,0:T(8,128)(2,1)S(1)}, u32[]{:S(2)}, u32[]{:S(2)}) collective-permute-start(bf16[2,4,256,128]{3,2,1,0:T(8,128)(2,1)S(1)} %pad_maximum_fusion.sides_ref), channel_id=1, source_target_pairs={{0,12},{1,13},{2,14},{3,15},{4,0},{5,1},{6,2},{7,3},{8,4},{9,5},{1... | collective-permute-start | bytes 1572872 | tf_op jit(solution)/shard_map/ppermute | solution.py:470
  46.7 10.4 %collective-permute-start.3 = (bf16[2,256,128]{2,1,0:T(8,128)(2,1)S(1)}, bf16[2,256,128]{2,1,0:T(8,128)(2,1)S(1)}, u32[]{:S(2)}, u32[]{:S(2)}) collective-permute-start(bf16[2,256,128]{2,1,0:T(8,128)(2,1)S(1)} %slice.17), channel_id=1, source_target_pairs={{0,3},{1,0},{2,1},{3,2},{4,7},{5,4},{6,5},{7,6},{8,11},{9,8},{10,9... | collective-permute-start | bytes 393224 | tf_op jit(solution)/shard_map/ppermute | solution.py:470
  50.6 20.3 %collective-permute-start.5 = (bf16[2,4,256,128]{3,2,1,0:T(8,128)(2,1)S(1)}, bf16[2,4,256,128]{3,2,1,0:T(8,128)(2,1)S(1)}, u32[]{:S(2)}, u32[]{:S(2)}) collective-permute-start(bf16[2,4,256,128]{3,2,1,0:T(8,128)(2,1)S(1)} %pad_maximum_fusion.sides_ref), channel_id=1, source_target_pairs={{0,4},{1,5},{2,6},{3,7},{4,8},{5,9},{6,10},{7,11},{8,12},{9,13},{1... | collective-permute-start | bytes 1572872 | tf_op jit(solution)/shard_map/ppermute | solution.py:470
  57.1 36.7 %copy-start.6 = (bf16[4,256,128]{2,1,0:T(8,128)(2,1)}, bf16[4,256,128]{2,1,0:T(8,128)(2,1)S(1)}, u32[]{:S(2)}) copy-start(bf16[4,256,128]{2,1,0:T(8,128)(2,1)S(1)} %constant_dynamic-update-slice_fusion) | copy-start | bytes 786436
  57.2 8.9 %collective-permute-start.9 = (bf16[4,256,128]{2,1,0:T(8,128)(2,1)S(1)}, bf16[4,256,128]{2,1,0:T(8,128)(2,1)S(1)}, u32[]{:S(2)}, u32[]{:S(2)}) collective-permute-start(bf16[4,256,128]{2,1,0:T(8,128)(2,1)S(1)} %constant_dynamic-update-slice_fusion), channel_id=1, source_target_pairs={{0,12},{1,13},{2,14},{3,15},{4,0},{5,1},{6,2},{7,3},{8,4},{9,5},{1... | collective-permute-start | bytes 786440 | tf_op jit(solution)/shard_map/ppermute | solution.py:470
  59.9 12.0 %collective-permute-start.4 = (bf16[4,256,128]{2,1,0:T(8,128)(2,1)}, bf16[4,256,128]{2,1,0:T(8,128)(2,1)S(1)}, u32[]{:S(2)}, u32[]{:S(2)}) collective-permute-start(bf16[4,256,128]{2,1,0:T(8,128)(2,1)} %get-tuple-element.12), channel_id=1, source_target_pairs={{0,4},{1,5},{2,6},{3,7},{4,8},{5,9},{6,10},{7,11},{8,12},{9,13},{1... | collective-permute-start | bytes 786440 | tf_op jit(solution)/shard_map/ppermute | solution.py:470
  63.0 30.9 %copy-start.2 = (bf16[2,4,256,128]{3,2,1,0:T(8,128)(2,1)}, bf16[2,4,256,128]{3,2,1,0:T(8,128)(2,1)S(1)}, u32[]{:S(2)}) copy-start(bf16[2,4,256,128]{3,2,1,0:T(8,128)(2,1)S(1)} %collective-permute-done.8.right_sides_ref) | copy-start | bytes 1572868
  66.0 27.9 %copy-start.4 = (bf16[4,256,128]{2,1,0:T(8,128)(2,1)}, bf16[4,256,128]{2,1,0:T(8,128)(2,1)S(1)}, u32[]{:S(2)}) copy-start(bf16[4,256,128]{2,1,0:T(8,128)(2,1)S(1)} %collective-permute-done.9) | copy-start | bytes 786436
  67.0 37.1 %collective-permute-start.11 = (bf16[2,4,256,128]{3,2,1,0:T(8,128)(2,1)}, bf16[2,4,256,128]{3,2,1,0:T(8,128)(2,1)S(1)}, u32[]{:S(2)}, u32[]{:S(2)}) collective-permute-start(bf16[2,4,256,128]{3,2,1,0:T(8,128)(2,1)} %pad_maximum_fusion.2), channel_id=1, source_target_pairs={{0,12},{1,13},{2,14},{3,15},{4,0},{5,1},{6,2},{7,3},{8,4},{9,5},{1... | collective-permute-start | bytes 1572872 | tf_op jit(solution)/shard_map/ppermute | solution.py:470
  70.9 23.0 %copy-start.3 = (bf16[2,4,256,128]{3,2,1,0:T(8,128)(2,1)}, bf16[2,4,256,128]{3,2,1,0:T(8,128)(2,1)S(1)}, u32[]{:S(2)}) copy-start(bf16[2,4,256,128]{3,2,1,0:T(8,128)(2,1)S(1)} %collective-permute-done.5.left_sides_ref) | copy-start | bytes 1572868
  71.9 22.0 %copy-start.5 = (bf16[4,256,128]{2,1,0:T(8,128)(2,1)}, bf16[4,256,128]{2,1,0:T(8,128)(2,1)S(1)}, u32[]{:S(2)}) copy-start(bf16[4,256,128]{2,1,0:T(8,128)(2,1)S(1)} %collective-permute-done.4) | copy-start | bytes 786436
  72.8 31.3 %collective-permute-start.10 = (bf16[2,4,256,128]{3,2,1,0:T(8,128)(2,1)}, bf16[2,4,256,128]{3,2,1,0:T(8,128)(2,1)S(1)}, u32[]{:S(2)}, u32[]{:S(2)}) collective-permute-start(bf16[2,4,256,128]{3,2,1,0:T(8,128)(2,1)} %pad_maximum_fusion.1), channel_id=1, source_target_pairs={{0,4},{1,5},{2,6},{3,7},{4,8},{5,9},{6,10},{7,11},{8,12},{9,13},{1... | collective-permute-start | bytes 1572872 | tf_op jit(solution)/shard_map/ppermute | solution.py:470
  74.7 11.9 %collective-permute-start.7 = (bf16[4,256,128]{2,1,0:T(8,128)(2,1)}, bf16[4,256,128]{2,1,0:T(8,128)(2,1)}, u32[]{:S(2)}, u32[]{:S(2)}) collective-permute-start(bf16[4,256,128]{2,1,0:T(8,128)(2,1)} %get-tuple-element.12), channel_id=1, source_target_pairs={{0,12},{1,13},{2,14},{3,15},{4,0},{5,1},{6,2},{7,3},{8,4},{9,5},{1... | collective-permute-start | bytes 786440 | tf_op jit(solution)/shard_map/ppermute | solution.py:470
  79.8 14.0 %collective-permute-start.6 = (bf16[4,256,128]{2,1,0:T(8,128)(2,1)S(1)}, bf16[4,256,128]{2,1,0:T(8,128)(2,1)}, u32[]{:S(2)}, u32[]{:S(2)}) collective-permute-start(bf16[4,256,128]{2,1,0:T(8,128)(2,1)S(1)} %constant_dynamic-update-slice_fusion), channel_id=1, source_target_pairs={{0,4},{1,5},{2,6},{3,7},{4,8},{5,9},{6,10},{7,11},{8,12},{9,13},{1... | collective-permute-start | bytes 786440 | tf_op jit(solution)/shard_map/ppermute | solution.py:470
  104.1 0.8 copy-start.7
  104.1 1.0 copy-start.8
Sparse Core Ops, SparseCore 0:
  20.8 56.1 all-gather.2
